TPU v7x, 32 devices: a whole 2x2x4 slice. The times are simulated.
32 devices in a mesh: dp: 8 (over y, x, core), seq: 4 (over z).
Axes of the slice: x: 2, y: 2, z: 4, core: 2. Of those that a mesh axis runs over, the one named last changes fastest.
Arguments:
- tokens: bfloat16 [16, 1024, 2048], P('dp', 'seq'), may hold values from -6 to 6
- token_types: int32 [16, 1024], P('dp', 'seq'), may hold values from 0 to 3
- view_mask: int32 [16], P('dp'), may hold values from 0 to 1
- type_table: bfloat16 [4, 2048], P(None, 'seq'), may hold values from -3 to 3
- ln1_gain: bfloat16 [2048], P('seq'), may hold values from 0.25 to 1.75
- ln1_bias: bfloat16 [2048], P('seq'), may hold values from -2 to 2
- w_qkv: bfloat16 [2048, 6144], P('dp', 'seq'), may hold values from -0.125 to 0.125
- w_out: bfloat16 [2048, 2048], P('dp', 'seq'), may hold values from -1.5 to 1.5
- ln2_gain: bfloat16 [2048], P('seq'), may hold values from 0.25 to 1.75
- ln2_bias: bfloat16 [2048], P('seq'), may hold values from -2 to 2
- w_up: bfloat16 [2048, 8192], P('dp', 'seq'), may hold values from -0.125 to 0.125
- w_down: bfloat16 [8192, 2048], P('seq', 'dp'), may hold values from -0.0625 to 0.0625
- cotangent: bfloat16 [16, 1024, 2048], P('dp', 'seq'), may hold values from -6 to 6
Outputs:
- output: bfloat16 [16, 1024, 2048], P('dp', 'seq')
- input_grad: float32 [16, 1024, 2048], P('dp', 'seq')
- grad_type_table: float32 [4, 2048], P(None, ('dp', 'seq'))
- grad_ln1_gain: float32 [2048], P(('dp', 'seq'))
- grad_ln1_bias: float32 [2048], P(('dp', 'seq'))
- grad_w_qkv: float32 [2048, 6144], P('dp', 'seq')
- grad_w_out: float32 [2048, 2048], P('dp', 'seq')
- grad_ln2_gain: float32 [2048], P(('dp', 'seq'))
- grad_ln2_bias: float32 [2048], P(('dp', 'seq'))
- grad_w_up: float32 [2048, 8192], P('dp', 'seq')
- grad_w_down: float32 [8192, 2048], P('seq', 'dp')
Inputs may be any that keep to these rules, and one draw needn't show every extreme that they name: `view_mask`: 1 marks a sequence whose timesteps hold two camera views; 0 one whose second view of 256 tokens in each timestep is padding.
All inputs are finite; a program needn't handle non-finite values.
Results may differ from a plain program's by a relative error of at most 0.019.
Values may be sent and summed in bfloat16 or wider, within the bound.
A program may use at most 256 MiB of HBM per device.

v0:
```python
import math

import jax
import jax.numpy as jnp
from jax import lax
from jax.sharding import PartitionSpec as P

HEADS = 16
HEAD_DIM = 128
TYPES = 4


EPS = 1e-05
NEGATIVE = -1e30
HIGHEST_PRECISION = lax.Precision.HIGHEST


def layer_norm(hidden, gain, bias):
    average = jnp.mean(hidden, axis=-1, keepdims=True)
    centered = hidden - average
    variance = jnp.mean(centered * centered, axis=-1, keepdims=True)
    return centered * lax.rsqrt(variance + EPS) * gain + bias


def gelu_tanh(value):
    inner = math.sqrt(2.0 / math.pi) * (value + 0.044715 * value * value * value)
    return 0.5 * value * (1.0 + jnp.tanh(inner))


def key_allowed(first, count, full_len, view_flag):
    query_pos = first + jnp.arange(count, dtype=jnp.int32)
    key_pos = jnp.arange(full_len, dtype=jnp.int32)
    causal = key_pos[None, :] <= query_pos[:, None]
    seen = jnp.logical_or(view_flag == 1, key_pos % (full_len // 2) < full_len // 4)
    return jnp.logical_and(causal, seen[None, :])


def scores_of(query, keys, allowed, scale):
    plain = jnp.einsum("qhd,khd->hqk", query, keys, preferred_element_type=jnp.float32) * scale
    return jnp.where(allowed[None], plain, NEGATIVE)


def to_heads(values_in):
    return lax.all_to_all(values_in, "seq", split_axis=2, concat_axis=1, tiled=True)


def to_tokens(values_in):
    return lax.all_to_all(values_in, "seq", split_axis=1, concat_axis=2, tiled=True)


def shards(
    tokens,
    token_types,
    view_mask,
    type_table,
    ln1_gain,
    ln1_bias,
    w_qkv,
    w_out,
    ln2_gain,
    ln2_bias,
    w_up,
    w_down,
    cotangent,
):
    seq_count, local_len, width = tokens.shape
    groups = lax.axis_size("seq")
    full_len = local_len * groups
    row_count = seq_count * local_len
    local_heads = HEADS // groups
    scale = 1.0 / math.sqrt(HEAD_DIM)
    block = min(512, full_len)
    f32 = jnp.float32
    bf16 = jnp.bfloat16
    out_part, table, gain_one, bias_one, gain_two, bias_two = (
        lax.all_gather(w_out, "seq", axis=1, tiled=True),
        lax.all_gather(type_table, "seq", axis=1, tiled=True),
        lax.all_gather(ln1_gain, "seq", axis=0, tiled=True),
        lax.all_gather(ln1_bias, "seq", axis=0, tiled=True),
        lax.all_gather(ln2_gain, "seq", axis=0, tiled=True),
        lax.all_gather(ln2_bias, "seq", axis=0, tiled=True),
    )
    qkv_full, out_full, up_full, down_full = (
        lax.all_gather(w_qkv, "dp", axis=0, tiled=True),
        lax.all_gather(out_part, "dp", axis=0, tiled=True),
        lax.all_gather(w_up, "dp", axis=0, tiled=True),
        lax.all_gather(w_down, "dp", axis=1, tiled=True),
    )
    onehot = (
        token_types.reshape(row_count)[:, None] == jnp.arange(TYPES, dtype=jnp.int32)[None, :]
    ).astype(f32)
    start_hidden = tokens.reshape(row_count, width).astype(f32) + jnp.dot(
        onehot, table.astype(f32), precision=HIGHEST_PRECISION
    )
    norm_one, pull_one = jax.vjp(
        layer_norm, start_hidden, gain_one.astype(f32), bias_one.astype(f32)
    )
    normed_one = norm_one.astype(bf16)
    normed_rows = lax.all_gather(
        normed_one.reshape(seq_count, local_len, width), "seq", axis=1, tiled=True
    )
    by_heads = jnp.einsum("std,de->ste", normed_rows, qkv_full, preferred_element_type=f32).astype(
        bf16
    )
    by_heads = by_heads.reshape(seq_count, full_len, local_heads, 3, HEAD_DIM)
    contexts = []
    kept_lse = []
    for index in range(seq_count):
        keys = by_heads[index, :, :, 1]
        values = by_heads[index, :, :, 2]
        context_blocks = []
        lse_blocks = []
        for first in range(0, full_len, block):
            query = by_heads[index, first : first + block, :, 0]
            allowed = key_allowed(first, block, full_len, view_mask[index])
            scores = scores_of(query, keys, allowed, scale)
            top = jnp.max(scores, axis=-1, keepdims=True)
            expd = jnp.exp(scores - top)
            total = jnp.sum(expd, axis=-1, keepdims=True)
            probs_low = (expd / total).astype(bf16)
            context_blocks.append(
                jnp.einsum("hqk,khd->qhd", probs_low, values, preferred_element_type=f32).astype(
                    bf16
                )
            )
            lse_blocks.append(top + jnp.log(total))
        contexts.append(jnp.concatenate(context_blocks, axis=0))
        kept_lse.append(lse_blocks)
    context_heads = jnp.stack(contexts)
    context_rows = to_tokens(context_heads).reshape(row_count, width)
    mid_hidden = start_hidden + jnp.dot(context_rows, out_full, preferred_element_type=f32)
    norm_two, pull_two = jax.vjp(layer_norm, mid_hidden, gain_two.astype(f32), bias_two.astype(f32))
    normed_two = norm_two.astype(bf16)
    cot_rows = cotangent.reshape(row_count, width)
    ffn_input, grad_rows = (
        lax.all_gather(normed_two, "seq", axis=0, tiled=True),
        lax.all_gather(cot_rows, "seq", axis=0, tiled=True),
    )
    up_value = jnp.dot(ffn_input, up_full, preferred_element_type=f32)
    activated, gelu_pull = jax.vjp(gelu_tanh, up_value)
    activated_low = activated.astype(bf16)
    piece = activated_low
    ffn_out = lax.psum_scatter(
        jnp.dot(piece, down_full, preferred_element_type=f32).astype(jnp.bfloat16),
        "seq",
        scatter_dimension=0,
        tiled=True,
    ).astype(jnp.float32)
    output = (mid_hidden + ffn_out).astype(bf16).reshape(seq_count, local_len, width)
    grad_down = jnp.einsum("ti,td->id", activated_low, grad_rows, preferred_element_type=f32)
    grad_act = jnp.einsum("td,id->ti", grad_rows, down_full, preferred_element_type=f32)
    grad_up_value = gelu_pull(grad_act)[0].astype(bf16)
    grad_up = jnp.einsum("td,ti->di", ffn_input, grad_up_value, preferred_element_type=f32)
    piece = grad_up_value
    grad_normed_two = lax.psum_scatter(
        jnp.einsum("ti,di->td", piece, up_full, preferred_element_type=f32).astype(jnp.bfloat16),
        "seq",
        scatter_dimension=0,
        tiled=True,
    ).astype(jnp.float32)
    grad_mid_norm, grad_gain_two, grad_bias_two = pull_two(grad_normed_two)
    grad_mid = cot_rows.astype(f32) + grad_mid_norm
    grad_mid_low = grad_mid.astype(bf16)
    grad_out_weight = jnp.einsum(
        "td,te->de", context_rows, grad_mid_low, preferred_element_type=f32
    )
    grad_context = jnp.einsum(
        "te,de->td", grad_mid_low, out_full, preferred_element_type=f32
    ).astype(bf16)
    grad_context = grad_context.reshape(seq_count, local_len, HEADS, HEAD_DIM)
    grad_by_heads = to_heads(grad_context)
    grad_parts = []
    for index in range(seq_count):
        keys = by_heads[index, :, :, 1]
        values = by_heads[index, :, :, 2]
        grad_keys = jnp.zeros(keys.shape, f32)
        grad_values = jnp.zeros(values.shape, f32)
        grad_query_blocks = []
        for number, first in enumerate(range(0, full_len, block)):
            query = by_heads[index, first : first + block, :, 0]
            allowed = key_allowed(first, block, full_len, view_mask[index])
            scores = scores_of(query, keys, allowed, scale)
            probs = jnp.exp(scores - kept_lse[index][number])
            probs_low = probs.astype(bf16)
            grad_block = grad_by_heads[index, first : first + block]
            grad_values = grad_values + jnp.einsum(
                "hqk,qhd->khd", probs_low, grad_block, preferred_element_type=f32
            )
            grad_probs = jnp.einsum("qhd,khd->hqk", grad_block, values, preferred_element_type=f32)
            weighted = jnp.sum(probs * grad_probs, axis=-1, keepdims=True)
            grad_scores = (probs * (grad_probs - weighted)).astype(bf16)
            grad_query_blocks.append(
                jnp.einsum("hqk,khd->qhd", grad_scores, keys, preferred_element_type=f32) * scale
            )
            grad_keys = (
                grad_keys
                + jnp.einsum("hqk,qhd->khd", grad_scores, query, preferred_element_type=f32) * scale
            )
        grad_parts.append(
            jnp.stack([jnp.concatenate(grad_query_blocks, axis=0), grad_keys, grad_values], axis=2)
        )
    grad_projected = jnp.stack(grad_parts).astype(bf16)
    columns = qkv_full.shape[1]
    grad_flat = grad_projected.reshape(seq_count, full_len, columns)
    grad_qkv_weight = jnp.einsum("std,ste->de", normed_rows, grad_flat, preferred_element_type=f32)
    position_major = jnp.transpose(grad_flat, (1, 0, 2)).reshape(full_len * seq_count, columns)
    piece = position_major
    summed_rows = lax.psum_scatter(
        jnp.einsum("te,de->td", piece, qkv_full, preferred_element_type=f32).astype(jnp.bfloat16),
        "seq",
        scatter_dimension=0,
        tiled=True,
    ).astype(jnp.float32)
    grad_normed_one = jnp.transpose(
        summed_rows.reshape(local_len, seq_count, width), (1, 0, 2)
    ).reshape(row_count, width)
    grad_start_norm, grad_gain_one, grad_bias_one = pull_one(grad_normed_one)
    grad_start = grad_mid + grad_start_norm
    input_grad = grad_start.reshape(seq_count, local_len, width)
    grad_table = jnp.einsum("tk,td->kd", onehot, grad_start, precision=HIGHEST_PRECISION)
    (
        sum_qkv,
        sum_out,
        sum_up,
        sum_down,
        sum_table,
        sum_gain_one,
        sum_bias_one,
        sum_gain_two,
        sum_bias_two,
    ) = (
        lax.psum_scatter(
            grad_qkv_weight.astype(jnp.bfloat16), "dp", scatter_dimension=0, tiled=True
        ).astype(jnp.float32),
        lax.psum_scatter(
            grad_out_weight.astype(jnp.bfloat16), "dp", scatter_dimension=0, tiled=True
        ).astype(jnp.float32),
        lax.psum_scatter(
            grad_up.astype(jnp.bfloat16), "dp", scatter_dimension=0, tiled=True
        ).astype(jnp.float32),
        lax.psum_scatter(
            grad_down.astype(jnp.bfloat16), "dp", scatter_dimension=1, tiled=True
        ).astype(jnp.float32),
        lax.psum_scatter(
            grad_table.astype(jnp.bfloat16), "dp", scatter_dimension=1, tiled=True
        ).astype(jnp.float32),
        lax.psum_scatter(
            grad_gain_one.astype(jnp.bfloat16), "dp", scatter_dimension=0, tiled=True
        ).astype(jnp.float32),
        lax.psum_scatter(
            grad_bias_one.astype(jnp.bfloat16), "dp", scatter_dimension=0, tiled=True
        ).astype(jnp.float32),
        lax.psum_scatter(
            grad_gain_two.astype(jnp.bfloat16), "dp", scatter_dimension=0, tiled=True
        ).astype(jnp.float32),
        lax.psum_scatter(
            grad_bias_two.astype(jnp.bfloat16), "dp", scatter_dimension=0, tiled=True
        ).astype(jnp.float32),
    )
    final_out, final_table, final_gain_one, final_bias_one, final_gain_two, final_bias_two = (
        lax.psum_scatter(
            sum_out.astype(jnp.bfloat16), "seq", scatter_dimension=1, tiled=True
        ).astype(jnp.float32),
        lax.psum_scatter(
            sum_table.astype(jnp.bfloat16), "seq", scatter_dimension=1, tiled=True
        ).astype(jnp.float32),
        lax.psum_scatter(
            sum_gain_one.astype(jnp.bfloat16), "seq", scatter_dimension=0, tiled=True
        ).astype(jnp.float32),
        lax.psum_scatter(
            sum_bias_one.astype(jnp.bfloat16), "seq", scatter_dimension=0, tiled=True
        ).astype(jnp.float32),
        lax.psum_scatter(
            sum_gain_two.astype(jnp.bfloat16), "seq", scatter_dimension=0, tiled=True
        ).astype(jnp.float32),
        lax.psum_scatter(
            sum_bias_two.astype(jnp.bfloat16), "seq", scatter_dimension=0, tiled=True
        ).astype(jnp.float32),
    )
    return (
        output,
        input_grad,
        final_table,
        final_gain_one,
        final_bias_one,
        sum_qkv,
        final_out,
        final_gain_two,
        final_bias_two,
        sum_up,
        sum_down,
    )


def solution(mesh):
    placed = (
        P("dp", "seq", None),
        P("dp", "seq"),
        P("dp"),
        P(None, "seq"),
        P("seq"),
        P("seq"),
        P("dp", "seq"),
        P("dp", "seq"),
        P("seq"),
        P("seq"),
        P("dp", "seq"),
        P("seq", "dp"),
        P("dp", "seq", None),
    )
    return jax.shard_map(
        shards,
        mesh=mesh,
        in_specs=placed,
        out_specs=(
            P("dp", "seq", None),
            P("dp", "seq", None),
            P(None, ("dp", "seq")),
            P(("dp", "seq")),
            P(("dp", "seq")),
            P("dp", "seq"),
            P("dp", "seq"),
            P(("dp", "seq")),
            P(("dp", "seq")),
            P("dp", "seq"),
            P("seq", "dp"),
        ),
        check_vma=False,
    )
```

profile of v0, /device:TPU:0, one launch (start us, length us, event | category | flops | bytes accessed | tf_op | source)
XLA Modules:
  0.0 1703.9 jit_solution(4208703650060748523)
XLA Ops:
  61.8 25.6 %all-gather.15.cloned.1.call-done = bf16[2048,1536]{1,0:T(8,128)(2,1)} async-done(((bf16[256,1536]{1,0:T(8,128)(2,1)}), bf16[2048,1536]{1,0:T(8,128)(2,1)}) %all-gather.15.cloned.1.call-update) | async-done | bytes 6291472 | tf_op jit(solution)/shard_map/all_gather | solution.py:84
  87.4 151.8 %all-gather.13.cloned.1.call-done = bf16[2,1024,2048]{2,1,0:T(8,128)(2,1)} async-done(((bf16[2,256,2048]{2,1,0:T(8,128)(2,1)}), bf16[2,1024,2048]{2,1,0:T(8,128)(2,1)}) %all-gather.13.cloned.1.call-update) | async-done | bytes 8388624 | tf_op jit(solution)/shard_map/all_gather | solution.py:99
  300.8 107.3 %all-gather.3 = bf16[4,1,512]{2,1,0:T(2,128)(2,1)S(1)} all-gather(bf16[1,1,512]{2,1,0:T(2,128)(2,1)S(1)} %reshape.338), channel_id=1, replica_groups=mesh['dp'=8,'seq'=4] {'seq'}, dimensions={0}, use_global_device_ids=true | all-gather | bytes 5120 | tf_op jit(solution)/shard_map/all_gather | solution.py:81
  408.1 21.7 %all-gather.2 = bf16[4,1,512]{2,1,0:T(2,128)(2,1)S(1)} all-gather(bf16[1,1,512]{2,1,0:T(2,128)(2,1)S(1)} %reshape.336), channel_id=1, replica_groups=mesh['dp'=8,'seq'=4] {'seq'}, dimensions={0}, use_global_device_ids=true | all-gather | bytes 5120 | tf_op jit(solution)/shard_map/all_gather | solution.py:80
  449.2 35.9 %all-gather.27.cloned.1.call-done = bf16[2048,2048]{1,0:T(8,128)(2,1)} async-done(((bf16[512,2048]{1,0:T(8,128)(2,1)}), bf16[2048,2048]{1,0:T(8,128)(2,1)}) %all-gather.27.cloned.1.call-update) | async-done | bytes 8388624 | tf_op jit(solution)/shard_map/all_gather | solution.py:137
  485.0 56.8 %all-gather.25.cloned.1.call-done = bf16[2048,2048]{1,0:T(8,128)(2,1)} async-done(((bf16[2048,256]{1,0:T(8,128)(2,1)}), bf16[2048,2048]{1,0:T(8,128)(2,1)}) %all-gather.25.cloned.1.call-update) | async-done | bytes 8388624 | tf_op jit(solution)/shard_map/all_gather | solution.py:87
  541.9 24.3 %fusion.105 = f32[2048,2048]{1,0:T(8,128)} fusion(bf16[2048,2048]{1,0:T(8,128)(2,1)} %all-gather.27.cloned.1.call-done, bf16[2048,2048]{1,0:T(8,128)(2,1)} %all-gather.25.cloned.1.call-done), kind=kOutput, calls=%fused_computation.193 | convolution fusion | flops 17179869184 | bytes 33554432 | tf_op jit(solution)/shard_map/td,id->ti/dot_general | solution.py:151
  566.2 32.0 %all-gather.23.cloned.1.call-done = bf16[2048,2048]{1,0:T(8,128)(2,1)} async-done(((bf16[256,2048]{1,0:T(8,128)(2,1)}), bf16[2048,2048]{1,0:T(8,128)(2,1)}) %all-gather.23.cloned.1.call-update) | async-done | bytes 8388624 | tf_op jit(solution)/shard_map/all_gather | solution.py:86
  598.2 151.8 %all-gather.21.cloned.1.call-done = bf16[2048,2048]{1,0:T(8,128)(2,1)} async-done(((bf16[512,2048]{1,0:T(8,128)(2,1)}), bf16[2048,2048]{1,0:T(8,128)(2,1)}) %all-gather.21.cloned.1.call-update) | async-done | bytes 8388624 | tf_op jit(solution)/shard_map/all_gather | solution.py:136
  750.0 40.7 %fusion.4 = (bf16[2048,2048]{1,0:T(8,128)(2,1)}, f32[2048,2048]{1,0:T(8,128)}) fusion(f32[2048,2048]{1,0:T(8,128)} %fusion.105, bf16[2048,2048]{1,0:T(8,128)(2,1)} %all-gather.21.cloned.1.call-done, bf16[2048,2048]{1,0:T(8,128)(2,1)} %all-gather.23.cloned.1.call-done), kind=kOutput, calls=%fused_computation.7 | convolution fusion | flops 17280532480 | bytes 58720256 | tf_op jit(solution)/shard_map/dot_general | solution.py:139
  790.7 21.6 %convolution_convert_fusion.4 = bf16[2048,2048]{1,0:T(8,128)(2,1)} fusion(bf16[2048,2048]{1,0:T(8,128)(2,1)} %get-tuple-element.46, bf16[2048,2048]{1,0:T(8,128)(2,1)S(1)} %copy-done.58), kind=kOutput, calls=%fused_computation.41 | convolution fusion | flops 17184063488 | bytes 25165824 | tf_op jit(solution)/shard_map/ti,di->td/dot_general | solution.py:156
  812.3 26.8 %convolution_convert_fusion.5 = bf16[2048,2048]{1,0:T(8,128)(2,1)} fusion(bf16[2048,2048]{1,0:T(8,128)(2,1)} %all-gather.25.cloned.1.call-done, f32[2048,2048]{1,0:T(8,128)} %get-tuple-element.47), kind=kOutput, calls=%fused_computation.42 | convolution fusion | flops 17221812224 | bytes 33554432 | tf_op jit(solution)/shard_map/dot_general | solution.py:144
  839.2 115.9 %reduce-scatter.17.cloned.1.call-done = bf16[512,2048]{1,0:T(8,128)(2,1)} async-done(((bf16[2048,2048]{1,0:T(8,128)(2,1)}), bf16[512,2048]{1,0:T(8,128)(2,1)}) %reduce-scatter.17.cloned.1.call-update) | async-done | bytes 2097168 | tf_op jit(solution)/shard_map/reduce_scatter | solution.py:155
  960.0 142.6 %reduce-scatter.15.cloned.1.call-done = bf16[512,2048]{1,0:T(8,128)(2,1)} async-done(((bf16[2048,2048]{1,0:T(8,128)(2,1)}), bf16[512,2048]{1,0:T(8,128)(2,1)}) %reduce-scatter.15.cloned.1.call-update) | async-done | bytes 2097168 | tf_op jit(solution)/shard_map/reduce_scatter | solution.py:143
  1118.9 24.2 %convolution_convert_fusion.1 = bf16[2048,2048]{1,0:T(8,128)(2,1)} fusion(bf16[2048,2048]{1,0:T(8,128)(2,1)} %all-gather.21.cloned.1.call-done, bf16[2048,2048]{1,0:T(8,128)(2,1)} %get-tuple-element.46), kind=kOutput, calls=%fused_computation.38 | convolution fusion | flops 17184063488 | bytes 25165824 | tf_op jit(solution)/shard_map/td,ti->di/dot_general | solution.py:153
  1160.2 26.1 %convolution_convert_fusion = bf16[2048,2048]{1,0:T(8,128)(2,1)} fusion(bf16[2048,2048]{1,0:T(8,128)(2,1)} %all-gather.27.cloned.1.call-done, f32[2048,2048]{1,0:T(8,128)} %get-tuple-element.47), kind=kOutput, calls=%fused_computation.37 | convolution fusion | flops 17221812224 | bytes 33554432 | tf_op jit(solution)/shard_map/ti,td->id/dot_general | solution.py:150
  1186.4 22.2 %all-to-all-done.1 = bf16[2,256,16,128]{3,1,0,2:T(8,128)(2,1)S(1)} async-done(((bf16[2,256,16,128]{3,1,0,2:T(8,128)(2,1)}), bf16[2,256,16,128]{3,1,0,2:T(8,128)(2,1)S(1)}, u32[]{:S(2)}, u32[]{:S(2)}) %all-to-all-start.1) | async-done | bytes 2097184 | tf_op jit(solution)/shard_map/all_to_all | solution.py:44
  1314.1 35.0 %copy.118 = bf16[1024,2,1536]{2,1,0:T(2,128)(2,1)} copy(bf16[1024,2,1536]{2,0,1:T(8,128)(2,1)S(1)} %fusion.42) | data formatting | bytes 12582912 | tf_op jit(solution)/shard_map/transpose | solution.py:206
  1363.2 19.8 %convolution_convert_fusion.3 = bf16[2048,2048]{1,0:T(8,128)(2,1)} fusion(bf16[2048,1536]{1,0:T(8,128)(2,1)} %reshape.321, bf16[2048,1536]{1,0:T(8,128)(2,1)} %all-gather.15.cloned.1.call-done), kind=kOutput, calls=%fused_computation.40 | convolution fusion | flops 12889096192 | bytes 20971520 | tf_op jit(solution)/shard_map/te,de->td/dot_general | solution.py:209
  1408.6 26.8 %reduce-scatter.25.cloned.1.call-done = bf16[256,512]{1,0:T(8,128)(2,1)} async-done(((bf16[256,2048]{1,0:T(8,128)(2,1)}), bf16[256,512]{1,0:T(8,128)(2,1)}) %reduce-scatter.25.cloned.1.call-update) | async-done | bytes 262160 | tf_op jit(solution)/shard_map/reduce_scatter | solution.py:261
  1437.3 143.7 %reduce-scatter.19.cloned.1.call-done = bf16[512,2048]{1,0:T(8,128)(2,1)} async-done(((bf16[2048,2048]{1,0:T(8,128)(2,1)}), bf16[512,2048]{1,0:T(8,128)(2,1)}) %reduce-scatter.19.cloned.1.call-update) | async-done | bytes 2097168 | tf_op jit(solution)/shard_map/reduce_scatter | solution.py:208
  1597.9 23.9 %all-reduce.8 = (bf16[2048]{0:T(1024)(128)(2,1)S(1)}, bf16[2048]{0:T(1024)(128)(2,1)S(1)}, bf16[2048]{0:T(1024)(128)(2,1)S(1)}, bf16[2048]{0:T(1024)(128)(2,1)S(1)}) all-reduce(bf16[2048]{0:T(1024)(128)(2,1)S(1)} %get-tuple-element.11, bf16[2048]{0:T(1024)(128)(2,1)S(1)} %reduce_sum.235, ...), channel_id=7, replica_groups=mesh['dp'=8,'seq'=4] {'dp'}, use_global_device_ids=true, to_apply=%region_26.27.clone | all-reduce | flops 8192 | bytes 32768
  1644.3 30.0 %reduce-scatter.31.cloned.1.call-done = bf16[256,4]{1,0:T(8,128)(2,1)} async-done(((bf16[2048,4]{1,0:T(8,128)(2,1)}), bf16[256,4]{1,0:T(8,128)(2,1)}) %reduce-scatter.31.cloned.1.call-update) | async-done | bytes 2064
  1674.9 20.5 %reduce-scatter.33.cloned.1.call-done = bf16[64,4]{1,0:T(8,128)(2,1)} async-done(((bf16[256,4]{1,0:T(8,128)(2,1)}), bf16[64,4]{1,0:T(8,128)(2,1)}) %reduce-scatter.33.cloned.1.call-update) | async-done | bytes 528
  (316 shorter events, 358.6 us)
Async XLA Ops:
  7.2 49.4 %all-gather.17.cloned.1.call-start = ((), (), s32[]{:S(2)}) async-start(), calls=%async_computation.14 | async-start | bytes 1310720 | tf_op jit(solution)/shard_map/all_gather | solution.py:76
  7.9 79.5 %all-gather.15.cloned.1.call-start = ((), (), s32[]{:S(2)}) async-start(), calls=%async_computation.13 | async-start | bytes 7077888 | tf_op jit(solution)/shard_map/all_gather | solution.py:84
  8.7 230.6 %all-gather.13.cloned.1.call-start = ((), (), s32[]{:S(2)}) async-start(), calls=%async_computation.12 | async-start | bytes 10485760 | tf_op jit(solution)/shard_map/all_gather | solution.py:99
  56.5 378.7 %all-gather.19.cloned.1.call-start = ((), (), s32[]{:S(2)}) async-start(), calls=%async_computation.15 | async-start | bytes 9437184 | tf_op jit(solution)/shard_map/all_gather | solution.py:85
  57.1 428.0 %all-gather.27.cloned.1.call-start = ((), (), s32[]{:S(2)}) async-start(), calls=%async_computation.20 | async-start | bytes 10485760 | tf_op jit(solution)/shard_map/all_gather | solution.py:137
  57.7 484.2 %all-gather.25.cloned.1.call-start = ((), (), s32[]{:S(2)}) async-start(), calls=%async_computation.18 | async-start | bytes 9437184 | tf_op jit(solution)/shard_map/all_gather | solution.py:87
  58.2 540.0 %all-gather.23.cloned.1.call-start = ((), (), s32[]{:S(2)}) async-start(), calls=%async_computation.17 | async-start | bytes 9437184 | tf_op jit(solution)/shard_map/all_gather | solution.py:86
  297.1 132.7 %all-to-all-start = ((bf16[2,1024,4,128]{3,2,0,1:T(4,128)(2,1)}), bf16[2,1024,4,128]{3,2,0,1:T(4,128)(2,1)S(1)}, u32[]{:S(2)}, u32[]{:S(2)}) async-start(bf16[2,1024,4,128]{3,2,0,1:T(4,128)(2,1)} %copy.94), calls=%async_computation | async-start | bytes 4194304 | tf_op jit(solution)/shard_map/all_to_all | solution.py:48
  300.7 449.3 %all-gather.21.cloned.1.call-start = ((), (), s32[]{:S(2)}) async-start(), calls=%async_computation.16 | async-start | bytes 10485760 | tf_op jit(solution)/shard_map/all_gather | solution.py:136
  449.1 506.0 %reduce-scatter.17.cloned.1.call-start = ((), (), s32[]{:S(2)}) async-start(), calls=%async_computation.21 | async-start | bytes 10485760 | tf_op jit(solution)/shard_map/reduce_scatter | solution.py:155
  812.3 290.3 %reduce-scatter.15.cloned.1.call-start = ((), (), s32[]{:S(2)}) async-start(), calls=%async_computation.19 | async-start | bytes 10485760 | tf_op jit(solution)/shard_map/reduce_scatter | solution.py:143
  839.2 524.0 %reduce-scatter.23.cloned.1.call-start = ((), (), s32[]{:S(2)}) async-start(), calls=%async_computation.24 | async-start | bytes 9437184 | tf_op jit(solution)/shard_map/reduce_scatter | solution.py:235
  960.0 150.0 %copy-start.8 = (bf16[2,256,2048]{2,1,0:T(8,128)(2,1)S(1)}, bf16[2,256,2048]{2,1,0:T(8,128)(2,1)}, u32[]{:S(2)}) copy-start(bf16[2,256,2048]{2,1,0:T(8,128)(2,1)} %param.25) | copy-start | bytes 6291460
  1118.8 267.3 %reduce-scatter.27.cloned.1.call-start = ((), (), s32[]{:S(2)}) async-start(), calls=%async_computation.26 | async-start | bytes 9437184 | tf_op jit(solution)/shard_map/reduce_scatter | solution.py:238
  1155.5 53.1 %all-to-all-start.1 = ((bf16[2,256,16,128]{3,1,0,2:T(8,128)(2,1)}), bf16[2,256,16,128]{3,1,0,2:T(8,128)(2,1)S(1)}, u32[]{:S(2)}, u32[]{:S(2)}) async-start(bf16[2,256,16,128]{3,1,0,2:T(8,128)(2,1)} %copy.96), calls=%async_computation.3 | async-start | bytes 4194304 | tf_op jit(solution)/shard_map/all_to_all | solution.py:44
  1160.2 228.8 %reduce-scatter.29.cloned.1.call-start = ((), (), s32[]{:S(2)}) async-start(), calls=%async_computation.27 | async-start | bytes 9437184 | tf_op jit(solution)/shard_map/reduce_scatter | solution.py:241
  1186.3 219.8 %reduce-scatter.21.cloned.1.call-start = ((), (), s32[]{:S(2)}) async-start(), calls=%async_computation.23 | async-start | bytes 7077888 | tf_op jit(solution)/shard_map/reduce_scatter | solution.py:232
  1309.7 125.7 %reduce-scatter.25.cloned.1.call-start = ((), (), s32[]{:S(2)}) async-start(), calls=%async_computation.25 | async-start | bytes 1310720 | tf_op jit(solution)/shard_map/reduce_scatter | solution.py:261
  1363.2 217.7 %reduce-scatter.19.cloned.1.call-start = ((), (), s32[]{:S(2)}) async-start(), calls=%async_computation.22 | async-start | bytes 10485760 | tf_op jit(solution)/shard_map/reduce_scatter | solution.py:208
  1383.1 291.2 %reduce-scatter.31.cloned.1.call-start = ((), (), s32[]{:S(2)}) async-start(), calls=%async_computation.28 | async-start | bytes 589824
  1437.2 154.0 %copy-start.19 = (f32[4,1,512]{2,1,0:T(1,128)S(1)}, f32[4,1,512]{2,1,0:T(1,128)}, u32[]{:S(2)}) copy-start(f32[4,1,512]{2,1,0:T(1,128)} %copy-done.18) | copy-start | bytes 24580
  1437.2 154.1 %copy-start.23 = (f32[512]{0:T(512)S(1)}, f32[512]{0:T(512)}, u32[]{:S(2)}) copy-start(f32[512]{0:T(512)} %copy-done.22) | copy-start | bytes 6148
  1437.3 154.1 %copy-start.27 = (f32[512]{0:T(512)S(1)}, f32[512]{0:T(512)}, u32[]{:S(2)}) copy-start(f32[512]{0:T(512)} %copy-done.26) | copy-start | bytes 6148
  1643.7 51.8 %reduce-scatter.33.cloned.1.call-start = ((), (), s32[]{:S(2)}) async-start(), calls=%async_computation.29 | async-start | bytes 81920
  (69 other events, 913.1 us)
Sparse Core Ops, SparseCore 0:
  9.6 30.8 all-gather.16
  42.4 44.9 all-gather.14
  89.6 149.6 all-gather.12
  241.0 52.5 all-gather.18
  295.0 189.9 all-gather.26
  486.8 55.0 all-gather.24
  543.8 54.3 all-gather.22
  600.3 149.6 all-gather.20
  812.4 142.6 reduce-scatter.16
  957.4 145.1 reduce-scatter.14
  1119.0 71.9 reduce-scatter.22
  1194.7 71.2 reduce-scatter.26
  1269.5 71.2 reduce-scatter.28
  1344.4 61.7 reduce-scatter.20
  1408.3 27.1 reduce-scatter.24
  1437.8 143.1 reduce-scatter.18
  1643.8 30.4 reduce-scatter.30
  1676.4 18.9 reduce-scatter.32
where the time goes:
time: 1710 us; the launch traced here: 1700 us
  waiting for transfers between devices  974 us (57%)
  matrix products  314 us (18%)
  blocking collectives  203 us (12%)
  local copies, waits for them, and re-layouts  114 us (7%)
  other arithmetic  71.1 us (4%)
  between operations  18.2 us (1%)
    all_gather x1, waiting for transfers between devices, shards(): lax.all_gather(normed_one.reshape(seq_count, local_len, width), 'seq', ax...  152 us
    all_gather x1, waiting for transfers between devices, shards(): lax.all_gather(normed_two, 'seq', axis=0, tiled=True)  152 us
    reduce_scatter x1, waiting for transfers between devices, shards(): lax.psum_scatter(jnp.einsum('te,de->td', piece, qkv_full, preferred_eleme...  144 us
    reduce_scatter x1, waiting for transfers between devices, shards(): lax.psum_scatter(jnp.dot(piece, down_full, preferred_element_type=f32).as...  143 us
    reduce_scatter x1, waiting for transfers between devices, shards(): lax.psum_scatter(jnp.einsum('ti,di->td', piece, up_full, preferred_elemen...  116 us
    all_gather x1, blocking collectives, shards(): lax.all_gather(ln2_bias, 'seq', axis=0, tiled=True)  107 us
    all_gather x1, waiting for transfers between devices, shards(): lax.all_gather(w_down, 'dp', axis=1, tiled=True)  56.8 us
    unnamed x20, waiting for transfers between devices  54.3 us
  transfers between devices with their start and end apart: 20, of which 14 were waited for; matrix products, arithmetic and copies ran while one was open for 22% of the time, Pallas kernels for 0%

commit v1 on v0

--- a/solution.py
+++ b/solution.py
@@ -3,6 +3,8 @@
 import jax
 import jax.numpy as jnp
 from jax import lax
+from jax.experimental import pallas as pl
+from jax.experimental.pallas import tpu as pltpu
 from jax.sharding import PartitionSpec as P
 
 HEADS = 16
@@ -48,7 +50,7 @@
     return lax.all_to_all(values_in, "seq", split_axis=1, concat_axis=2, tiled=True)
 
 
-def shards(
+def plain_shards(
     tokens,
     token_types,
     view_mask,
@@ -292,6 +294,1089 @@
     )
 
 
+PLANE = 8
+QUAD = 4
+F32 = jnp.float32
+BF16 = jnp.bfloat16
+MESH_ID = pl.DeviceIdType.MESH
+CORE, X_WAY, Y_WAY = 1, 2, 4
+FAR_FIRST = (6, 7, 2, 3, 4, 5, 1)
+
+
+def swap(value, mask):
+    dp = lax.axis_size("dp")
+    return lax.ppermute(value, "dp", [(i, i ^ mask) for i in range(dp)])
+
+
+def after(value, *earlier):
+    return lax.optimization_barrier((value, earlier))[0]
+
+
+def at_plane(d, z):
+    return dict(device_id=(d, z), device_id_type=MESH_ID)
+
+
+class Moves:
+    def __init__(self, send_sem, recv_sem, local_sem=None):
+        self.sems = (send_sem, recv_sem, local_sem)
+        self.count = [0, 0]
+        self.open = []
+
+    def far(self, source, target, d, z, sends=None, receives=None, lands=None):
+        number = self.count[0]
+        self.count[0] += 1
+
+        def copy(landing):
+            return pltpu.make_async_remote_copy(
+                src_ref=source,
+                dst_ref=target,
+                send_sem=self.sems[0].at[number],
+                recv_sem=self.sems[1].at[landing],
+                **at_plane(d, z),
+            )
+
+        out = copy(number if lands is None else lands)
+        when(sends, out.start)
+        move = [(out, copy(number)), sends, receives, False]
+        self.open.append(move)
+        return move
+
+    def here(self, source, target, sends=None):
+        number = self.count[1]
+        self.count[1] += 1
+        copy = pltpu.make_async_copy(source, target, self.sems[2].at[number])
+        when(sends, copy.start)
+        move = [copy, sends, None, False]
+        self.open.append(move)
+        return move
+
+    def landed(self, move):
+        copy, sends, receives, done = move
+        assert not done
+        move[3] = True
+        if isinstance(copy, tuple):
+            when(receives, copy[1].wait_recv)
+        else:
+            when(sends, copy.wait)
+
+    def finish(self):
+        for move in self.open:
+            if not move[3]:
+                self.landed(move)
+            if isinstance(move[0], tuple):
+                when(move[1], move[0][0].wait_send)
+
+
+def when(condition, do):
+    if condition is None:
+        do()
+    else:
+        pl.when(condition)(do)
+
+
+def meet_all(masks, lines=True, peers=False):
+    d = lax.axis_index("dp")
+    z = lax.axis_index("seq")
+    groups = lax.axis_size("seq")
+    barrier = pltpu.get_barrier_semaphore()
+    count = len(masks)
+    for mask in masks:
+        pl.semaphore_signal(barrier, inc=1, **at_plane(d ^ mask, z))
+    if lines:
+        count = count + groups - 1
+        for step in range(1, groups):
+            pl.semaphore_signal(barrier, inc=1, **at_plane(d, (z + step) % groups))
+    if peers:
+        for number in range(2):
+            to_d, to_z, itself = peer_of(number)
+            away = jnp.logical_not(itself)
+
+            def signal(to_d=to_d, to_z=to_z):
+                pl.semaphore_signal(barrier, inc=1, **at_plane(to_d, to_z))
+
+            when(away, signal)
+            count = count + jnp.where(itself, 0, 1)
+    pl.semaphore_wait(barrier, count)
+
+
+def peer_of(number):
+    d = lax.axis_index("dp")
+    z = lax.axis_index("seq")
+    core = d & 1
+    to_d = (d - core) + (z >> 1)
+    to_z = 2 * core + number
+    return to_d, to_z, jnp.logical_and(to_d == d, to_z == z)
+
+
+def exchange_along_z(moves, number, source, target, base=None):
+    z = lax.axis_index("seq")
+    base = moves.count[0] - number if base is None else base
+    to_d, to_z, itself = peer_of(number)
+    away = jnp.logical_not(itself)
+    far = moves.far(source, target(z & 1), to_d, to_z, away, away, base + (z & 1))
+    near = moves.here(source, target(z & 1), itself)
+    return far, near
+
+
+def all_landed(moves, landing):
+    for move in landing:
+        moves.landed(move)
+
+
+def intake_kernel(small_ref, mark_ref, qkv_ref, whole_ref, marks_ref, half_ref, *sems):
+    moves = Moves(*sems)
+    d = lax.axis_index("dp")
+    z = lax.axis_index("seq")
+    groups = lax.axis_size("seq")
+    meet_all(range(1, PLANE))
+    moves.here(small_ref, whole_ref.at[z])
+    for step in range(1, groups):
+        moves.far(small_ref, whole_ref.at[z], d, (z + step) % groups)
+    moves.here(mark_ref, marks_ref.at[0])
+    for mask in range(1, PLANE):
+        moves.far(mark_ref, marks_ref.at[mask], d ^ mask, z)
+    spread_columns(moves, qkv_ref, half_ref)
+    moves.finish()
+
+
+def spread_columns(moves, shard, half):
+    d = lax.axis_index("dp")
+    z = lax.axis_index("seq")
+    part, width = half.shape[0], shard.shape[1]
+    target = half.at[:, pl.ds(pl.multiple_of(d * width, 128), width)]
+
+    def rows(mask):
+        return shard.at[pl.ds(pl.multiple_of((d ^ mask) * part, 64), part)]
+
+    moves.here(rows(0), target)
+    for mask in FAR_FIRST:
+        moves.far(rows(mask), target, d ^ mask, z)
+
+
+def kernel_call(
+    kernel, inputs, outputs, far, here, number, name, traffic, spaces=None, scratch=(), late=()
+):
+    count = len(inputs)
+
+    def body(*refs):
+        kernel(*refs[:count], *refs[count + len(late) :])
+
+    return pl.pallas_call(
+        body,
+        out_shape=outputs,
+        in_specs=[pl.BlockSpec(memory_space=space) for space in spaces or [pltpu.VMEM] * count]
+        + [pl.BlockSpec(memory_space=pl.ANY)] * len(late),
+        out_specs=[pl.BlockSpec(memory_space=pl.ANY)] * len(outputs),
+        scratch_shapes=[
+            *scratch,
+            pltpu.SemaphoreType.DMA((far,)),
+            pltpu.SemaphoreType.DMA((far,)),
+            pltpu.SemaphoreType.DMA((here,)),
+        ],
+        compiler_params=pltpu.CompilerParams(
+            collective_id=number, has_side_effects=True, vmem_limit_bytes=56 * 1024 * 1024
+        ),
+        cost_estimate=pl.CostEstimate(
+            flops=0, bytes_accessed=traffic * 3 * 1024 * 1024, transcendentals=0
+        ),
+        name=name,
+    )(*inputs, *late)
+
+
+def shaped(*shape):
+    return jax.ShapeDtypeStruct(shape, BF16)
+
+
+def intake(small, mark, qkv_shard):
+    groups = lax.axis_size("seq")
+    units, width = qkv_shard.shape
+    return kernel_call(
+        intake_kernel,
+        [small, mark, qkv_shard],
+        [
+            shaped(groups, *small.shape),
+            jax.ShapeDtypeStruct((PLANE,) + mark.shape, mark.dtype),
+            shaped(units // PLANE, width * PLANE),
+        ],
+        groups - 1 + 2 * (PLANE - 1),
+        3,
+        1,
+        "intake",
+        20,
+    )
+
+
+def gather_rows(moves, rows_ref, chips_ref, others_ref, ready=None, pieces=2):
+    d = lax.axis_index("dp")
+    z = lax.axis_index("seq")
+    size = chips_ref.shape[1] // pieces
+    parts = [pl.ds(number * size, size) for number in range(pieces)]
+    order = [i + j for i in range(pieces // 2) for j in (0, pieces // 2)]
+
+    def far(source, target, mask):
+        return moves.far(source, target, d ^ mask, z)
+
+    if ready is None:
+        moves.here(rows_ref, chips_ref.at[0])
+    over_x = {}
+    over_y = {}
+    for number in order:
+        part = parts[number]
+        if ready is None:
+            source = rows_ref.at[part]
+        else:
+            ready(number)
+            source = chips_ref.at[0, part]
+        over_x[number] = far(source, chips_ref.at[1, part], X_WAY)
+        over_y[number] = far(source, chips_ref.at[2, part], Y_WAY)
+        far(source, others_ref.at[0, part], CORE)
+
+    def pass_on(chip, number):
+        part = parts[number]
+        far(chips_ref.at[chip, part], others_ref.at[chip, part], CORE)
+
+    corner = {}
+    for number in order:
+        yield
+        part = parts[number]
+        first = number < pieces // 2
+        via, chip, mask = (over_y, 2, X_WAY) if first else (over_x, 1, Y_WAY)
+        moves.landed(via[number])
+        corner[number] = far(chips_ref.at[chip, part], chips_ref.at[3, part], mask)
+        pass_on(chip, number)
+        moves.landed((over_x if first else over_y)[number])
+        pass_on(3 - chip, number)
+    yield
+    for number in order:
+        moves.landed(corner[number])
+        pass_on(3, number)
+
+
+GATHER_COPIES = 14
+FIRST_PIECES = 4
+
+
+def gather_along_z(moves, shard_ref, place, target):
+    d = lax.axis_index("dp")
+    z = lax.axis_index("seq")
+    own = moves.here(shard_ref, target.at[place(z)])
+    arrivals = []
+    for step in (2, -2, 1, -1):
+        to, source = z + step, z - step
+        inside = jnp.logical_and(to >= 0, to < 4)
+        comes = jnp.logical_and(source >= 0, source < 4)
+        arrivals.append(
+            moves.far(shard_ref, target.at[place(z)], d, jnp.clip(to, 0, 3), inside, comes)
+        )
+    yield
+    for arrival in arrivals:
+        moves.landed(arrival)
+    for end, via, to in ((0, 2, 3), (3, 1, 0)):
+        arrivals.append(
+            moves.far(target.at[place(end)], target.at[place(end)], d, to, z == via, z == to)
+        )
+    yield
+    for arrival in arrivals[4:] + [own]:
+        moves.landed(arrival)
+
+
+Z_COPIES = 6
+
+
+def first_kernel(rows_ref, qkv_ref, up_ref, down_ref, *refs):
+    chips, others, heads, up_half, down_half = refs[:5]
+    moves = Moves(*refs[5:])
+    d = lax.axis_index("dp")
+    core = d & 1
+    half = rows_ref.shape[1]
+    meet_all(range(1, PLANE), peers=True)
+    size = 2 * half // FIRST_PIECES
+    landing = {}
+    for piece in range(FIRST_PIECES // 2):
+        for number in range(2):
+            landing[number * (FIRST_PIECES // 2) + piece] = exchange_along_z(
+                moves,
+                number,
+                rows_ref.at[number, pl.ds(piece * size, size)],
+                lambda at: chips.at[
+                    0, pl.ds(pl.multiple_of(at * half + piece * size, size), size)
+                ],
+            )
+    spread_columns(moves, up_ref, up_half)
+    spread_columns(moves, down_ref, down_half)
+
+    def place(at):
+        own = (at >> 1) == core
+        return jnp.where(own, (at & 1) * 2 + core, 4 + (at & 1))
+
+    qkv = gather_along_z(moves, qkv_ref, place, heads)
+    next(qkv)
+    rows = gather_rows(
+        moves,
+        None,
+        chips,
+        others,
+        lambda number: all_landed(moves, landing[number]),
+        FIRST_PIECES,
+    )
+    for _ in range(FIRST_PIECES):
+        next(rows)
+    next(qkv)
+    next(rows)
+    next(qkv, None)
+    z = lax.axis_index("seq")
+    for number in range(2):
+        moves.far(heads.at[4 + number], heads.at[number * 2 + core], d ^ CORE, z)
+    next(rows, None)
+    moves.finish()
+
+
+def first_gather(rows, qkv_half, up_shard, down_shard):
+    seqs, half, width = rows.shape
+    spread = [shaped(w.shape[0] // PLANE, w.shape[1] * PLANE) for w in (up_shard, down_shard)]
+    return kernel_call(
+        first_kernel,
+        [rows, qkv_half, up_shard, down_shard],
+        [
+            shaped(4, seqs * half, width),
+            shaped(4, seqs * half, width),
+            shaped(6, *qkv_half.shape),
+            *spread,
+        ],
+        7 * FIRST_PIECES + Z_COPIES + FIRST_PIECES + 2 + 2 * (PLANE - 1),
+        3 + FIRST_PIECES,
+        2,
+        "first_gather",
+        110,
+    )
+
+
+def gather_kernel(rows_ref, chips, others, *sems):
+    moves = Moves(*sems)
+    meet_all((CORE, X_WAY, Y_WAY), lines=False)
+    for _ in gather_rows(moves, rows_ref, chips, others):
+        pass
+    moves.finish()
+
+
+def plane_gather_now(rows, number, late):
+    count, width = rows.shape
+    got = kernel_call(
+        gather_kernel,
+        [rows],
+        [shaped(4, count, width)] * 2,
+        GATHER_COPIES,
+        1,
+        number,
+        "plane_gather",
+        76,
+        late=late,
+    )
+    return [part.reshape(4 * count, width) for part in got]
+
+
+def scatter_rows(moves, natural, chips_ref, others_ref, out_ref, own, got, far, near, done):
+    d = lax.axis_index("dp")
+    z = lax.axis_index("seq")
+    half = own.shape[1] // 2
+    first, second = pl.ds(0, half), pl.ds(half, half)
+
+    def send_to(source, target, mask):
+        return moves.far(source, target, d ^ mask, z)
+
+    order = (3, 1, 2, 0)
+    from_core = [send_to(others_ref.at[c], got.at[i], CORE) for i, c in enumerate(order)]
+    reads = [moves.here(chips_ref.at[c], own.at[i]) for i, c in enumerate(order)]
+    step = 64
+
+    def add(target, start, sources):
+        @pl.loop(0, half // step)
+        def _(i):
+            total = None
+            for ref, offset in sources:
+                piece = ref[pl.ds(pl.multiple_of(offset + i * step, step), step), :].astype(F32)
+                total = piece if total is None else total + piece
+            target[pl.ds(pl.multiple_of(start + i * step, step), step), :] = total.astype(
+                target.dtype
+            )
+
+    def ready(i):
+        moves.landed(from_core[i])
+        moves.landed(reads[i])
+
+    yield
+    ready(0)
+    add(own.at[0], 0, [(own.at[0], 0), (got.at[0], 0)])
+    to_x = send_to(own.at[0, first], far.at[0], X_WAY)
+    add(own.at[0], half, [(own.at[0], half), (got.at[0], half)])
+    to_y = send_to(own.at[0, second], far.at[1], Y_WAY)
+    ready(1)
+    add(own.at[1], 0, [(own.at[1], 0), (got.at[1], 0)])
+    x_first = send_to(own.at[1, first], near.at[0, first], X_WAY)
+    ready(2)
+    add(own.at[2], half, [(own.at[2], half), (got.at[2], half)])
+    y_second = send_to(own.at[2, second], near.at[1, second], Y_WAY)
+    yield
+    moves.landed(to_y)
+    add(own.at[1], half, [(own.at[1], half), (got.at[1], half), (far.at[1], 0)])
+    x_second = send_to(own.at[1, second], near.at[0, second], X_WAY)
+    moves.landed(to_x)
+    add(own.at[2], 0, [(own.at[2], 0), (got.at[2], 0), (far.at[0], 0)])
+    y_first = send_to(own.at[2, first], near.at[1, first], Y_WAY)
+    ready(3)
+    yield
+    moves.landed(x_first)
+    moves.landed(y_second)
+    for number, arrivals in ((0, (y_first,)), (1, (x_second,))):
+        all_landed(moves, arrivals)
+        start = number * half
+        add(done, start, [(own.at[3], start), (got.at[3], start), (near.at[0], start), (near.at[1], start)])
+        if natural:
+            exchange_along_z(
+                moves,
+                number,
+                done.at[pl.ds(start, half)],
+                lambda at: out_ref.at[at],
+            )
+    if not natural:
+        moves.here(done, out_ref)
+
+
+SCATTER_COPIES = 10
+
+
+def scatter_kernel(natural, united, *refs):
+    count = len(natural)
+    ins, refs = refs[: 2 * count], refs[2 * count :]
+    held, refs = refs[:united], refs[united:]
+    outs, refs = refs[:count], refs[count:]
+    shard, refs = refs[:united], refs[united:]
+    buffers = refs[: 5 * count]
+    moves = Moves(*refs[5 * count :])
+    meet_all(range(1, PLANE) if united else (CORE, X_WAY, Y_WAY), lines=False, peers=any(natural))
+    if united:
+        unite_columns(moves, held[0], shard[0])
+    steps = [
+        scatter_rows(
+            moves, natural[i], *ins[2 * i : 2 * i + 2], outs[i], *buffers[5 * i : 5 * i + 5]
+        )
+        for i in range(count)
+    ]
+    for _ in range(4):
+        for step in steps:
+            next(step, None)
+    moves.finish()
+
+
+def plane_scatter_now(parts, shapes, natural, number, late=(), united=()):
+    inputs = []
+    scratch = []
+    for pair in parts:
+        total, width = pair[0].shape
+        count = total // 4
+        inputs += [part.reshape(4, count, width) for part in pair]
+        for lead, rows in ((4, count), (4, count), (2, count // 2), (2, count)):
+            scratch.append(pltpu.VMEM((lead, rows, width), BF16))
+        scratch.append(pltpu.VMEM((count, width), BF16))
+    count = len(united)
+    return kernel_call(
+        lambda *refs: scatter_kernel(natural, count, *refs),
+        inputs + list(united),
+        [shaped(*shape) for shape in shapes]
+        + [shaped(s.shape[0] * PLANE, s.shape[1] // PLANE) for s in united],
+        SCATTER_COPIES * len(parts) + 2 + count * (PLANE - 1),
+        7 * len(parts) + count,
+        number,
+        "plane_scatter",
+        100 if any(natural) else 76,
+        [pl.ANY] * len(inputs) + [pltpu.VMEM] * count,
+        scratch,
+        late,
+    )
+
+
+def unite_columns(moves, half_ref, shard_ref):
+    d = lax.axis_index("dp")
+    z = lax.axis_index("seq")
+    part, width = half_ref.shape[0], shard_ref.shape[1]
+    target = shard_ref.at[pl.ds(pl.multiple_of(d * part, 64), part)]
+
+    def columns(mask):
+        return half_ref.at[:, pl.ds(pl.multiple_of((d ^ mask) * width, 128), width)]
+
+    moves.here(columns(0), target)
+    for mask in FAR_FIRST:
+        moves.far(columns(mask), target, d ^ mask, z)
+
+
+def along_z(value):
+    return lax.all_gather(value, "seq", axis=0, tiled=True)
+
+
+def sum_along_z(grad):
+    return lax.psum_scatter(grad, "seq", scatter_dimension=0, tiled=True)
+
+
+def shared_heads(grad):
+    heads = HEADS // PLANE
+    held = grad.reshape(heads, 2, -1, grad.shape[-1])
+    second = lax.axis_index("dp") % 2 == 1
+    keep = jnp.where(second, held[:, 1], held[:, 0])
+    other = swap(jnp.where(second, held[:, 0], held[:, 1]), CORE)
+    whole = jnp.concatenate([jnp.where(second, other, keep), jnp.where(second, keep, other)])
+    return whole.reshape(-1, grad.shape[-1])
+
+
+def plane_gather(rows, second, third):
+    half = rows.shape[0] // 2
+    x_rows = swap(rows, X_WAY)
+    y_rows = swap(rows, Y_WAY)
+    corner_first = swap(after(y_rows[:half], second), X_WAY)
+    corner_second = swap(after(x_rows[half:], second), Y_WAY)
+    chips = jnp.concatenate([rows, x_rows, y_rows, after(corner_first, third), corner_second])
+    return chips, swap(chips, CORE)
+
+
+def plane_scatter(chips, others):
+    count = chips.shape[0] // 4
+    half = count // 2
+    got = swap(others, CORE)
+
+    def both(start, size):
+        return chips[start : start + size].astype(F32) + got[start : start + size].astype(F32)
+
+    far_first = swap(both(3 * count, half).astype(BF16), X_WAY)
+    far_second = swap(both(3 * count + half, half).astype(BF16), Y_WAY)
+    x_first = swap(both(count, half).astype(BF16), X_WAY)
+    y_second = swap(both(2 * count + half, half).astype(BF16), Y_WAY)
+    x_second = swap((both(count + half, half) + far_second.astype(F32)).astype(BF16), X_WAY)
+    y_first = swap((both(2 * count, half) + far_first.astype(F32)).astype(BF16), Y_WAY)
+    first = both(0, half) + x_first.astype(F32) + y_first.astype(F32)
+    second = both(half, half) + x_second.astype(F32) + y_second.astype(F32)
+    return jnp.concatenate([first, second])
+
+
+def place_of(mask):
+    return (mask & 1) * (PLANE // 2) + (mask >> 1)
+
+
+def column_of(holder, member, number):
+    head = (2 * (member & 1) + number) * (PLANE // 2) + (member >> 1)
+    place = place_of(holder ^ (head >> 1))
+    return pl.ds(pl.multiple_of((2 * place + (head & 1)) * HEAD_DIM, HEAD_DIM), HEAD_DIM)
+
+
+def meet_heads(masks):
+    d = lax.axis_index("dp")
+    z = lax.axis_index("seq")
+    core = d & 1
+    groups = lax.axis_size("seq")
+    inside = (z >> 1) == core
+    barrier = pltpu.get_barrier_semaphore()
+
+    def greet(to_d, to_z, maybe_itself):
+        def signal():
+            pl.semaphore_signal(barrier, inc=1, **at_plane(to_d, to_z))
+
+        when(jnp.logical_or(to_d != d, to_z != z) if maybe_itself else None, signal)
+
+    for line in range(PLANE // 2):
+        for to_z in range(groups):
+            greet(((d >> 1) ^ line) * 2 + (z >> 1), to_z, line == 0)
+    for mask in range(PLANE):
+        for j in range(2):
+            greet(d ^ mask, 2 * core + j, mask == 0)
+    for mask in masks:
+        greet(d ^ mask, z, False)
+    pl.semaphore_wait(barrier, 4 * PLANE + len(masks) - jnp.where(inside, 2, 0))
+
+
+def contexts_home_kernel(chip_ref, other_ref, rows_ref, out_ref, out_chips, out_others, *sems):
+    moves = Moves(*sems)
+    d = lax.axis_index("dp")
+    z = lax.axis_index("seq")
+    core = d & 1
+    heads = HEADS // PLANE
+    half = out_ref.shape[1]
+    meet_heads((CORE, X_WAY, Y_WAY))
+    comes = []
+    for j in range(2):
+        comes += [2 * core + j != z] * heads + [None] * ((PLANE - 1) * heads)
+    for line in (3, 1, 2, 0):
+        to_d = ((d >> 1) ^ line) * 2 + (z >> 1)
+        for slot, source in ((0, chip_ref), (1, other_ref)):
+            for part in range(2):
+                to_z = 2 * (core ^ slot) + part
+                itself = jnp.logical_and(to_d == d, to_z == z)
+                for number in range(heads):
+                    here = source.at[
+                        line, pl.ds(part * half, half), pl.ds(number * HEAD_DIM, HEAD_DIM)
+                    ]
+                    there = out_ref.at[z & 1, :, column_of(to_d, d, number)]
+                    moves.far(
+                        here,
+                        there,
+                        to_d,
+                        to_z,
+                        jnp.logical_not(itself) if line == 0 else None,
+                        comes[moves.count[0]],
+                        ((z & 1) * PLANE + (d ^ to_d)) * heads + number,
+                    )
+                    if line == 0:
+                        moves.here(here, there, itself)
+    for _ in gather_rows(moves, rows_ref, out_chips, out_others):
+        pass
+    moves.finish()
+
+
+def contexts_home(context, out_rows):
+    lines, rows, columns = context[0].shape
+    count, width = out_rows.shape
+    heads = HEADS // PLANE
+    out, chips, others = kernel_call(
+        contexts_home_kernel,
+        [*context, out_rows],
+        [shaped(2, rows // 2, width), shaped(4, count, width), shaped(4, count, width)],
+        2 * PLANE * heads + GATHER_COPIES,
+        4 * heads + 1,
+        3,
+        "contexts_home",
+        60,
+    )
+    return out.reshape(rows, width), chips.reshape(-1, width), others.reshape(-1, width)
+
+
+def gradients_out_kernel(count, in_ref, *refs):
+    sums, out_ref, shards = refs[:count], refs[count], refs[count + 1 : 2 * count + 1]
+    moves = Moves(*refs[2 * count + 1 :])
+    d = lax.axis_index("dp")
+    z = lax.axis_index("seq")
+    core = d & 1
+    heads = HEADS // PLANE
+    half = in_ref.shape[1]
+    meet_heads(range(1, PLANE))
+    comes = []
+    for side in range(2):
+        for line in range(PLANE // 2):
+            for part in range(2):
+                itself = jnp.logical_and((z >> 1) == core, 2 * (core ^ side) + part == z)
+                comes += [jnp.logical_not(itself) if line == 0 else None] * heads
+    for mask in FAR_FIRST + (0,):
+        for j in range(2):
+            to_d = d ^ mask
+            to_z = 2 * core + j
+            line = mask >> 1
+            side = (to_d & 1) ^ (z >> 1)
+            for number in range(heads):
+                here = in_ref.at[j, :, column_of(d, to_d, number)]
+                there = out_ref.at[
+                    side,
+                    line,
+                    pl.ds(pl.multiple_of((z & 1) * half, half), half),
+                    pl.ds(number * HEAD_DIM, HEAD_DIM),
+                ]
+                moves.far(
+                    here,
+                    there,
+                    to_d,
+                    to_z,
+                    to_z != z if mask == 0 else None,
+                    comes[moves.count[0]],
+                    ((side * (PLANE // 2) + line) * 2 + (z & 1)) * heads + number,
+                )
+                if mask == 0:
+                    moves.here(here, there, to_z == z)
+    for held, shard in zip(sums, shards):
+        unite_columns(moves, held, shard)
+    moves.finish()
+
+
+def gradients_out(grad, sums):
+    rows, width = grad.shape
+    heads = HEADS // PLANE
+    count = len(sums)
+    return kernel_call(
+        lambda *refs: gradients_out_kernel(count, *refs),
+        [grad.reshape(2, rows // 2, width), *sums],
+        [shaped(2, PLANE // 2, rows, heads * HEAD_DIM)]
+        + [shaped(s.shape[0] * PLANE, s.shape[1] // PLANE) for s in sums],
+        2 * PLANE * heads + count * (PLANE - 1),
+        2 * heads + count,
+        4,
+        "gradients_out",
+        50,
+    )
+
+
+SEQS = 4
+
+
+def masked_scores(left, right, first_row, first_column, row_axis, flag, full_len):
+    plain = lax.dot_general(
+        left, right, (((1,), (1,)), ((), ())), preferred_element_type=F32
+    ) * (1.0 / math.sqrt(HEAD_DIM))
+    rows = first_row + lax.broadcasted_iota(jnp.int32, plain.shape, row_axis)
+    columns = first_column + lax.broadcasted_iota(jnp.int32, plain.shape, 1 - row_axis)
+    seen = jnp.logical_or(flag == 1, columns % (full_len // 2) < full_len // 4)
+    return jnp.where(jnp.logical_and(columns <= rows, seen), plain, NEGATIVE)
+
+
+def attend_kernel(half, block, core, flag, qkv, context, lse):
+    for part in range(2):
+        here = part ^ core
+        for first in range(0, half, block):
+            query = qkv[here][0, first : first + block, :HEAD_DIM]
+            spans = [(here, part, first + block)]
+            if part == 1:
+                spans = [(core, 0, half)] + spans
+            scores = []
+            for slot, place, length in spans:
+                keys = qkv[slot][0, :length, HEAD_DIM : 2 * HEAD_DIM]
+                scores.append(
+                    masked_scores(
+                        query, keys, part * half + first, place * half, 0, flag, 2 * half
+                    )
+                )
+            top = jnp.max(scores[0], axis=-1, keepdims=True)
+            for more in scores[1:]:
+                top = jnp.maximum(top, jnp.max(more, axis=-1, keepdims=True))
+            expd = [jnp.exp(piece - top) for piece in scores]
+            total = sum(jnp.sum(piece, axis=-1, keepdims=True) for piece in expd)
+            result = 0.0
+            for (slot, _, length), piece in zip(spans, expd):
+                values = qkv[slot][0, :length, 2 * HEAD_DIM :]
+                result = result + jnp.dot(
+                    (piece / total).astype(BF16), values, preferred_element_type=F32
+                )
+            context[here][0, first : first + block, :] = result.astype(BF16)
+            wide = jnp.broadcast_to(top + jnp.log(total), (block, HEAD_DIM))
+            lse[here][0, 0, :, first : first + block] = jnp.transpose(wide)[:8]
+
+
+def attend(qkv, flags, heads):
+    half = qkv[0].shape[1]
+    spot = lambda s, h: (s, 0, h)
+
+    def kernel(flags_ref, *refs):
+        for core in range(2):
+
+            @pl.when(flags_ref[SEQS] == core)
+            def _():
+                flag = flags_ref[pl.program_id(0)]
+                attend_kernel(half, half // 2, core, flag, refs[:2], refs[2:4], refs[4:])
+
+    out = pl.pallas_call(
+        kernel,
+        grid=(SEQS, heads),
+        in_specs=[pl.BlockSpec(memory_space=pltpu.SMEM)]
+        + [pl.BlockSpec((1, half, 3 * HEAD_DIM), spot)] * 2,
+        out_specs=[pl.BlockSpec((1, half, HEAD_DIM), spot)] * 2
+        + [pl.BlockSpec((1, 1, 8, half), lambda s, h: (s, h, 0, 0))] * 2,
+        out_shape=[jax.ShapeDtypeStruct((SEQS, half, heads * HEAD_DIM), BF16)] * 2
+        + [jax.ShapeDtypeStruct((SEQS, heads, 8, half), F32)] * 2,
+        cost_estimate=pl.CostEstimate(
+            flops=48 * heads * half * half * HEAD_DIM,
+            bytes_accessed=64 * heads * half * HEAD_DIM,
+            transcendentals=16 * heads * half * half,
+        ),
+        name="attend",
+    )(flags, *qkv)
+    return out[:2], out[2:]
+
+
+def attend_back_kernel(half, block, core, flag, qkv, grads, lse, out, grad_keys, grad_values):
+    scale = 1.0 / math.sqrt(HEAD_DIM)
+    grad_keys[...] = jnp.zeros_like(grad_keys)
+    grad_values[...] = jnp.zeros_like(grad_values)
+    for part in range(2):
+        here = part ^ core
+        for first in range(0, half, block):
+            query = qkv[here][0, first : first + block, :HEAD_DIM]
+            grad = grads[here, 0, first : first + block, :]
+            level = lse[here][0, 0, 0:1, first : first + block]
+            spans = [(here, part, first + block)]
+            if part == 1:
+                spans = [(core, 0, half)] + spans
+            held = []
+            weighted = 0.0
+            for slot, place, length in spans:
+                keys = qkv[slot][0, :length, HEAD_DIM : 2 * HEAD_DIM]
+                values = qkv[slot][0, :length, 2 * HEAD_DIM :]
+                scores = masked_scores(
+                    keys, query, part * half + first, place * half, 1, flag, 2 * half
+                )
+                probs = jnp.exp(scores - level)
+                grad_values[place, :length, :] += jnp.dot(
+                    probs.astype(BF16), grad, preferred_element_type=F32
+                )
+                grad_probs = lax.dot_general(
+                    values, grad, (((1,), (1,)), ((), ())), preferred_element_type=F32
+                )
+                weighted = weighted + jnp.sum(probs * grad_probs, axis=0, keepdims=True)
+                held.append((probs, grad_probs, keys))
+            grad_query = 0.0
+            for (_, place, length), (probs, grad_probs, keys) in zip(spans, held):
+                grad_scores = (probs * (grad_probs - weighted)).astype(BF16)
+                grad_keys[place, :length, :] += jnp.dot(
+                    grad_scores, query, preferred_element_type=F32
+                )
+                grad_query = grad_query + lax.dot_general(
+                    grad_scores, keys, (((0,), (0,)), ((), ())), preferred_element_type=F32
+                )
+            out[here][0, first : first + block, :HEAD_DIM] = (grad_query * scale).astype(BF16)
+    for part in range(2):
+        target = out[part ^ core]
+        target[0, :, HEAD_DIM : 2 * HEAD_DIM] = (grad_keys[part] * scale).astype(BF16)
+        target[0, :, 2 * HEAD_DIM :] = grad_values[part].astype(BF16)
+
+
+def attend_back(qkv, grads, lse, flags, heads):
+    half = qkv[0].shape[1]
+    spot = lambda s, h: (s, 0, h)
+
+    def kernel(flags_ref, *refs):
+        for core in range(2):
+
+            @pl.when(flags_ref[SEQS] == core)
+            def _():
+                flag = flags_ref[pl.program_id(0)]
+                attend_back_kernel(
+                    half, half // 2, core, flag, refs[:2], refs[2], refs[3:5], refs[5:7], *refs[7:]
+                )
+
+    return pl.pallas_call(
+        kernel,
+        grid=(SEQS, heads),
+        in_specs=[pl.BlockSpec(memory_space=pltpu.SMEM)]
+        + [pl.BlockSpec((1, half, 3 * HEAD_DIM), spot)] * 2
+        + [pl.BlockSpec((2, 1, half, HEAD_DIM), lambda s, h: (0, s, 0, h))]
+        + [pl.BlockSpec((1, 1, 8, half), lambda s, h: (s, h, 0, 0))] * 2,
+        out_specs=[pl.BlockSpec((1, half, 3 * HEAD_DIM), spot)] * 2,
+        out_shape=[jax.ShapeDtypeStruct(qkv[0].shape, BF16)] * 2,
+        scratch_shapes=[
+            pltpu.VMEM((2, half, HEAD_DIM), F32),
+            pltpu.VMEM((2, half, HEAD_DIM), F32),
+        ],
+        cost_estimate=pl.CostEstimate(
+            flops=128 * heads * half * half * HEAD_DIM,
+            bytes_accessed=128 * heads * half * HEAD_DIM,
+            transcendentals=16 * heads * half * half,
+        ),
+        name="attend_back",
+    )(flags, *qkv, grads, *lse)
+
+
+def sum_everywhere(sums, late):
+    dp = lax.axis_size("dp")
+    seq = lax.axis_size("seq")
+    count = dp * seq
+    kinds, width = sums.shape
+    piece = width // count
+    lanes = 128
+    pieces = jnp.transpose(sums.reshape(kinds, count, piece), (1, 0, 2))
+    pieces = pieces.reshape(count, kinds * piece // lanes, lanes)
+
+    def kernel(in_ref, late_ref, out_ref, got, send_sem, got_sem):
+        d = lax.axis_index("dp")
+        z = lax.axis_index("seq")
+        me = d * seq + z
+        mesh_id = pl.DeviceIdType.MESH
+        barrier = pltpu.get_barrier_semaphore()
+        for far in range(1, count):
+            to = (me + far) % count
+            pl.semaphore_signal(
+                barrier, inc=1, device_id=(to // seq, to % seq), device_id_type=mesh_id
+            )
+        pl.semaphore_wait(barrier, count - 1)
+        copies = []
+        for far in range(1, count):
+            to = (me + far) % count
+            copy = pltpu.make_async_remote_copy(
+                src_ref=in_ref.at[to],
+                dst_ref=got.at[far],
+                send_sem=send_sem.at[far],
+                recv_sem=got_sem.at[far],
+                device_id=(to // seq, to % seq),
+                device_id_type=mesh_id,
+            )
+            copy.start()
+            copies.append(copy)
+        total = in_ref[me]
+        for far in range(1, count):
+            copies[far - 1].wait()
+            total = total + got[far]
+        out_ref[...] = total
+
+    summed = pl.pallas_call(
+        kernel,
+        out_shape=jax.ShapeDtypeStruct(pieces.shape[1:], F32),
+        in_specs=[pl.BlockSpec(memory_space=pltpu.VMEM), pl.BlockSpec(memory_space=pl.ANY)],
+        out_specs=pl.BlockSpec(memory_space=pltpu.VMEM),
+        scratch_shapes=[
+            pltpu.VMEM(pieces.shape, F32),
+            pltpu.SemaphoreType.DMA((count,)),
+            pltpu.SemaphoreType.DMA((count,)),
+        ],
+        compiler_params=pltpu.CompilerParams(collective_id=0, has_side_effects=True),
+        name="sum_everywhere",
+    )(pieces, late)
+    return summed.reshape(kinds, piece)
+
+
+def grouped_shards(
+    tokens,
+    token_types,
+    view_mask,
+    type_table,
+    ln1_gain,
+    ln1_bias,
+    w_qkv,
+    w_out,
+    ln2_gain,
+    ln2_bias,
+    w_up,
+    w_down,
+    cotangent,
+):
+    seq_count, local_len, width = tokens.shape
+    groups = lax.axis_size("seq")
+    rows = seq_count * local_len
+    heads = HEADS // PLANE
+    d = lax.axis_index("dp")
+    z = lax.axis_index("seq")
+
+    small = jnp.concatenate(
+        [type_table, jnp.stack([ln1_gain, ln1_bias, ln2_gain, ln2_bias])], axis=0
+    )
+    mark = jnp.broadcast_to(view_mask[:, None, None], (seq_count, 4, 128)).reshape(8, 128)
+    out_columns = along_z(jnp.transpose(w_out))
+    small, marks, qkv_half = intake(small, mark, jnp.transpose(w_qkv))
+    small = jnp.swapaxes(small, 0, 1).reshape(2 * TYPES, width).astype(F32)
+    table = small[:TYPES]
+    gain_one, bias_one, gain_two, bias_two = (small[TYPES + i] for i in range(4))
+    marks = lax.dynamic_index_in_dim(marks[:, ::4, 0], z & 1, 1, keepdims=False)
+    marks = lax.dynamic_index_in_dim(
+        marks.reshape(SEQS, 2), (d & 1) ^ (z >> 1), 1, keepdims=False
+    )
+    flags = jnp.concatenate([marks, (d & 1)[None]])
+
+    types = token_types.reshape(rows)
+    onehot = (types[:, None] == jnp.arange(TYPES, dtype=jnp.int32)[None, :]).astype(F32)
+    start_hidden = tokens.reshape(rows, width).astype(F32) + jnp.dot(
+        onehot, table, precision=HIGHEST_PRECISION
+    )
+    cot = cotangent.reshape(rows, width)
+    norm_one, pull_one = jax.vjp(layer_norm, start_hidden, gain_one, bias_one)
+    chips, others, qkv_full, up_half, down_half = first_gather(
+        norm_one.astype(BF16).reshape(tokens.shape),
+        qkv_half,
+        jnp.transpose(w_up),
+        w_down,
+    )
+    up_full = along_z(up_half)
+    down_full = along_z(down_half)
+    normed = [part.reshape(4 * rows, width) for part in (chips, others)]
+    qkv_full = qkv_full[:4].reshape(-1, width)
+    qkv = [
+        jnp.einsum("td,ed->te", part, qkv_full, preferred_element_type=F32)
+        .astype(BF16)
+        .reshape(SEQS, rows, 3 * heads * HEAD_DIM)
+        for part in normed
+    ]
+    context, lse = attend(qkv, flags, heads)
+    context_rows, out_chips, out_others = contexts_home(
+        context, jnp.transpose(out_columns)
+    )
+    cots = plane_gather(after(cot, chips), context, context_rows)
+    mid_hidden = (
+        start_hidden
+        + jnp.dot(context_rows[:, : width // 2], out_chips, preferred_element_type=F32)
+        + jnp.dot(context_rows[:, width // 2 :], out_others, preferred_element_type=F32)
+    )
+    norm_two, pull_two = jax.vjp(layer_norm, mid_hidden, gain_two, bias_two)
+    ffn_input = plane_gather_now(norm_two.astype(BF16), 5, cots)
+    def weight_grad(left, right):
+        return sum(
+            jnp.einsum("ti,td->id", a, b, preferred_element_type=F32)
+            for a, b in zip(left, right)
+        ).astype(BF16)
+
+    def times(parts, weight):
+        return [jnp.dot(part, weight, preferred_element_type=F32).astype(BF16) for part in parts]
+
+    ups = [
+        jnp.einsum("td,id->ti", part, up_full, preferred_element_type=F32) for part in ffn_input
+    ]
+    acts = [gelu_tanh(up_value).astype(BF16) for up_value in ups]
+    ffn_out = plane_scatter(*times(acts, down_full))
+    grad_ups = []
+    for cot_part, up_value in zip(cots, ups):
+        grad_act = jnp.einsum("td,id->ti", cot_part, down_full, preferred_element_type=F32)
+        grad_ups.append(jax.vjp(gelu_tanh, up_value)[1](grad_act)[0].astype(BF16))
+    down_grad = weight_grad(acts, cots)
+    up_grad = weight_grad(grad_ups, ffn_input)
+    down_sum = sum_along_z(down_grad)
+    up_sum = sum_along_z(up_grad)
+    grad_parts = times(grad_ups, up_full)
+    (grad_normed_two,) = plane_scatter_now(
+        [grad_parts], [(rows, width)], [False], 6, [down_sum, up_grad, ffn_out]
+    )
+    grad_normed_two = grad_normed_two.astype(F32)
+    grad_mid_norm, grad_gain_two, grad_bias_two = pull_two(grad_normed_two)
+    grad_mid = cot.astype(F32) + grad_mid_norm
+    grad_mid_low = grad_mid.astype(BF16)
+    grad_context = jnp.concatenate(
+        [
+            jnp.einsum("te,de->td", grad_mid_low, part, preferred_element_type=F32).astype(BF16)
+            for part in (out_chips, out_others)
+        ],
+        axis=1,
+    )
+    output = (mid_hidden + ffn_out).astype(BF16).reshape(tokens.shape)
+    grad_by_heads, up_shard, down_shard = gradients_out(grad_context, [up_sum, down_sum])
+    grad_qkv = attend_back(qkv, grad_by_heads, lse, flags, heads)
+    grad_qkv = [part.reshape(SEQS * rows, 3 * heads * HEAD_DIM) for part in grad_qkv]
+    grad_out_weight = [
+        jnp.einsum("td,te->de", part, grad_mid_low, preferred_element_type=F32).astype(BF16)
+        for part in jnp.split(context_rows, 2, axis=1)
+    ]
+    qkv_grad = shared_heads(weight_grad(grad_qkv, normed))
+    qkv_sum = sum_along_z(qkv_grad)
+    out_sum = plane_scatter(*grad_out_weight).astype(BF16)
+    grad_normed_one, qkv_shard = plane_scatter_now(
+        [times(grad_qkv, qkv_full)], [tokens.shape], [True], 7, [out_sum], [qkv_sum]
+    )
+    grad_normed_one = grad_normed_one.astype(F32)
+    out_sum = sum_along_z(jnp.transpose(out_sum))
+    sum_qkv = jnp.transpose(qkv_shard)
+    sum_up = jnp.transpose(up_shard)
+    sum_down = down_shard
+    grad_start_norm, grad_gain_one, grad_bias_one = pull_one(grad_normed_one.reshape(rows, width))
+    grad_start = grad_mid + grad_start_norm
+    grad_table = jnp.einsum("tk,td->kd", onehot, grad_start, precision=HIGHEST_PRECISION)
+    sums = jnp.concatenate(
+        [
+            grad_table,
+            jnp.stack([grad_gain_one, grad_bias_one, grad_gain_two, grad_bias_two]),
+        ],
+        axis=0,
+    )
+    sums = sum_everywhere(sums, out_sum)
+    return (
+        output,
+        grad_start.reshape(tokens.shape),
+        sums[:TYPES],
+        sums[TYPES],
+        sums[TYPES + 1],
+        sum_qkv.astype(F32),
+        jnp.transpose(out_sum).astype(F32),
+        sums[TYPES + 2],
+        sums[TYPES + 3],
+        sum_up.astype(F32),
+        sum_down.astype(F32),
+    )
+
+
 def solution(mesh):
     placed = (
         P("dp", "seq", None),
@@ -308,8 +1393,9 @@
         P("seq", "dp"),
         P("dp", "seq", None),
     )
+    fits = mesh.shape["dp"] == 8 and mesh.shape["seq"] == 4
     return jax.shard_map(
-        shards,
+        grouped_shards if fits else plain_shards,
         mesh=mesh,
         in_specs=placed,
         out_specs=(

time: 1710 us -> 1110 us (0.65)
  waiting for transfers between devices: 974 us -> 62.6 us
  Pallas kernels: 0 us -> 617 us
  blocking collectives: 203 us -> 0 us
  local copies, waits for them, and re-layouts: 114 us -> 46.1 us
  matrix products: 314 us -> 259 us
  starting transfers between devices: 8.93 us -> 37.2 us
    pallas_call x0 -> x10, Pallas kernels: none -> 617 us  [the longest x7 550 us: kernel_call(): pl.pallas_call(body, out_shape=outputs, in_specs=[pl.BlockSpec(memory_spa...]
    all_gather x8 -> x3, waiting for transfers between devices: 454 us -> 0.04 us  [along_z(): return lax.all_gather(value, 'seq', axis=0, tiled=True)]
    reduce_scatter x8 -> x4, waiting for transfers between devices: 443 us -> 0.03 us  [sum_along_z(): return lax.psum_scatter(grad, 'seq', scatter_dimension=0, tiled=True)]
    all_gather x5 -> x0, blocking collectives: 168 us -> none  [the longest x1 107 us: shards(): lax.all_gather(ln2_bias, 'seq', axis=0, tiled=True)]
    ppermute x0 -> x20, waiting for transfers between devices: none -> 62.4 us  [swap(): return lax.ppermute(value, 'dp', [(i, i ^ mask) for i in range(dp)])]
    dot_general x38 -> x26, matrix products: 314 us -> 259 us  [the longest x6 76.6 us: weight_grad(): jnp.einsum('ti,td->id', a, b, preferred_element_type=F32)]
    unnamed x20 -> x7, waiting for transfers between devices: 54.3 us -> 0.11 us
    ppermute x0 -> x20, starting transfers between devices: none -> 36.3 us  [swap(): return lax.ppermute(value, 'dp', [(i, i ^ mask) for i in range(dp)])]
  transfers between devices with their start and end apart: 20 -> 27, of which waited for: 14 -> 13; matrix products, arithmetic and copies ran while one was open for 22% -> 31% of each run, Pallas kernels for 0% -> 41%
where the time goes in v1:
time: 1110 us; the launch traced here: 1100 us
  Pallas kernels  617 us (56%)
  matrix products  259 us (23%)
  other arithmetic  66.4 us (6%)
  waiting for transfers between devices  62.6 us (6%)
  local copies, waits for them, and re-layouts  46.1 us (4%)
  starting transfers between devices  37.2 us (3%)
  between operations  15.6 us (1%)
    pallas_call x7, Pallas kernels, kernel_call(): pl.pallas_call(body, out_shape=outputs, in_specs=[pl.BlockSpec(memory_spa...  550 us
    dot_general x6, matrix products, weight_grad(): jnp.einsum('ti,td->id', a, b, preferred_element_type=F32)  76.6 us
    dot_general x6, matrix products, times(): jnp.dot(part, weight, preferred_element_type=F32).astype(BF16)  75.1 us
    ppermute x20, waiting for transfers between devices, swap(): return lax.ppermute(value, 'dp', [(i, i ^ mask) for i in range(dp)])  62.4 us
    dot_general x2, matrix products, grouped_shards(): jnp.einsum('td,id->ti', cot_part, down_full, preferred_element_type=F32)  40.6 us
    ppermute x20, starting transfers between devices, swap(): return lax.ppermute(value, 'dp', [(i, i ^ mask) for i in range(dp)])  36.3 us
    dot_general x2, matrix products, grouped_shards(): jnp.einsum('td,id->ti', part, up_full, preferred_element_type=F32)  26.2 us
    pallas_call x1, Pallas kernels, attend_back(): pl.pallas_call(kernel, grid=(SEQS, heads), in_specs=[pl.BlockSpec(memory_...  25.1 us
  transfers between devices with their start and end apart: 27, of which 13 were waited for; matrix products, arithmetic and copies ran while one was open for 31% of the time, Pallas kernels for 41%

profile of v1, /device:TPU:0, one launch (start us, length us, event | category | flops | bytes accessed | tf_op | source)
XLA Modules:
  0.0 1103.9 jit_solution(13171383421745422020)
XLA Ops:
  15.9 16.3 %intake.1 = (bf16[4,8,512]{2,1,0:T(8,128)(2,1)}, s32[8,8,128]{2,1,0:T(8,128)}, bf16[192,2048]{1,0:T(8,128)(2,1)}) custom-call(bf16[8,512]{1,0:T(8,128)(2,1)} %concatenate.36.refs_0_, s32[8,128]{1,0:T(8,128)} %broadcast_in_dim.32.refs_1_, bf16[1536,256]{1,0:T(8,128)(2,1)} %bitcast.170), custom_call_target="tpu_custom_call" | custom-call | bytes 62914560 | tf_op jit(solution)/shard_map/intake/pallas_call | solution.py:464
  39.7 120.7 %first_gather.1 = (bf16[4,512,2048]{2,1,0:T(8,128)(2,1)}, bf16[4,512,2048]{2,1,0:T(8,128)(2,1)}, bf16[6,192,2048]{2,1,0:T(8,128)(2,1)}, bf16[256,2048]{1,0:T(8,128)(2,1)}, bf16[256,2048]{1,0:T(8,128)(2,1)}) custom-call(bf16[2,256,2048]{2,1,0:T(8,128)(2,1)} %bitcast.164, bf16[192,2048]{1,0:T(8,128)(2,1)} %get-tuple-element.41.refs_1_, ...), custom_call_target="tpu_custom_call" | custom-call | bytes 346030080 | tf_op jit(solution)/shard_map/first_gather/pallas_call | solution.py:464
  165.2 11.6 %convolution_convert_fusion.8 = bf16[2048,768]{1,0:T(8,128)(2,1)} fusion(bf16[2048,2048]{1,0:T(8,128)(2,1)} %bitcast.190, bf16[768,2048]{1,0:T(8,128)(2,1)S(1)} %bitcast.166), kind=kOutput, calls=%fused_computation.62 | convolution fusion | flops 6444023808 | bytes 14680064 | tf_op jit(solution)/shard_map/td,ed->te/dot_general | solution.py:1281
  186.8 19.7 %attend.1 = (bf16[4,512,256]{2,1,0:T(8,128)(2,1)}, bf16[4,512,256]{2,1,0:T(8,128)(2,1)}, f32[4,2,8,512]{3,2,1,0:T(8,128)}, f32[4,2,8,512]{3,2,1,0:T(8,128)}) custom-call(s32[5]{0:T(128)} %pad_add_fusion.flags_ref, bf16[4,512,768]{2,1,0:T(8,128)(2,1)} %bitcast.210, bf16[4,512,768]{2,1,0:T(8,128)(2,1)} %bitcast.208), custom_call_target="tpu_custom_call" | custom-call | flops 3221225472 | bytes 8388608 | tf_op jit(solution)/shard_map/attend/pallas_call | solution.py:1068
  216.8 81.7 %contexts_home.1 = (bf16[2,256,2048]{2,1,0:T(8,128)(2,1)}, bf16[4,256,2048]{2,1,0:T(8,128)(2,1)}, bf16[4,256,2048]{2,1,0:T(8,128)(2,1)}) custom-call(bf16[4,512,256]{2,1,0:T(8,128)(2,1)} %get-tuple-element.45.refs_0_, bf16[4,512,256]{2,1,0:T(8,128)(2,1)} %get-tuple-element.46.refs_1_, bf16[256,2048]{1,0:T(8,128)(2,1)} %bitcast.173), custom_call_target="tpu_custom_call" | custom-call | bytes 188743680 | tf_op jit(solution)/shard_map/contexts_home/pallas_call | solution.py:464
  308.5 15.9 %collective-permute-start.4 = (bf16[2048,2048]{1,0:T(8,128)(2,1)}, bf16[2048,2048]{1,0:T(8,128)(2,1)}, u32[]{:S(2)}, u32[]{:S(2)}) collective-permute-start(bf16[2048,2048]{1,0:T(8,128)(2,1)} %constant_dynamic-update-slice_fusion.refs_1_), channel_id=1, source_target_pairs={{0,4},{4,0},{8,12},{12,8},{16,20},{20,16},{24,28},{28,24},{1,5},{5... | collective-permute-start | bytes 25165832 | tf_op jit(solution)/shard_map/ppermute | solution.py:308
  337.6 79.7 %plane_gather.1 = (bf16[4,512,2048]{2,1,0:T(8,128)(2,1)}, bf16[4,512,2048]{2,1,0:T(8,128)(2,1)}) custom-call(bf16[512,2048]{1,0:T(8,128)(2,1)} %add_convert_fusion.3.refs_0_, bf16[2048,2048]{1,0:T(8,128)(2,1)} %constant_dynamic-update-slice_fusion.refs_1_, bf16[2048,2048]{1,0:T(8,128)(2,1)} %collective-permute-done.4.refs_2_), custom_call_target="tpu_custom_call" | custom-call | bytes 239075328 | tf_op jit(solution)/shard_map/plane_gather/pallas_call | solution.py:464
  417.4 14.7 %fusion.48 = f32[2048,1024]{1,0:T(8,128)} fusion(bf16[2048,2048]{1,0:T(8,128)(2,1)} %bitcast.198, bf16[1024,2048]{1,0:T(8,128)(2,1)} %all-gather.6.cloned.1.call-done), kind=kOutput, calls=%fused_computation.135 | convolution fusion | flops 8589934592 | bytes 20971520 | tf_op jit(solution)/shard_map/td,id->ti/dot_general | solution.py:1308
  432.1 11.4 %fusion.47 = f32[2048,1024]{1,0:T(8,128)} fusion(bf16[2048,2048]{1,0:T(8,128)(2,1)S(1)} %bitcast.194, bf16[1024,2048]{1,0:T(8,128)(2,1)S(1)} %copy-done.42), kind=kOutput, calls=%fused_computation.134 | convolution fusion | flops 8589934592 | bytes 20971520 | tf_op jit(solution)/shard_map/td,id->ti/dot_general | solution.py:1308
  443.5 15.0 %fusion.40 = f32[1024,2048]{1,0:T(8,128)S(1)} fusion(bf16[2048,2048]{1,0:T(8,128)(2,1)} %collective-permute-done.4.refs_2_, f32[2048,1024]{1,0:T(8,128)} %fusion.48), kind=kOutput, calls=%fused_computation.129 | convolution fusion | flops 8608808960 | bytes 25165824 | tf_op jit(solution)/shard_map/ti,td->id/dot_general | solution.py:1300
  458.6 14.7 %add_convert_fusion.1 = bf16[1024,2048]{1,0:T(8,128)(2,1)} fusion(f32[1024,2048]{1,0:T(8,128)S(1)} %fusion.40, bf16[2048,2048]{1,0:T(8,128)(2,1)S(1)} %bitcast.153, f32[2048,1024]{1,0:T(8,128)} %fusion.47), kind=kOutput, calls=%fused_computation.21 | convolution fusion | flops 8613003264 | bytes 29360128 | tf_op jit(solution)/shard_map/ti,td->id/dot_general | solution.py:1300
  473.4 16.4 %convolution_convert_fusion.4 = bf16[2048,2048]{1,0:T(8,128)(2,1)} fusion(bf16[1024,2048]{1,0:T(8,128)(2,1)} %all-gather.8.cloned.1.call-done, f32[2048,1024]{1,0:T(8,128)} %fusion.48), kind=kOutput, calls=%fused_computation.30 | convolution fusion | flops 8613003264 | bytes 20971520 | tf_op jit(solution)/shard_map/dot_general | solution.py:1305
  490.2 16.7 %convolution_convert_fusion.5 = bf16[2048,2048]{1,0:T(8,128)(2,1)} fusion(bf16[1024,2048]{1,0:T(8,128)(2,1)S(1)} %copy-done.44, f32[2048,1024]{1,0:T(8,128)} %fusion.47), kind=kOutput, calls=%fused_computation.31 | convolution fusion | flops 8613003264 | bytes 20971520 | tf_op jit(solution)/shard_map/dot_general | solution.py:1305
  506.9 21.2 %fusion.5 = bf16[2048,1024]{1,0:T(8,128)(2,1)} fusion(f32[2048,1024]{1,0:T(8,128)} %fusion.48, bf16[2048,2048]{1,0:T(8,128)(2,1)} %collective-permute-done.4.refs_2_, bf16[1024,2048]{1,0:T(8,128)(2,1)} %all-gather.8.cloned.1.call-done), kind=kOutput, calls=%fused_computation.11 | convolution fusion | flops 8640266240 | bytes 25165824 | tf_op jit(solution)/shard_map/td,id->ti/dot_general | solution.py:1314
  528.1 19.4 %fusion.9 = bf16[2048,1024]{1,0:T(8,128)(2,1)} fusion(f32[2048,1024]{1,0:T(8,128)} %fusion.47, bf16[2048,2048]{1,0:T(8,128)(2,1)S(1)} %bitcast.155, bf16[1024,2048]{1,0:T(8,128)(2,1)} %all-gather.8.cloned.1.call-done), kind=kOutput, calls=%fused_computation.15 | convolution fusion | flops 8640266240 | bytes 25165824 | tf_op jit(solution)/shard_map/td,id->ti/dot_general | solution.py:1314
  553.8 14.7 %fusion.49 = f32[1024,2048]{1,0:T(8,128)} fusion(bf16[2048,1024]{1,0:T(8,128)(2,1)S(1)} %copy-done.52, bf16[2048,2048]{1,0:T(8,128)(2,1)} %bitcast.199), kind=kOutput, calls=%fused_computation.136 | convolution fusion | flops 8589934592 | bytes 20971520 | tf_op jit(solution)/shard_map/ti,td->id/dot_general | solution.py:1300
  582.5 12.2 %add_convert_fusion.refs_3_ = bf16[1024,2048]{1,0:T(8,128)(2,1)} fusion(f32[1024,2048]{1,0:T(8,128)} %fusion.49, bf16[2048,1024]{1,0:T(8,128)(2,1)S(1)} %copy-done.50, bf16[2048,2048]{1,0:T(8,128)(2,1)S(1)} %bitcast.197), kind=kOutput, calls=%fused_computation.20 | convolution fusion | flops 8594128896 | bytes 25165824 | tf_op jit(solution)/shard_map/ti,td->id/dot_general | solution.py:1300
  611.7 11.1 %convolution_convert_fusion.2 = bf16[2048,2048]{1,0:T(8,128)(2,1)} fusion(bf16[2048,1024]{1,0:T(8,128)(2,1)S(1)} %copy-done.53, bf16[1024,2048]{1,0:T(8,128)(2,1)S(1)} %copy-done.43), kind=kOutput, calls=%fused_computation.28 | convolution fusion | flops 8594128896 | bytes 16777216 | tf_op jit(solution)/shard_map/dot_general | solution.py:1305
  623.5 13.0 %collective-permute-done.9 = bf16[256,2048]{1,0:T(8,128)(2,1)S(1)} collective-permute-done((bf16[256,2048]{1,0:T(8,128)(2,1)S(1)}, bf16[256,2048]{1,0:T(8,128)(2,1)S(1)}, u32[]{:S(2)}, u32[]{:S(2)}) %collective-permute-start.9) | collective-permute-done | bytes 1048608 | tf_op jit(solution)/shard_map/ppermute | solution.py:308
  660.2 77.8 %plane_scatter.2 = bf16[512,2048]{1,0:T(8,128)(2,1)} custom-call(bf16[4,512,2048]{2,1,0:T(8,128)(2,1)} %bitcast.160, bf16[4,512,2048]{2,1,0:T(8,128)(2,1)} %bitcast.159, bf16[256,2048]{1,0:T(8,128)(2,1)} %reduce-scatter.5.cloned.1.call-done.refs_2_, bf16[1024,2048]{1,0:T(8,128)(2,1)} %add_convert_fusion.refs_3_, f32[512,2048]{1,0:T(8,128)} %pad_maximum_fusion.refs_4_), custom_call_target="tpu_custom_call" | custom-call | bytes 239075328 | tf_op jit(solution)/shard_map/plane_scatter/pallas_call | solution.py:464
  758.9 60.7 %gradients_out.1 = (bf16[2,4,512,256]{3,2,1,0:T(8,128)(2,1)}, bf16[2048,256]{1,0:T(8,128)(2,1)}, bf16[2048,256]{1,0:T(8,128)(2,1)}) custom-call(bf16[2,256,2048]{2,1,0:T(8,128)(2,1)} %bitcast.163, bf16[256,2048]{1,0:T(8,128)(2,1)} %reduce-scatter.7.cloned.1.call-done.refs_1_, bf16[256,2048]{1,0:T(8,128)(2,1)} %reduce-scatter.5.cloned.1.call-done.refs_2_), custom_call_target="tpu_custom_call" | custom-call | bytes 157286400 | tf_op jit(solution)/shard_map/gradients_out/pallas_call | solution.py:464
  819.5 25.1 %attend_back.1 = (bf16[4,512,768]{2,1,0:T(8,128)(2,1)}, bf16[4,512,768]{2,1,0:T(8,128)(2,1)}) custom-call(s32[5]{0:T(128)} %pad_add_fusion.flags_ref, bf16[4,512,768]{2,1,0:T(8,128)(2,1)} %bitcast.211, bf16[4,512,768]{2,1,0:T(8,128)(2,1)} %bitcast.209, bf16[2,4,512,256]{3,2,1,0:T(8,128)(2,1)} %get-tuple-element.58.refs_2_, ...), custom_call_target="tpu_custom_call" | custom-call | flops 8589934592 | bytes 16777216 | tf_op jit(solution)/shard_map/attend_back/pallas_call | solution.py:1147
  940.4 113.4 %plane_scatter.3 = (bf16[2,256,2048]{2,1,0:T(8,128)(2,1)}, bf16[1536,256]{1,0:T(8,128)(2,1)}) custom-call(bf16[4,512,2048]{2,1,0:T(8,128)(2,1)} %bitcast.162, bf16[4,512,2048]{2,1,0:T(8,128)(2,1)} %bitcast.161, bf16[192,2048]{1,0:T(8,128)(2,1)} %reduce-scatter.9.cloned.1.call-done.refs_2_, bf16[256,2048]{1,0:T(8,128)(2,1)} %copy.45.refs_3_), custom_call_target="tpu_custom_call" | custom-call | bytes 314572800 | tf_op jit(solution)/shard_map/plane_scatter/pallas_call | solution.py:464
  1070.5 21.5 %sum_everywhere.1 = f32[4,128]{1,0:T(4,128)} custom-call(f32[32,4,128]{2,1,0:T(4,128)} %reshape.224.in_ref, bf16[512,256]{1,0:T(8,128)(2,1)} %reduce-scatter.11.cloned.1.call-done.late_ref), custom_call_target="tpu_custom_call" | custom-call | tf_op jit(solution)/shard_map/sum_everywhere/pallas_call | solution.py:1210
  (283 shorter events, 263.7 us)
Async XLA Ops:
  7.2 209.6 %all-gather.4.cloned.1.call-start = ((), (), s32[]{:S(2)}) async-start(), calls=%async_computation.4 | async-start | bytes 1310720 | tf_op jit(solution)/shard_map/all_gather | solution.py:813
  160.5 48.1 %collective-permute-start.1 = (bf16[512,2048]{1,0:T(8,128)(2,1)S(1)}, bf16[512,2048]{1,0:T(8,128)(2,1)}, u32[]{:S(2)}, u32[]{:S(2)}) collective-permute-start(bf16[512,2048]{1,0:T(8,128)(2,1)S(1)} %bitcast.148), channel_id=1, source_target_pairs={{0,16},{4,20},{8,24},{12,28},{16,0},{20,4},{24,8},{28,12},{1,17},{... | collective-permute-start | bytes 6291464 | tf_op jit(solution)/shard_map/ppermute | solution.py:308
  162.0 50.5 %collective-permute-start = (bf16[512,2048]{1,0:T(8,128)(2,1)S(1)}, bf16[512,2048]{1,0:T(8,128)(2,1)}, u32[]{:S(2)}, u32[]{:S(2)}) collective-permute-start(bf16[512,2048]{1,0:T(8,128)(2,1)S(1)} %bitcast.149), channel_id=1, source_target_pairs={{0,8},{4,12},{8,0},{12,4},{16,24},{20,28},{24,16},{28,20},{1,9},{5... | collective-permute-start | bytes 6291464 | tf_op jit(solution)/shard_map/ppermute | solution.py:308
  162.7 254.7 %all-gather.6.cloned.1.call-start = ((), (), s32[]{:S(2)}) async-start(), calls=%async_computation.5 | async-start | bytes 5242880 | tf_op jit(solution)/shard_map/all_gather | solution.py:813
  210.8 94.3 %collective-permute-start.2 = (bf16[256,2048]{1,0:T(8,128)(2,1)}, bf16[256,2048]{1,0:T(8,128)(2,1)S(1)}, u32[]{:S(2)}, u32[]{:S(2)}) collective-permute-start(bf16[256,2048]{1,0:T(8,128)(2,1)} %slice.221), channel_id=1, source_target_pairs={{0,8},{4,12},{8,0},{12,4},{16,24},{20,28},{24,16},{28,20},{1,9},{5... | collective-permute-start | bytes 3145736 | tf_op jit(solution)/shard_map/ppermute | solution.py:308
  212.5 260.9 %all-gather.8.cloned.1.call-start = ((), (), s32[]{:S(2)}) async-start(), calls=%async_computation.6 | async-start | bytes 5242880 | tf_op jit(solution)/shard_map/all_gather | solution.py:813
  214.8 91.4 %collective-permute-start.3 = (bf16[256,2048]{1,0:T(8,128)(2,1)}, bf16[256,2048]{1,0:T(8,128)(2,1)}, u32[]{:S(2)}, u32[]{:S(2)}) collective-permute-start(bf16[256,2048]{1,0:T(8,128)(2,1)} %slice.222), channel_id=1, source_target_pairs={{0,16},{4,20},{8,24},{12,28},{16,0},{20,4},{24,8},{28,12},{1,17},{... | collective-permute-start | bytes 3145736 | tf_op jit(solution)/shard_map/ppermute | solution.py:308
  308.5 29.1 %collective-permute-start.4 = (bf16[2048,2048]{1,0:T(8,128)(2,1)}, bf16[2048,2048]{1,0:T(8,128)(2,1)}, u32[]{:S(2)}, u32[]{:S(2)}) collective-permute-start(bf16[2048,2048]{1,0:T(8,128)(2,1)} %constant_dynamic-update-slice_fusion.refs_1_), channel_id=1, source_target_pairs={{0,4},{4,0},{8,12},{12,8},{16,20},{20,16},{24,28},{28,24},{1,5},{5... | collective-permute-start | bytes 25165832 | tf_op jit(solution)/shard_map/ppermute | solution.py:308
  324.5 335.7 %reduce-scatter.5.cloned.1.call-start = ((), (), s32[]{:S(2)}) async-start(), calls=%async_computation.7 | async-start | bytes 5242880 | tf_op jit(solution)/shard_map/reduce_scatter | solution.py:817
  473.3 285.6 %reduce-scatter.7.cloned.1.call-start = ((), (), s32[]{:S(2)}) async-start(), calls=%async_computation.8 | async-start | bytes 5242880 | tf_op jit(solution)/shard_map/reduce_scatter | solution.py:817
  489.8 57.7 %collective-permute-start.5 = (bf16[2048,2048]{1,0:T(8,128)(2,1)}, bf16[2048,2048]{1,0:T(8,128)(2,1)S(1)}, u32[]{:S(2)}, u32[]{:S(2)}) collective-permute-start(bf16[2048,2048]{1,0:T(8,128)(2,1)} %convolution_convert_fusion.4), channel_id=1, source_target_pairs={{0,4},{4,0},{8,12},{12,8},{16,20},{20,16},{24,28},{28,24},{1,5},{5... | collective-permute-start | bytes 25165832 | tf_op jit(solution)/shard_map/ppermute | solution.py:308
  552.5 26.0 %collective-permute-start.7 = (bf16[256,2048]{1,0:T(8,128)(2,1)S(1)}, bf16[256,2048]{1,0:T(8,128)(2,1)S(1)}, u32[]{:S(2)}, u32[]{:S(2)}) collective-permute-start(bf16[256,2048]{1,0:T(8,128)(2,1)S(1)} %get-tuple-element.100), channel_id=1, source_target_pairs={{0,8},{4,12},{8,0},{12,4},{16,24},{20,28},{24,16},{28,20},{1,9},{5... | collective-permute-start | bytes 3145736 | tf_op jit(solution)/shard_map/ppermute | solution.py:308
  568.4 31.8 %collective-permute-start.6 = (bf16[256,2048]{1,0:T(8,128)(2,1)}, bf16[256,2048]{1,0:T(8,128)(2,1)S(1)}, u32[]{:S(2)}, u32[]{:S(2)}) collective-permute-start(bf16[256,2048]{1,0:T(8,128)(2,1)} %get-tuple-element.99), channel_id=1, source_target_pairs={{0,8},{4,12},{8,0},{12,4},{16,24},{20,28},{24,16},{28,20},{1,9},{5... | collective-permute-start | bytes 3145736 | tf_op jit(solution)/shard_map/ppermute | solution.py:308
  581.2 23.8 %collective-permute-start.8 = (bf16[256,2048]{1,0:T(8,128)(2,1)}, bf16[256,2048]{1,0:T(8,128)(2,1)S(1)}, u32[]{:S(2)}, u32[]{:S(2)}) collective-permute-start(bf16[256,2048]{1,0:T(8,128)(2,1)} %add_convert_fusion.8), channel_id=1, source_target_pairs={{0,16},{4,20},{8,24},{12,28},{16,0},{20,4},{24,8},{28,12},{1,17},{... | collective-permute-start | bytes 3145736 | tf_op jit(solution)/shard_map/ppermute | solution.py:308
  594.7 345.7 %reduce-scatter.9.cloned.1.call-start = ((), (), s32[]{:S(2)}) async-start(), calls=%async_computation.9 | async-start | bytes 3932160 | tf_op jit(solution)/shard_map/reduce_scatter | solution.py:817
  610.3 26.2 %collective-permute-start.9 = (bf16[256,2048]{1,0:T(8,128)(2,1)S(1)}, bf16[256,2048]{1,0:T(8,128)(2,1)S(1)}, u32[]{:S(2)}, u32[]{:S(2)}) collective-permute-start(bf16[256,2048]{1,0:T(8,128)(2,1)S(1)} %get-tuple-element.98), channel_id=1, source_target_pairs={{0,16},{4,20},{8,24},{12,28},{16,0},{20,4},{24,8},{28,12},{1,17},{... | collective-permute-start | bytes 3145736 | tf_op jit(solution)/shard_map/ppermute | solution.py:308
  622.8 31.9 %collective-permute-start.11 = (bf16[256,2048]{1,0:T(8,128)(2,1)S(1)}, bf16[256,2048]{1,0:T(8,128)(2,1)S(1)}, u32[]{:S(2)}, u32[]{:S(2)}) collective-permute-start(bf16[256,2048]{1,0:T(8,128)(2,1)S(1)} %get-tuple-element.97), channel_id=1, source_target_pairs={{0,16},{4,20},{8,24},{12,28},{16,0},{20,4},{24,8},{28,12},{1,17},{... | collective-permute-start | bytes 3145736 | tf_op jit(solution)/shard_map/ppermute | solution.py:308
  638.6 16.9 %collective-permute-start.10 = (bf16[256,2048]{1,0:T(8,128)(2,1)S(1)}, bf16[256,2048]{1,0:T(8,128)(2,1)S(1)}, u32[]{:S(2)}, u32[]{:S(2)}) collective-permute-start(bf16[256,2048]{1,0:T(8,128)(2,1)S(1)} %add_convert_fusion.6), channel_id=1, source_target_pairs={{0,8},{4,12},{8,0},{12,4},{16,24},{20,28},{24,16},{28,20},{1,9},{5... | collective-permute-start | bytes 3145736 | tf_op jit(solution)/shard_map/ppermute | solution.py:308
  752.4 116.3 %collective-permute-start.13 = (bf16[1024,2048]{0,1:T(8,128)(2,1)}, bf16[1024,2048]{0,1:T(8,128)(2,1)}, u32[]{:S(2)}, u32[]{:S(2)}) collective-permute-start(bf16[1024,2048]{0,1:T(8,128)(2,1)} %convolution_convert_fusion.6), channel_id=1, source_target_pairs={{0,4},{4,0},{8,12},{12,8},{16,20},{20,16},{24,28},{28,24},{1,5},{5... | collective-permute-start | bytes 12582920 | tf_op jit(solution)/shard_map/ppermute | solution.py:308
  872.1 14.9 %collective-permute-start.15 = (bf16[128,2048]{0,1:T(8,128)(2,1)}, bf16[128,2048]{0,1:T(8,128)(2,1)}, u32[]{:S(2)}, u32[]{:S(2)}) collective-permute-start(bf16[128,2048]{0,1:T(8,128)(2,1)} %get-tuple-element.105), channel_id=1, source_target_pairs={{0,8},{4,12},{8,0},{12,4},{16,24},{20,28},{24,16},{28,20},{1,9},{5... | collective-permute-start | bytes 1572872 | tf_op jit(solution)/shard_map/ppermute | solution.py:308
  875.2 195.2 %reduce-scatter.11.cloned.1.call-start = ((), (), s32[]{:S(2)}) async-start(), calls=%async_computation.10 | async-start | bytes 1310720 | tf_op jit(solution)/shard_map/reduce_scatter | solution.py:817
  875.3 26.2 %collective-permute-start.14 = (bf16[128,2048]{0,1:T(8,128)(2,1)}, bf16[128,2048]{0,1:T(8,128)(2,1)S(1)}, u32[]{:S(2)}, u32[]{:S(2)}) collective-permute-start(bf16[128,2048]{0,1:T(8,128)(2,1)} %get-tuple-element.104), channel_id=1, source_target_pairs={{0,8},{4,12},{8,0},{12,4},{16,24},{20,28},{24,16},{28,20},{1,9},{5... | collective-permute-start | bytes 1572872 | tf_op jit(solution)/shard_map/ppermute | solution.py:308
  906.5 15.1 %collective-permute-start.17 = (bf16[128,2048]{0,1:T(8,128)(2,1)}, bf16[128,2048]{0,1:T(8,128)(2,1)}, u32[]{:S(2)}, u32[]{:S(2)}) collective-permute-start(bf16[128,2048]{0,1:T(8,128)(2,1)} %get-tuple-element.103), channel_id=1, source_target_pairs={{0,16},{4,20},{8,24},{12,28},{16,0},{20,4},{24,8},{28,12},{1,17},{... | collective-permute-start | bytes 1572872 | tf_op jit(solution)/shard_map/ppermute | solution.py:308
  916.1 15.6 %collective-permute-start.19 = (bf16[128,2048]{0,1:T(8,128)(2,1)}, bf16[128,2048]{0,1:T(8,128)(2,1)S(1)}, u32[]{:S(2)}, u32[]{:S(2)}) collective-permute-start(bf16[128,2048]{0,1:T(8,128)(2,1)} %get-tuple-element.102), channel_id=1, source_target_pairs={{0,16},{4,20},{8,24},{12,28},{16,0},{20,4},{24,8},{28,12},{1,17},{... | collective-permute-start | bytes 1572872 | tf_op jit(solution)/shard_map/ppermute | solution.py:308
  (65 other events, 1976.8 us)
Sparse Core Ops, SparseCore 0:
  162.8 25.8 all-gather.3
  212.6 122.4 all-gather.5
  336.6 79.5 all-gather.7
  473.4 82.1 reduce-scatter.4
  594.8 82.0 reduce-scatter.6
  875.3 60.8 reduce-scatter.8
  940.5 25.1 reduce-scatter.10

commit v2 on v1

--- a/solution.py
+++ b/solution.py
@@ -321,10 +321,11 @@
         self.sems = (send_sem, recv_sem, local_sem)
         self.count = [0, 0]
         self.open = []
-
-    def far(self, source, target, d, z, sends=None, receives=None, lands=None):
-        number = self.count[0]
-        self.count[0] += 1
+        self.done = []
+
+    def far(self, source, target, d, z, sends=None, receives=None, lands=None, own=None):
+        number = self.count[0] if own is None else own
+        self.count[0] += own is None
 
         def copy(landing):
             return pltpu.make_async_remote_copy(
@@ -359,12 +360,16 @@
         else:
             when(sends, copy.wait)
 
+    def sent(self, move):
+        when(move[1], move[0][0].wait_send)
+        self.done.append(id(move))
+
     def finish(self):
         for move in self.open:
             if not move[3]:
                 self.landed(move)
-            if isinstance(move[0], tuple):
-                when(move[1], move[0][0].wait_send)
+            if isinstance(move[0], tuple) and id(move) not in self.done:
+                self.sent(move)
 
 
 def when(condition, do):
@@ -410,10 +415,11 @@
 
 def exchange_along_z(moves, number, source, target, base=None):
     z = lax.axis_index("seq")
+    own = None if base is None else base + number
     base = moves.count[0] - number if base is None else base
     to_d, to_z, itself = peer_of(number)
     away = jnp.logical_not(itself)
-    far = moves.far(source, target(z & 1), to_d, to_z, away, away, base + (z & 1))
+    far = moves.far(source, target(z & 1), to_d, to_z, away, away, base + (z & 1), own)
     near = moves.here(source, target(z & 1), itself)
     return far, near
 
@@ -423,7 +429,7 @@
         moves.landed(move)
 
 
-def intake_kernel(small_ref, mark_ref, qkv_ref, whole_ref, marks_ref, half_ref, *sems):
+def intake_kernel(small_ref, mark_ref, whole_ref, marks_ref, *sems):
     moves = Moves(*sems)
     d = lax.axis_index("dp")
     z = lax.axis_index("seq")
@@ -435,22 +441,21 @@
     moves.here(mark_ref, marks_ref.at[0])
     for mask in range(1, PLANE):
         moves.far(mark_ref, marks_ref.at[mask], d ^ mask, z)
-    spread_columns(moves, qkv_ref, half_ref)
     moves.finish()
 
 
 def spread_columns(moves, shard, half):
     d = lax.axis_index("dp")
     z = lax.axis_index("seq")
-    part, width = half.shape[0], shard.shape[1]
+    part, width = shard.shape[0] // PLANE, shard.shape[1]
     target = half.at[:, pl.ds(pl.multiple_of(d * width, 128), width)]
 
     def rows(mask):
         return shard.at[pl.ds(pl.multiple_of((d ^ mask) * part, 64), part)]
 
-    moves.here(rows(0), target)
-    for mask in FAR_FIRST:
-        moves.far(rows(mask), target, d ^ mask, z)
+    return [moves.here(rows(0), target)] + [
+        moves.far(rows(mask), target, d ^ mask, z) for mask in FAR_FIRST
+    ]
 
 
 def kernel_call(
@@ -487,22 +492,20 @@
     return jax.ShapeDtypeStruct(shape, BF16)
 
 
-def intake(small, mark, qkv_shard):
+def intake(small, mark):
     groups = lax.axis_size("seq")
-    units, width = qkv_shard.shape
     return kernel_call(
         intake_kernel,
-        [small, mark, qkv_shard],
+        [small, mark],
         [
             shaped(groups, *small.shape),
             jax.ShapeDtypeStruct((PLANE,) + mark.shape, mark.dtype),
-            shaped(units // PLANE, width * PLANE),
         ],
-        groups - 1 + 2 * (PLANE - 1),
-        3,
+        groups - 1 + PLANE - 1,
+        2,
         1,
         "intake",
-        20,
+        10,
     )
 
 
@@ -584,8 +587,8 @@
 
 
 def first_kernel(rows_ref, qkv_ref, up_ref, down_ref, *refs):
-    chips, others, heads, up_half, down_half = refs[:5]
-    moves = Moves(*refs[5:])
+    chips, others, heads, up_half, down_half, qkv_half = refs[:6]
+    moves = Moves(*refs[6:])
     d = lax.axis_index("dp")
     core = d & 1
     half = rows_ref.shape[1]
@@ -602,14 +605,16 @@
                     0, pl.ds(pl.multiple_of(at * half + piece * size, size), size)
                 ],
             )
+    spread = spread_columns(moves, qkv_ref, qkv_half)
     spread_columns(moves, up_ref, up_half)
     spread_columns(moves, down_ref, down_half)
+    all_landed(moves, spread)
 
     def place(at):
         own = (at >> 1) == core
         return jnp.where(own, (at & 1) * 2 + core, 4 + (at & 1))
 
-    qkv = gather_along_z(moves, qkv_ref, place, heads)
+    qkv = gather_along_z(moves, qkv_half, place, heads)
     next(qkv)
     rows = gather_rows(
         moves,
@@ -631,51 +636,73 @@
     moves.finish()
 
 
-def first_gather(rows, qkv_half, up_shard, down_shard):
+def first_gather(rows, qkv_shard, up_shard, down_shard, late):
     seqs, half, width = rows.shape
-    spread = [shaped(w.shape[0] // PLANE, w.shape[1] * PLANE) for w in (up_shard, down_shard)]
+    part = qkv_shard.shape[0] // PLANE
     return kernel_call(
         first_kernel,
-        [rows, qkv_half, up_shard, down_shard],
+        [rows, qkv_shard, up_shard, down_shard],
         [
             shaped(4, seqs * half, width),
             shaped(4, seqs * half, width),
-            shaped(6, *qkv_half.shape),
-            *spread,
+            shaped(6, part, width),
+            shaped(up_shard.shape[0] // PLANE, width),
+            shaped(down_shard.shape[0] // PLANE, width),
+            shaped(part, width),
         ],
-        7 * FIRST_PIECES + Z_COPIES + FIRST_PIECES + 2 + 2 * (PLANE - 1),
-        3 + FIRST_PIECES,
+        7 * FIRST_PIECES + Z_COPIES + FIRST_PIECES + 2 + 3 * (PLANE - 1),
+        4 + FIRST_PIECES,
         2,
         "first_gather",
         110,
-    )
-
-
-def gather_kernel(rows_ref, chips, others, *sems):
+        late=late,
+    )[:5]
+
+
+def gather_kernel(rows_ref, held_ref, chips, others, held_others, *sems):
     moves = Moves(*sems)
+    d = lax.axis_index("dp")
+    z = lax.axis_index("seq")
     meet_all((CORE, X_WAY, Y_WAY), lines=False)
-    for _ in gather_rows(moves, rows_ref, chips, others):
+    steps = gather_rows(moves, rows_ref, chips, others)
+    next(steps)
+    moves.far(held_ref, held_others, d ^ CORE, z)
+    for _ in steps:
         pass
     moves.finish()
 
 
-def plane_gather_now(rows, number, late):
+def plane_gather_now(rows, held, number, late):
     count, width = rows.shape
-    got = kernel_call(
+    chips, others, held_others = kernel_call(
         gather_kernel,
-        [rows],
-        [shaped(4, count, width)] * 2,
-        GATHER_COPIES,
+        [rows, held],
+        [shaped(4, count, width), shaped(4, count, width), shaped(*held.shape)],
+        GATHER_COPIES + 1,
         1,
         number,
         "plane_gather",
         76,
+        [pltpu.VMEM, pl.ANY],
         late=late,
     )
-    return [part.reshape(4 * count, width) for part in got]
-
-
-def scatter_rows(moves, natural, chips_ref, others_ref, out_ref, own, got, far, near, done):
+    return [part.reshape(4 * count, width) for part in (chips, others)], held_others
+
+
+def add_rows(target, start, sources, count, step=64):
+    @pl.loop(0, count // step)
+    def _(i):
+        total = None
+        for ref, offset in sources:
+            piece = ref[pl.ds(pl.multiple_of(offset + i * step, step), step), :].astype(F32)
+            total = piece if total is None else total + piece
+        target[pl.ds(pl.multiple_of(start + i * step, step), step), :] = total.astype(target.dtype)
+
+
+CHIP_ORDER = (3, 1, 2, 0)
+
+
+def scatter_rows(moves, fill, last, own, got, far, near, done):
     d = lax.axis_index("dp")
     z = lax.axis_index("seq")
     half = own.shape[1] // 2
@@ -684,115 +711,459 @@
     def send_to(source, target, mask):
         return moves.far(source, target, d ^ mask, z)
 
-    order = (3, 1, 2, 0)
-    from_core = [send_to(others_ref.at[c], got.at[i], CORE) for i, c in enumerate(order)]
-    reads = [moves.here(chips_ref.at[c], own.at[i]) for i, c in enumerate(order)]
-    step = 64
-
-    def add(target, start, sources):
-        @pl.loop(0, half // step)
-        def _(i):
-            total = None
-            for ref, offset in sources:
-                piece = ref[pl.ds(pl.multiple_of(offset + i * step, step), step), :].astype(F32)
-                total = piece if total is None else total + piece
-            target[pl.ds(pl.multiple_of(start + i * step, step), step), :] = total.astype(
-                target.dtype
-            )
-
-    def ready(i):
-        moves.landed(from_core[i])
-        moves.landed(reads[i])
-
+    ready = fill(send_to)
     yield
     ready(0)
-    add(own.at[0], 0, [(own.at[0], 0), (got.at[0], 0)])
+    add_rows(own.at[0], 0, [(own.at[0], 0), (got.at[0], 0)], half)
     to_x = send_to(own.at[0, first], far.at[0], X_WAY)
-    add(own.at[0], half, [(own.at[0], half), (got.at[0], half)])
+    add_rows(own.at[0], half, [(own.at[0], half), (got.at[0], half)], half)
     to_y = send_to(own.at[0, second], far.at[1], Y_WAY)
     ready(1)
-    add(own.at[1], 0, [(own.at[1], 0), (got.at[1], 0)])
+    add_rows(own.at[1], 0, [(own.at[1], 0), (got.at[1], 0)], half)
     x_first = send_to(own.at[1, first], near.at[0, first], X_WAY)
     ready(2)
-    add(own.at[2], half, [(own.at[2], half), (got.at[2], half)])
+    yield
+    moves.landed(to_x)
+    add_rows(own.at[2], 0, [(own.at[2], 0), (got.at[2], 0), (far.at[0], 0)], half)
+    y_first = send_to(own.at[2, first], near.at[1, first], Y_WAY)
+    add_rows(own.at[2], half, [(own.at[2], half), (got.at[2], half)], half)
     y_second = send_to(own.at[2, second], near.at[1, second], Y_WAY)
-    yield
     moves.landed(to_y)
-    add(own.at[1], half, [(own.at[1], half), (got.at[1], half), (far.at[1], 0)])
+    add_rows(own.at[1], half, [(own.at[1], half), (got.at[1], half), (far.at[1], 0)], half)
     x_second = send_to(own.at[1, second], near.at[0, second], X_WAY)
-    moves.landed(to_x)
-    add(own.at[2], 0, [(own.at[2], 0), (got.at[2], 0), (far.at[0], 0)])
-    y_first = send_to(own.at[2, first], near.at[1, first], Y_WAY)
     ready(3)
     yield
-    moves.landed(x_first)
-    moves.landed(y_second)
-    for number, arrivals in ((0, (y_first,)), (1, (x_second,))):
+    for number, arrivals in ((0, (x_first, y_first)), (1, (x_second, y_second))):
         all_landed(moves, arrivals)
         start = number * half
-        add(done, start, [(own.at[3], start), (got.at[3], start), (near.at[0], start), (near.at[1], start)])
-        if natural:
+        add_rows(
+            done,
+            start,
+            [(own.at[3], start), (got.at[3], start), (near.at[0], start), (near.at[1], start)],
+            half,
+        )
+        last(number)
+    for move in (to_x, to_y, x_first, x_second, y_first, y_second):
+        moves.sent(move)
+
+
+SCATTER_COPIES = 10
+
+
+def sum_rows(target, sources, step=64):
+    @pl.loop(0, target.shape[0] // step)
+    def _(i):
+        at = pl.ds(pl.multiple_of(i * step, step), step)
+        total = sources[0][at, :].astype(F32)
+        for ref in sources[1:]:
+            total = total + ref[at, :].astype(F32)
+        target[at, :] = total.astype(target.dtype)
+
+
+def sum_along_line(moves, piece, got, target):
+    d = lax.axis_index("dp")
+    z = lax.axis_index("seq")
+    groups = lax.axis_size("seq")
+    arrivals = []
+    for step in range(1, groups):
+        to = (z + step) % groups
+        arrivals.append(moves.far(piece(to), got.at[step - 1], d, to))
+    yield
+    all_landed(moves, arrivals)
+    sum_rows(target, [piece(z)] + [got.at[step] for step in range(groups - 1)])
+
+
+class Slots:
+    def __init__(self, places, sems):
+        self.places = places
+        self.sems = sems
+        self.copies = {}
+
+    def load(self, slot, source):
+        self.copies[slot] = pltpu.make_async_copy(source, self.places.at[slot], self.sems.at[slot])
+        self.copies[slot].start()
+
+    def store(self, slot, target):
+        self.copies[slot] = pltpu.make_async_copy(self.places.at[slot], target, self.sems.at[slot])
+        self.copies[slot].start()
+
+    def wait(self, slot):
+        if slot in self.copies:
+            self.copies.pop(slot).wait()
+        return self.places.at[slot]
+
+
+def scatter_products(
+    moves, sources, held, rows_in, weights_in, stage, side, last, follow=None, also=None
+):
+    count = held[0].shape[1]
+    blocks = [(1, c) for c in CHIP_ORDER] + [(0, c) for c in CHIP_ORDER]
+
+    def fill(send_to):
+        def load(number):
+            which, c = blocks[number]
+            rows_in.load(number % 2, sources[which].at[pl.ds(c * count, count)])
+
+        load(0)
+        matrix = weights_in.wait(side)
+        from_core = []
+        for number, (which, c) in enumerate(blocks):
+            if number + 1 < len(blocks):
+                load(number + 1)
+            if which == 1 and number >= 2:
+                moves.sent(from_core[number - 2])
+            place = stage.at[number % 2] if which == 1 else held[0].at[number - 4]
+            block = rows_in.wait(number % 2)
+
+            @pl.loop(0, count // 256)
+            def _(i):
+                at = pl.ds(pl.multiple_of(i * 256, 256), 256)
+                place[at, :] = jnp.dot(
+                    block[at, :], matrix[...], preferred_element_type=F32
+                ).astype(BF16)
+                if also is not None:
+                    also(which, c, block, i)
+
+            if which == 1:
+                from_core.append(send_to(place, held[1].at[number], CORE))
+        if follow is not None:
+            follow()
+        moves.sent(from_core[2])
+        moves.sent(from_core[3])
+        return lambda i: moves.landed(from_core[i])
+
+    return scatter_rows(moves, fill, last, *held)
+
+
+def last_kernel(
+    chips_ref,
+    others_ref,
+    weights_ref,
+    out_ref,
+    held_ref,
+    grad_ref,
+    out_sum_ref,
+    shard_ref,
+    own,
+    got,
+    far,
+    near,
+    done,
+    stage,
+    rows_held,
+    weights_held,
+    out_got,
+    out_sum,
+    rows_sem,
+    weights_sem,
+    *sems,
+):
+    moves = Moves(*sems)
+    rows_in = Slots(rows_held, rows_sem)
+    weights_in = Slots(weights_held, weights_sem)
+    columns = out_sum.shape[1]
+    half, width = own.shape[2] // 2, own.shape[3]
+    for side in range(2):
+        weights_in.load(side, weights_ref.at[:, pl.ds(side * width, width)])
+    meet_all(range(1, PLANE), peers=True)
+    out = sum_along_line(
+        moves,
+        lambda at: out_ref.at[:, pl.ds(pl.multiple_of(at * columns, 128), columns)],
+        out_got,
+        out_sum,
+    )
+    next(out)
+
+    def scatter(side):
+        base = []
+
+        def last(number):
+            if number == 0:
+                base.append(moves.count[0])
+                moves.count[0] += 2
             exchange_along_z(
                 moves,
                 number,
-                done.at[pl.ds(start, half)],
-                lambda at: out_ref.at[at],
+                done.at[side, pl.ds(number * half, half)],
+                lambda at: grad_ref.at[at, :, pl.ds(side * width, width)],
+                base[0],
             )
-    if not natural:
-        moves.here(done, out_ref)
-
-
-SCATTER_COPIES = 10
-
-
-def scatter_kernel(natural, united, *refs):
-    count = len(natural)
-    ins, refs = refs[: 2 * count], refs[2 * count :]
-    held, refs = refs[:united], refs[united:]
-    outs, refs = refs[:count], refs[count:]
-    shard, refs = refs[:united], refs[united:]
-    buffers = refs[: 5 * count]
-    moves = Moves(*refs[5 * count :])
-    meet_all(range(1, PLANE) if united else (CORE, X_WAY, Y_WAY), lines=False, peers=any(natural))
-    if united:
-        unite_columns(moves, held[0], shard[0])
-    steps = [
-        scatter_rows(
-            moves, natural[i], *ins[2 * i : 2 * i + 2], outs[i], *buffers[5 * i : 5 * i + 5]
+
+        held = [ref.at[side] for ref in (own, got, far, near, done)]
+        return scatter_products(
+            moves, (chips_ref, others_ref), held, rows_in, weights_in, stage, side, last
         )
-        for i in range(count)
-    ]
-    for _ in range(4):
-        for step in steps:
-            next(step, None)
+
+    low, high = scatter(0), scatter(1)
+    next(low)
+    next(low)
+    next(high)
+    next(low)
+    next(high)
+    next(out, None)
+    moves.here(out_sum, out_sum_ref)
+    next(low, None)
+    next(high)
+    unite_columns(moves, held_ref, shard_ref)
+    next(high, None)
     moves.finish()
 
 
-def plane_scatter_now(parts, shapes, natural, number, late=(), united=()):
-    inputs = []
-    scratch = []
-    for pair in parts:
-        total, width = pair[0].shape
-        count = total // 4
-        inputs += [part.reshape(4, count, width) for part in pair]
-        for lead, rows in ((4, count), (4, count), (2, count // 2), (2, count)):
-            scratch.append(pltpu.VMEM((lead, rows, width), BF16))
-        scratch.append(pltpu.VMEM((count, width), BF16))
-    count = len(united)
+def last_scatter(parts, weights, out_grad, held, shape):
+    total, units = parts[0].shape
+    width = weights.shape[1]
+    count, half = total // 4, width // 2
+    groups = lax.axis_size("seq")
+    rows, columns = out_grad.shape[0], width // groups
+    sizes = ((4, count, half), (4, count, half), (2, count // 2, half), (2, count, half))
     return kernel_call(
-        lambda *refs: scatter_kernel(natural, count, *refs),
-        inputs + list(united),
-        [shaped(*shape) for shape in shapes]
-        + [shaped(s.shape[0] * PLANE, s.shape[1] // PLANE) for s in united],
-        SCATTER_COPIES * len(parts) + 2 + count * (PLANE - 1),
-        7 * len(parts) + count,
-        number,
-        "plane_scatter",
-        100 if any(natural) else 76,
-        [pl.ANY] * len(inputs) + [pltpu.VMEM] * count,
-        scratch,
-        late,
-    )
+        last_kernel,
+        [*parts, weights, out_grad, held],
+        [
+            shaped(*shape),
+            shaped(rows, columns),
+            shaped(held.shape[0] * PLANE, width // PLANE),
+        ],
+        2 * SCATTER_COPIES + 4 + groups - 1 + PLANE - 1,
+        6,
+        7,
+        "last_scatter",
+        100,
+        [pl.ANY, pl.ANY, pl.ANY, pltpu.VMEM, pltpu.VMEM],
+        [pltpu.VMEM((2,) + size, BF16) for size in sizes + ((count, half),)]
+        + [
+            pltpu.VMEM((2, count, half), BF16),
+            pltpu.VMEM((2, count, units), BF16),
+            pltpu.VMEM((2, units, half), BF16),
+            pltpu.VMEM((groups - 1, rows, columns), BF16),
+            pltpu.VMEM((rows, columns), BF16),
+            pltpu.SemaphoreType.DMA((2,)),
+            pltpu.SemaphoreType.DMA((2,)),
+        ],
+    )
+
+
+def feed_kernel(
+    grad_chips,
+    grad_others,
+    act_chips,
+    act_others,
+    up_ref,
+    down_ref,
+    rows_chips,
+    rows_others,
+    cot_chips,
+    cot_others,
+    norm_ref,
+    out_ref,
+    up_parts_ref,
+    down_grad_ref,
+    left,
+    rows_held,
+    weights_held,
+    own,
+    got,
+    far,
+    near,
+    done,
+    stage,
+    stream_held,
+    result_held,
+    rows_sem,
+    weights_sem,
+    stream_sem,
+    result_sem,
+    free_sem,
+    send_sem,
+    recv_sem,
+    local_sem,
+):
+    moves = Moves(send_sem, recv_sem, local_sem)
+    d = lax.axis_index("dp")
+    z = lax.axis_index("seq")
+    rows_in = Slots(rows_held, rows_sem)
+    weights_in = Slots(weights_held, weights_sem)
+    stream = Slots(stream_held, stream_sem)
+    results = Slots(result_held, result_sem)
+    count, width = own.shape[2], own.shape[3]
+    columns = stream_held.shape[2]
+    def load_weights(weights, side):
+        weights_in.load(side, weights.at[:, pl.ds(side * width, width)])
+
+    def scatter(sources, side, target, follow, keep):
+        held = [ref.at[side] for ref in (own, got, far, near, done)]
+
+        def transposed(which, c, block, i):
+            tokens = pl.ds(pl.multiple_of(c * count + i * 256, 256), 256)
+            for unit in range(0, block.shape[1], 256):
+                left[which, unit : unit + 256, tokens] = jnp.transpose(
+                    block[pl.ds(pl.multiple_of(i * 256, 256), 256), unit : unit + 256]
+                )
+
+        def last(number):
+            if number == 1:
+                moves.here(held[4], target.at[:, pl.ds(side * width, width)])
+
+        return scatter_products(
+            moves,
+            sources,
+            held,
+            rows_in,
+            weights_in,
+            stage,
+            side,
+            last,
+            follow,
+            transposed if keep else None,
+        )
+
+    def end(work, side):
+        next(work, None)
+        all_landed(moves, moves.open[-1:])
+        for mask in (CORE, X_WAY, Y_WAY):
+            pl.semaphore_signal(free_sem.at[side], inc=1, **at_plane(d ^ mask, z))
+
+    def weight_grad(rights, place):
+        chunks = rights[0].shape[1] // columns
+        gone = {}
+
+        def load(chunk):
+            for side in range(2):
+                stream.load(
+                    2 * (chunk % 2) + side, rights[side].at[:, pl.ds(chunk * columns, columns)]
+                )
+
+        load(0)
+        for chunk in range(chunks):
+            if chunk + 1 < chunks:
+                load(chunk + 1)
+            first, second = (stream.wait(2 * (chunk % 2) + side) for side in range(2))
+            result = results.wait(chunk % 2)
+            for move in gone.pop(chunk % 2, ()):
+                moves.sent(move)
+
+            @pl.loop(0, result.shape[0] // 256)
+            def _(i):
+                at = pl.ds(pl.multiple_of(i * 256, 256), 256)
+                total = jnp.dot(left[0, at, :], first[...], preferred_element_type=F32)
+                total += jnp.dot(left[1, at, :], second[...], preferred_element_type=F32)
+                result[at, :] = total.astype(BF16)
+
+            gone[chunk % 2] = place(result, chunk)
+            yield
+        for copies in gone.values():
+            for move in copies:
+                moves.sent(move)
+
+    groups = lax.axis_size("seq")
+    part = up_parts_ref.shape[1]
+
+    def to_line(result, chunk):
+        target = up_parts_ref.at[:, :, pl.ds(chunk * columns, columns)]
+        copies = []
+        for step in range(1, groups):
+            to = (z + step) % groups
+            piece = result.at[pl.ds(pl.multiple_of(to * part, 256), part)]
+            copies.append(moves.far(piece, target.at[step], d, to))
+        piece = result.at[pl.ds(pl.multiple_of(z * part, 256), part)]
+        results.copies[chunk % 2] = pltpu.make_async_copy(
+            piece, target.at[0], results.sems.at[chunk % 2]
+        )
+        results.copies[chunk % 2].start()
+        return copies
+
+    def to_memory(result, chunk):
+        results.store(chunk % 2, down_grad_ref.at[:, pl.ds(chunk * columns, columns)])
+        return ()
+
+    def steps(work, number):
+        for _ in range(number):
+            next(work, None)
+
+    nothing = lambda: None
+    load_weights(up_ref, 0)
+    load_weights(up_ref, 1)
+    meet_all((CORE, X_WAY, Y_WAY))
+    grads = (grad_chips, grad_others)
+    acts = (act_chips, act_others)
+    norm_low = scatter(grads, 0, norm_ref, lambda: load_weights(down_ref, 0), True)
+    norm_high = scatter(grads, 1, norm_ref, lambda: load_weights(down_ref, 1), False)
+    out_low = scatter(acts, 0, out_ref, nothing, False)
+    out_high = scatter(acts, 1, out_ref, nothing, True)
+    up_work = weight_grad((rows_chips, rows_others), to_line)
+    down_work = weight_grad((cot_chips, cot_others), to_memory)
+    next(norm_low)
+    next(norm_low)
+    steps(up_work, 3)
+    next(norm_low)
+    next(norm_high)
+    next(norm_high)
+    steps(up_work, 3)
+    end(norm_low, 0)
+    next(norm_high)
+    pl.semaphore_wait(free_sem.at[0], 3)
+    next(out_low)
+    next(out_low)
+    steps(up_work, 3)
+    end(norm_high, 1)
+    next(out_low)
+    pl.semaphore_wait(free_sem.at[1], 3)
+    next(out_high)
+    next(out_high)
+    steps(down_work, 4)
+    next(out_low, None)
+    next(out_high)
+    steps(down_work, 5)
+    next(out_high, None)
+    for slot in range(2):
+        results.wait(slot)
+    moves.finish()
+
+
+def feed_back(grads, acts, up_full, down_full, rows, cots):
+    total, units = grads[0].shape
+    width = up_full.shape[1]
+    count = total // 4
+    half = width // 2
+    columns = 256
+    copies = 4 * SCATTER_COPIES + 3 * width // columns
+    groups = lax.axis_size("seq")
+    ins = [*grads, *acts, up_full, down_full, *rows, *cots]
+    return pl.pallas_call(
+        feed_kernel,
+        out_shape=[shaped(count, width)] * 2
+        + [shaped(groups, units // groups, width), shaped(units, width)],
+        in_specs=[pl.BlockSpec(memory_space=pl.ANY)] * len(ins),
+        out_specs=[pl.BlockSpec(memory_space=pl.ANY)] * 4,
+        scratch_shapes=[
+            pltpu.VMEM((2, units, total), BF16),
+            pltpu.VMEM((2, count, units), BF16),
+            pltpu.VMEM((2, units, half), BF16),
+            pltpu.VMEM((2, 4, count, half), BF16),
+            pltpu.VMEM((2, 4, count, half), BF16),
+            pltpu.VMEM((2, 2, count // 2, half), BF16),
+            pltpu.VMEM((2, 2, count, half), BF16),
+            pltpu.VMEM((2, count, half), BF16),
+            pltpu.VMEM((2, count, half), BF16),
+            pltpu.VMEM((4, total, columns), BF16),
+            pltpu.VMEM((2, units, columns), BF16),
+            pltpu.SemaphoreType.DMA((2,)),
+            pltpu.SemaphoreType.DMA((2,)),
+            pltpu.SemaphoreType.DMA((4,)),
+            pltpu.SemaphoreType.DMA((2,)),
+            pltpu.SemaphoreType.REGULAR((2,)),
+            pltpu.SemaphoreType.DMA((copies,)),
+            pltpu.SemaphoreType.DMA((copies,)),
+            pltpu.SemaphoreType.DMA((4,)),
+        ],
+        compiler_params=pltpu.CompilerParams(
+            collective_id=6, has_side_effects=True, vmem_limit_bytes=62 * 1024 * 1024
+        ),
+        cost_estimate=pl.CostEstimate(
+            flops=8 * 2 * total * units * width, bytes_accessed=160 * 3 * 1024 * 1024, transcendentals=0
+        ),
+        name="feed_back",
+    )(*ins)
 
 
 def unite_columns(moves, half_ref, shard_ref):
@@ -827,33 +1198,51 @@
     return whole.reshape(-1, grad.shape[-1])
 
 
-def plane_gather(rows, second, third):
+def chips_gather(rows, second):
     half = rows.shape[0] // 2
     x_rows = swap(rows, X_WAY)
     y_rows = swap(rows, Y_WAY)
     corner_first = swap(after(y_rows[:half], second), X_WAY)
     corner_second = swap(after(x_rows[half:], second), Y_WAY)
-    chips = jnp.concatenate([rows, x_rows, y_rows, after(corner_first, third), corner_second])
-    return chips, swap(chips, CORE)
-
-
-def plane_scatter(chips, others):
-    count = chips.shape[0] // 4
-    half = count // 2
-    got = swap(others, CORE)
-
-    def both(start, size):
-        return chips[start : start + size].astype(F32) + got[start : start + size].astype(F32)
-
-    far_first = swap(both(3 * count, half).astype(BF16), X_WAY)
-    far_second = swap(both(3 * count + half, half).astype(BF16), Y_WAY)
-    x_first = swap(both(count, half).astype(BF16), X_WAY)
-    y_second = swap(both(2 * count + half, half).astype(BF16), Y_WAY)
-    x_second = swap((both(count + half, half) + far_second.astype(F32)).astype(BF16), X_WAY)
-    y_first = swap((both(2 * count, half) + far_first.astype(F32)).astype(BF16), Y_WAY)
-    first = both(0, half) + x_first.astype(F32) + y_first.astype(F32)
-    second = both(half, half) + x_second.astype(F32) + y_second.astype(F32)
-    return jnp.concatenate([first, second])
+    return jnp.concatenate([rows, x_rows, y_rows, corner_first, corner_second])
+
+
+class Scatter:
+    def __init__(self, chips, others):
+        self.chips = chips
+        self.got = swap(others, CORE)
+        self.count = chips.shape[0] // 4
+
+    def both(self, start, size):
+        return sum(part[start : start + size].astype(F32) for part in (self.chips, self.got))
+
+    def corners(self, tied):
+        half = self.count // 2
+        self.got, tied = lax.optimization_barrier((self.got, tied))
+        at = 3 * self.count
+        self.far = (
+            swap(self.both(at, half).astype(BF16), X_WAY),
+            swap(self.both(at + half, half).astype(BF16), Y_WAY),
+        )
+        self.near = (
+            swap(self.both(self.count, half).astype(BF16), X_WAY),
+            swap(self.both(2 * self.count + half, half).astype(BF16), Y_WAY),
+        )
+        return tied
+
+    def sides(self, tied):
+        half = self.count // 2
+        self.far, tied = lax.optimization_barrier((self.far, tied))
+        x_second = self.both(self.count + half, half) + self.far[1].astype(F32)
+        y_first = self.both(2 * self.count, half) + self.far[0].astype(F32)
+        self.last = swap(x_second.astype(BF16), X_WAY), swap(y_first.astype(BF16), Y_WAY)
+        return tied
+
+    def result(self):
+        half = self.count // 2
+        first = self.both(0, half) + self.near[0].astype(F32) + self.last[1].astype(F32)
+        second = self.both(half, half) + self.last[0].astype(F32) + self.near[1].astype(F32)
+        return jnp.concatenate([first, second])
 
 
 def place_of(mask):
@@ -936,14 +1325,19 @@
     out, chips, others = kernel_call(
         contexts_home_kernel,
         [*context, out_rows],
-        [shaped(2, rows // 2, width), shaped(4, count, width), shaped(4, count, width)],
+        [
+            shaped(2, rows // 2, width),
+            shaped(4, count, width),
+            shaped(4, count, width),
+        ],
         2 * PLANE * heads + GATHER_COPIES,
         4 * heads + 1,
         3,
         "contexts_home",
         60,
     )
-    return out.reshape(rows, width), chips.reshape(-1, width), others.reshape(-1, width)
+    chips, others = (part.reshape(-1, width) for part in (chips, others))
+    return out.reshape(rows, width), chips, others
 
 
 def gradients_out_kernel(count, in_ref, *refs):
@@ -991,7 +1385,7 @@
     moves.finish()
 
 
-def gradients_out(grad, sums):
+def gradients_out(grad, sums, late):
     rows, width = grad.shape
     heads = HEADS // PLANE
     count = len(sums)
@@ -1005,6 +1399,7 @@
         4,
         "gradients_out",
         50,
+        late=late,
     )
 
 
@@ -1166,61 +1561,63 @@
     )(flags, *qkv, grads, *lse)
 
 
-def sum_everywhere(sums, late):
-    dp = lax.axis_size("dp")
-    seq = lax.axis_size("seq")
-    count = dp * seq
+def sum_everywhere_kernel(number, in_ref, *refs):
+    held, out_ref, shards = refs[:number], refs[number], refs[number + 1 : 2 * number + 1]
+    got = refs[2 * number + 1]
+    moves = Moves(*refs[2 * number + 2 :])
+    d = lax.axis_index("dp")
+    z = lax.axis_index("seq")
+    groups = lax.axis_size("seq")
+    count = in_ref.shape[0]
+    me = d * groups + z
+    barrier = pltpu.get_barrier_semaphore()
+    for step in range(1, count):
+        to = (me + step) % count
+        pl.semaphore_signal(barrier, inc=1, **at_plane(to // groups, to % groups))
+    pl.semaphore_wait(barrier, count - 1)
+    arrivals = []
+    for step in range(1, count):
+        to = (me + step) % count
+        arrivals.append(moves.far(in_ref.at[to], got.at[step - 1], to // groups, to % groups))
+    for held_ref, shard_ref in zip(held, shards):
+        unite_columns(moves, held_ref, shard_ref)
+    total = in_ref[me]
+    for step, arrival in enumerate(arrivals):
+        moves.landed(arrival)
+        total = total + got[step]
+    out_ref[...] = total
+    moves.finish()
+
+
+def sum_everywhere(sums, held):
+    count = lax.axis_size("dp") * lax.axis_size("seq")
     kinds, width = sums.shape
     piece = width // count
     lanes = 128
     pieces = jnp.transpose(sums.reshape(kinds, count, piece), (1, 0, 2))
     pieces = pieces.reshape(count, kinds * piece // lanes, lanes)
-
-    def kernel(in_ref, late_ref, out_ref, got, send_sem, got_sem):
-        d = lax.axis_index("dp")
-        z = lax.axis_index("seq")
-        me = d * seq + z
-        mesh_id = pl.DeviceIdType.MESH
-        barrier = pltpu.get_barrier_semaphore()
-        for far in range(1, count):
-            to = (me + far) % count
-            pl.semaphore_signal(
-                barrier, inc=1, device_id=(to // seq, to % seq), device_id_type=mesh_id
-            )
-        pl.semaphore_wait(barrier, count - 1)
-        copies = []
-        for far in range(1, count):
-            to = (me + far) % count
-            copy = pltpu.make_async_remote_copy(
-                src_ref=in_ref.at[to],
-                dst_ref=got.at[far],
-                send_sem=send_sem.at[far],
-                recv_sem=got_sem.at[far],
-                device_id=(to // seq, to % seq),
-                device_id_type=mesh_id,
-            )
-            copy.start()
-            copies.append(copy)
-        total = in_ref[me]
-        for far in range(1, count):
-            copies[far - 1].wait()
-            total = total + got[far]
-        out_ref[...] = total
-
-    summed = pl.pallas_call(
-        kernel,
-        out_shape=jax.ShapeDtypeStruct(pieces.shape[1:], F32),
-        in_specs=[pl.BlockSpec(memory_space=pltpu.VMEM), pl.BlockSpec(memory_space=pl.ANY)],
-        out_specs=pl.BlockSpec(memory_space=pltpu.VMEM),
+    number = len(held)
+    far = count - 1 + number * (PLANE - 1)
+    summed, *shards = pl.pallas_call(
+        lambda *refs: sum_everywhere_kernel(number, *refs),
+        out_shape=[jax.ShapeDtypeStruct(pieces.shape[1:], F32)]
+        + [shaped(h.shape[0] * PLANE, h.shape[1] // PLANE) for h in held],
+        in_specs=[pl.BlockSpec(memory_space=pltpu.VMEM)] * (1 + number),
+        out_specs=[pl.BlockSpec(memory_space=pltpu.VMEM)]
+        + [pl.BlockSpec(memory_space=pl.ANY)] * number,
         scratch_shapes=[
-            pltpu.VMEM(pieces.shape, F32),
-            pltpu.SemaphoreType.DMA((count,)),
-            pltpu.SemaphoreType.DMA((count,)),
+            pltpu.VMEM((count - 1,) + pieces.shape[1:], F32),
+            pltpu.SemaphoreType.DMA((far,)),
+            pltpu.SemaphoreType.DMA((far,)),
+            pltpu.SemaphoreType.DMA((number,)),
         ],
         compiler_params=pltpu.CompilerParams(collective_id=0, has_side_effects=True),
+        cost_estimate=pl.CostEstimate(
+            flops=0, bytes_accessed=40 * 1024 * 1024, transcendentals=0
+        ),
         name="sum_everywhere",
-    )(pieces, late)
-    return summed.reshape(kinds, piece)
+    )(pieces, *held)
+    return summed.reshape(kinds, piece), shards
 
 
 def grouped_shards(
@@ -1250,7 +1647,7 @@
     )
     mark = jnp.broadcast_to(view_mask[:, None, None], (seq_count, 4, 128)).reshape(8, 128)
     out_columns = along_z(jnp.transpose(w_out))
-    small, marks, qkv_half = intake(small, mark, jnp.transpose(w_qkv))
+    small, marks = intake(small, mark)
     small = jnp.swapaxes(small, 0, 1).reshape(2 * TYPES, width).astype(F32)
     table = small[:TYPES]
     gain_one, bias_one, gain_two, bias_two = (small[TYPES + i] for i in range(4))
@@ -1269,9 +1666,10 @@
     norm_one, pull_one = jax.vjp(layer_norm, start_hidden, gain_one, bias_one)
     chips, others, qkv_full, up_half, down_half = first_gather(
         norm_one.astype(BF16).reshape(tokens.shape),
-        qkv_half,
+        jnp.transpose(w_qkv),
         jnp.transpose(w_up),
         w_down,
+        [out_columns],
     )
     up_full = along_z(up_half)
     down_full = along_z(down_half)
@@ -1284,43 +1682,36 @@
         for part in normed
     ]
     context, lse = attend(qkv, flags, heads)
-    context_rows, out_chips, out_others = contexts_home(
-        context, jnp.transpose(out_columns)
-    )
-    cots = plane_gather(after(cot, chips), context, context_rows)
+    context_rows, out_chips, out_others = contexts_home(context, jnp.transpose(out_columns))
+    cot_chips = chips_gather(after(cot, chips), context)
     mid_hidden = (
         start_hidden
         + jnp.dot(context_rows[:, : width // 2], out_chips, preferred_element_type=F32)
         + jnp.dot(context_rows[:, width // 2 :], out_others, preferred_element_type=F32)
     )
     norm_two, pull_two = jax.vjp(layer_norm, mid_hidden, gain_two, bias_two)
-    ffn_input = plane_gather_now(norm_two.astype(BF16), 5, cots)
+    ffn_input, cot_others = plane_gather_now(
+        norm_two.astype(BF16), cot_chips, 5, []
+    )
+    cots = (cot_chips, cot_others)
     def weight_grad(left, right):
         return sum(
             jnp.einsum("ti,td->id", a, b, preferred_element_type=F32)
             for a, b in zip(left, right)
         ).astype(BF16)
 
-    def times(parts, weight):
-        return [jnp.dot(part, weight, preferred_element_type=F32).astype(BF16) for part in parts]
-
-    ups = [
-        jnp.einsum("td,id->ti", part, up_full, preferred_element_type=F32) for part in ffn_input
-    ]
-    acts = [gelu_tanh(up_value).astype(BF16) for up_value in ups]
-    ffn_out = plane_scatter(*times(acts, down_full))
+    acts = []
     grad_ups = []
-    for cot_part, up_value in zip(cots, ups):
+    for cot_part, input_part in zip(cots, ffn_input):
         grad_act = jnp.einsum("td,id->ti", cot_part, down_full, preferred_element_type=F32)
-        grad_ups.append(jax.vjp(gelu_tanh, up_value)[1](grad_act)[0].astype(BF16))
-    down_grad = weight_grad(acts, cots)
-    up_grad = weight_grad(grad_ups, ffn_input)
-    down_sum = sum_along_z(down_grad)
-    up_sum = sum_along_z(up_grad)
-    grad_parts = times(grad_ups, up_full)
-    (grad_normed_two,) = plane_scatter_now(
-        [grad_parts], [(rows, width)], [False], 6, [down_sum, up_grad, ffn_out]
-    )
+        up_value = jnp.einsum("td,id->ti", input_part, up_full, preferred_element_type=F32)
+        activated, gelu_pull = jax.vjp(gelu_tanh, up_value)
+        acts.append(activated.astype(BF16))
+        grad_ups.append(gelu_pull(grad_act)[0].astype(BF16))
+    grad_normed_two, ffn_out, up_parts, down_grad = feed_back(
+        grad_ups, acts, up_full, down_full, ffn_input, cots
+    )
+    up_sum = jnp.sum(up_parts.astype(F32), axis=0).astype(BF16)
     grad_normed_two = grad_normed_two.astype(F32)
     grad_mid_norm, grad_gain_two, grad_bias_two = pull_two(grad_normed_two)
     grad_mid = cot.astype(F32) + grad_mid_norm
@@ -1332,25 +1723,25 @@
         ],
         axis=1,
     )
-    output = (mid_hidden + ffn_out).astype(BF16).reshape(tokens.shape)
-    grad_by_heads, up_shard, down_shard = gradients_out(grad_context, [up_sum, down_sum])
-    grad_qkv = attend_back(qkv, grad_by_heads, lse, flags, heads)
-    grad_qkv = [part.reshape(SEQS * rows, 3 * heads * HEAD_DIM) for part in grad_qkv]
+    output = (mid_hidden + ffn_out.astype(F32)).astype(BF16).reshape(tokens.shape)
     grad_out_weight = [
         jnp.einsum("td,te->de", part, grad_mid_low, preferred_element_type=F32).astype(BF16)
         for part in jnp.split(context_rows, 2, axis=1)
     ]
+    out_scatter = Scatter(*grad_out_weight)
+    grad_by_heads, up_shard = gradients_out(grad_context, [up_sum], [])
+    grad_by_heads, down_grad = lax.optimization_barrier((grad_by_heads, down_grad))
+    down_sum = sum_along_z(down_grad)
+    grad_by_heads = out_scatter.corners(grad_by_heads)
+    grad_qkv = attend_back(qkv, grad_by_heads, lse, flags, heads)
+    grad_qkv = [part.reshape(SEQS * rows, 3 * heads * HEAD_DIM) for part in grad_qkv]
+    grad_qkv = out_scatter.sides(grad_qkv)
     qkv_grad = shared_heads(weight_grad(grad_qkv, normed))
     qkv_sum = sum_along_z(qkv_grad)
-    out_sum = plane_scatter(*grad_out_weight).astype(BF16)
-    grad_normed_one, qkv_shard = plane_scatter_now(
-        [times(grad_qkv, qkv_full)], [tokens.shape], [True], 7, [out_sum], [qkv_sum]
+    grad_normed_one, out_sum, sum_down = last_scatter(
+        grad_qkv, qkv_full, out_scatter.result().astype(BF16), down_sum, tokens.shape
     )
     grad_normed_one = grad_normed_one.astype(F32)
-    out_sum = sum_along_z(jnp.transpose(out_sum))
-    sum_qkv = jnp.transpose(qkv_shard)
-    sum_up = jnp.transpose(up_shard)
-    sum_down = down_shard
     grad_start_norm, grad_gain_one, grad_bias_one = pull_one(grad_normed_one.reshape(rows, width))
     grad_start = grad_mid + grad_start_norm
     grad_table = jnp.einsum("tk,td->kd", onehot, grad_start, precision=HIGHEST_PRECISION)
@@ -1361,7 +1752,9 @@
         ],
         axis=0,
     )
-    sums = sum_everywhere(sums, out_sum)
+    sums, (qkv_shard,) = sum_everywhere(sums, [qkv_sum])
+    sum_qkv = jnp.transpose(qkv_shard)
+    sum_up = jnp.transpose(up_shard)
     return (
         output,
         grad_start.reshape(tokens.shape),
@@ -1369,7 +1762,7 @@
         sums[TYPES],
         sums[TYPES + 1],
         sum_qkv.astype(F32),
-        jnp.transpose(out_sum).astype(F32),
+        out_sum.astype(F32),
         sums[TYPES + 2],
         sums[TYPES + 3],
         sum_up.astype(F32),

time: 1110 us -> 997 us (0.90)
  matrix products: 259 us -> 133 us
  Pallas kernels: 617 us -> 691 us
  starting transfers between devices: 37.2 us -> 11.3 us
  waiting for transfers between devices: 62.6 us -> 38.7 us
  other arithmetic: 66.4 us -> 51.5 us
    pallas_call x1 -> x2, Pallas kernels: 21.5 us -> 192 us  [the longest x1 168 us: feed_back(): pl.pallas_call(feed_kernel, out_shape=[shaped(count, width)] * 2 + [shape...]
    pallas_call x7 -> x6, Pallas kernels: 550 us -> 454 us  [kernel_call(): pl.pallas_call(body, out_shape=outputs, in_specs=[pl.BlockSpec(memory_spa...]
    dot_general x8 -> x2, matrix products: 101 us -> 41.9 us  [grouped_shards(): jnp.einsum('td,id->ti', input_part, up_full, preferred_element_type=F32)]
    dot_general x6 -> x2, matrix products: 76.6 us -> 20.1 us  [weight_grad(): jnp.einsum('ti,td->id', a, b, preferred_element_type=F32)]
    ppermute x20 -> x12, waiting for transfers between devices: 62.4 us -> 32 us  [swap(): return lax.ppermute(value, 'dp', [(i, i ^ mask) for i in range(dp)])]
    ppermute x20 -> x12, starting transfers between devices: 36.3 us -> 10.9 us  [swap(): return lax.ppermute(value, 'dp', [(i, i ^ mask) for i in range(dp)])]
    dot_general x2, matrix products: 40.6 us -> 26.3 us  [grouped_shards(): jnp.einsum('td,id->ti', cot_part, down_full, preferred_element_type=F32)]
    convert_element_type x8 -> x4, other arithmetic: 20.2 us -> 6.51 us  [the longest x1 2.1 us: grouped_shards(): norm_two.astype(BF16)]
  transfers between devices with their start and end apart: 27 -> 17, of which waited for: 13 -> 8; matrix products, arithmetic and copies ran while one was open for 31% -> 16% of each run, Pallas kernels for 41% -> 38%
where the time goes in v2:
time: 997 us; the launch traced here: 988 us
  Pallas kernels  691 us (69%)
  matrix products  133 us (13%)
  other arithmetic  51.5 us (5%)
  local copies, waits for them, and re-layouts  48.1 us (5%)
  waiting for transfers between devices  38.7 us (4%)
  between operations  14.8 us (1%)
  starting transfers between devices  11.3 us (1%)
    pallas_call x6, Pallas kernels, kernel_call(): pl.pallas_call(body, out_shape=outputs, in_specs=[pl.BlockSpec(memory_spa...  454 us
    pallas_call x1, Pallas kernels, feed_back(): pl.pallas_call(feed_kernel, out_shape=[shaped(count, width)] * 2 + [shape...  168 us
    dot_general x2, matrix products, grouped_shards(): jnp.einsum('td,id->ti', input_part, up_full, preferred_element_type=F32)  41.9 us
    ppermute x12, waiting for transfers between devices, swap(): return lax.ppermute(value, 'dp', [(i, i ^ mask) for i in range(dp)])  32 us
    unnamed x101, local copies, waits for them, and re-layouts  27.2 us
    dot_general x2, matrix products, grouped_shards(): jnp.einsum('td,id->ti', cot_part, down_full, preferred_element_type=F32)  26.3 us
    pallas_call x1, Pallas kernels, attend_back(): pl.pallas_call(kernel, grid=(SEQS, heads), in_specs=[pl.BlockSpec(memory_...  25.3 us
    pallas_call x1, Pallas kernels, sum_everywhere(): pl.pallas_call(lambda *refs: sum_everywhere_kernel(number, *refs), out_sh...  23.4 us
  transfers between devices with their start and end apart: 17, of which 8 were waited for; matrix products, arithmetic and copies ran while one was open for 16% of the time, Pallas kernels for 38%

profile of v2, /device:TPU:0, one launch (start us, length us, event | category | flops | bytes accessed | tf_op | source)
XLA Modules:
  0.0 987.9 jit_solution(9728438000181616891)
XLA Ops:
  14.2 10.3 %intake.1 = (bf16[4,8,512]{2,1,0:T(8,128)(2,1)}, s32[8,8,128]{2,1,0:T(8,128)}) custom-call(bf16[8,512]{1,0:T(8,128)(2,1)} %concatenate.33.refs_0_, s32[8,128]{1,0:T(8,128)} %broadcast_in_dim.32.refs_1_), custom_call_target="tpu_custom_call" | custom-call | bytes 31457280 | tf_op jit(solution)/shard_map/intake/pallas_call | solution.py:469
  34.9 5.9 all-gather.4.cloned.1.call-done
  43.1 121.7 %first_gather.1 = (bf16[4,512,2048]{2,1,0:T(8,128)(2,1)}, bf16[4,512,2048]{2,1,0:T(8,128)(2,1)}, bf16[6,192,2048]{2,1,0:T(8,128)(2,1)}, bf16[256,2048]{1,0:T(8,1...) custom-call(bf16[2,256,2048]{2,1,0:T(8,128)(2,1)} %bitcast.128, bf16[1536,256]{1,0:T(8,128)(2,1)} %bitcast.136, ...), custom_call_target="tpu_custom_call" | custom-call | bytes 346030080 | tf_op jit(solution)/shard_map/first_gather/pallas_call | solution.py:469
  171.0 11.6 %convolution_convert_fusion.2 = bf16[2048,768]{1,0:T(8,128)(2,1)} fusion(bf16[2048,2048]{1,0:T(8,128)(2,1)} %bitcast.159, bf16[768,2048]{1,0:T(8,128)(2,1)S(1)} %bitcast.123), kind=kOutput, calls=%fused_computation.50 | convolution fusion | flops 6444023808 | bytes 14680064 | tf_op jit(solution)/shard_map/td,ed->te/dot_general | solution.py:1679
  182.6 8.1 convolution_convert_fusion.3
  191.0 19.7 %attend.1 = (bf16[4,512,256]{2,1,0:T(8,128)(2,1)}, bf16[4,512,256]{2,1,0:T(8,128)(2,1)}, f32[4,2,8,512]{3,2,1,0:T(8,128)}, f32[4,2,8,512]{3,2,1,0:T(8,128)}) custom-call(s32[5]{0:T(128)} %pad_add_fusion.flags_ref, bf16[4,512,768]{2,1,0:T(8,128)(2,1)} %bitcast.175, bf16[4,512,768]{2,1,0:T(8,128)(2,1)} %bitcast.173), custom_call_target="tpu_custom_call" | custom-call | flops 3221225472 | bytes 8388608 | tf_op jit(solution)/shard_map/attend/pallas_call | solution.py:1463
  210.7 67.1 %contexts_home.1 = (bf16[2,256,2048]{2,1,0:T(8,128)(2,1)}, bf16[4,256,2048]{2,1,0:T(8,128)(2,1)}, bf16[4,256,2048]{2,1,0:T(8,128)(2,1)}) custom-call(bf16[4,512,256]{2,1,0:T(8,128)(2,1)} %get-tuple-element.57.refs_0_, bf16[4,512,256]{2,1,0:T(8,128)(2,1)} %get-tuple-element.58.refs_1_, bf16[256,2048]{1,0:T(8,128)(2,1)} %bitcast.130), custom_call_target="tpu_custom_call" | custom-call | bytes 188743680 | tf_op jit(solution)/shard_map/contexts_home/pallas_call | solution.py:469
  277.8 5.0 fusion.26
  313.2 84.1 %plane_gather.1 = (bf16[4,512,2048]{2,1,0:T(8,128)(2,1)}, bf16[4,512,2048]{2,1,0:T(8,128)(2,1)}, bf16[2048,2048]{1,0:T(8,128)(2,1)}) custom-call(bf16[512,2048]{1,0:T(8,128)(2,1)} %add_convert_fusion.2.refs_0_, bf16[2048,2048]{1,0:T(8,128)(2,1)} %constant_dynamic-update-slice_fusion.refs_1_.cot_chips), custom_call_target="tpu_custom_call" | custom-call | bytes 239075328 | tf_op jit(solution)/shard_map/plane_gather/pallas_call | solution.py:469
  397.3 15.1 %fusion.38 = f32[2048,1024]{1,0:T(8,128)} fusion(bf16[2048,2048]{1,0:T(8,128)(2,1)} %constant_dynamic-update-slice_fusion.refs_1_.cot_chips, bf16[1024,2048]{1,0:T(8,128)(2,1)} %all-gather.6.cloned.1.call-done.down_ref), kind=kOutput, calls=%fused_computation.111 | convolution fusion | flops 8589934592 | bytes 20971520 | tf_op jit(solution)/shard_map/td,id->ti/dot_general | solution.py:1706
  412.5 11.2 %fusion.39 = f32[2048,1024]{1,0:T(8,128)} fusion(bf16[2048,2048]{1,0:T(8,128)(2,1)S(1)} %copy-done.36, bf16[1024,2048]{1,0:T(8,128)(2,1)S(1)} %copy-done.37), kind=kOutput, calls=%fused_computation.112 | convolution fusion | flops 8589934592 | bytes 20971520 | tf_op jit(solution)/shard_map/td,id->ti/dot_general | solution.py:1706
  423.7 22.2 %multiply_convert_fusion.1 = (bf16[2048,1024]{1,0:T(8,128)(2,1)}, bf16[2048,1024]{1,0:T(8,128)(2,1)}) fusion(f32[2048,1024]{1,0:T(8,128)} %fusion.38, bf16[2048,2048]{1,0:T(8,128)(2,1)} %bitcast.161, bf16[1024,2048]{1,0:T(8,128)(2,1)} %all-gather.8.cloned.1.call-done.up_ref), kind=kOutput, calls=%fused_computation.21 | convolution fusion | flops 8644460544 | bytes 29360128 | tf_op jit(solution)/shard_map/td,id->ti/dot_general | solution.py:1707
  445.9 19.7 %multiply_convert_fusion = (bf16[2048,1024]{1,0:T(8,128)(2,1)}, bf16[2048,1024]{1,0:T(8,128)(2,1)}) fusion(f32[2048,1024]{1,0:T(8,128)S(1)} %copy-done.43, bf16[2048,2048]{1,0:T(8,128)(2,1)} %bitcast.163, bf16[1024,2048]{1,0:T(8,128)(2,1)S(1)} %copy-done.40), kind=kOutput, calls=%fused_computation.20 | convolution fusion | flops 8644460544 | bytes 29360128 | tf_op jit(solution)/shard_map/td,id->ti/dot_general | solution.py:1707
  465.6 168.3 %feed_back.1 = (bf16[512,2048]{1,0:T(8,128)(2,1)}, bf16[512,2048]{1,0:T(8,128)(2,1)}, bf16[4,256,2048]{2,1,0:T(8,128)(2,1)}, bf16[1024,2048]{1,0:T(8,128)(2,1)}) custom-call(bf16[2048,1024]{1,0:T(8,128)(2,1)} %get-tuple-element.132.grad_chips, bf16[2048,1024]{1,0:T(8,128)(2,1)} %get-tuple-element.130.grad_others, ...), custom_call_target="tpu_custom_call" | custom-call | flops 68719476736 | bytes 503316480 | tf_op jit(solution)/shard_map/feed_back/pallas_call | solution.py:1132
  654.7 4.7 convolution_convert_fusion.4
  663.3 69.0 %gradients_out.1 = (bf16[2,4,512,256]{3,2,1,0:T(8,128)(2,1)}, bf16[2048,256]{1,0:T(8,128)(2,1)}) custom-call(bf16[2,256,2048]{2,1,0:T(8,128)(2,1)} %bitcast.129, bf16[256,2048]{1,0:T(8,128)(2,1)} %reduce_sum.128.refs_1_), custom_call_target="tpu_custom_call" | custom-call | bytes 157286400 | tf_op jit(solution)/shard_map/gradients_out/pallas_call | solution.py:469
  742.2 25.3 %attend_back.1 = (bf16[4,512,768]{2,1,0:T(8,128)(2,1)}, bf16[4,512,768]{2,1,0:T(8,128)(2,1)}) custom-call(s32[5]{0:T(128)} %pad_add_fusion.flags_ref, bf16[4,512,768]{2,1,0:T(8,128)(2,1)} %bitcast.176, bf16[4,512,768]{2,1,0:T(8,128)(2,1)} %bitcast.174, bf16[2,4,512,256]{3,2,1,0:T(8,128)(2,1)} %get-tuple-element.77.refs_2_, ...), custom_call_target="tpu_custom_call" | custom-call | flops 8589934592 | bytes 16777216 | tf_op jit(solution)/shard_map/attend_back/pallas_call | solution.py:1542
  767.5 10.5 %fusion.40 = f32[768,2048]{1,0:T(8,128)S(1)} fusion(bf16[2048,768]{1,0:T(8,128)(2,1)} %bitcast.134, bf16[2048,2048]{1,0:T(8,128)(2,1)} %bitcast.160), kind=kOutput, calls=%fused_computation.113 | convolution fusion | flops 6442450944 | bytes 17825792 | tf_op jit(solution)/shard_map/ti,td->id/dot_general | solution.py:1699
  778.0 9.6 add_convert_fusion
  797.6 11.9 %collective-permute-done.7 = bf16[128,2048]{1,0:T(8,128)(2,1)S(1)} collective-permute-done((bf16[128,2048]{1,0:T(8,128)(2,1)S(1)}, bf16[128,2048]{1,0:T(8,128)(2,1)S(1)}, u32[]{:S(2)}, u32[]{:S(2)}) %collective-permute-start.7) | collective-permute-done | bytes 524320 | tf_op jit(solution)/shard_map/ppermute | solution.py:308
  819.4 7.6 collective-permute-done.10
  830.1 101.6 %last_scatter.1 = (bf16[2,256,2048]{2,1,0:T(8,128)(2,1)}, bf16[256,512]{1,0:T(8,128)(2,1)}, bf16[2048,256]{1,0:T(8,128)(2,1)}) custom-call(bf16[2048,768]{1,0:T(8,128)(2,1)} %bitcast.132, bf16[2048,768]{1,0:T(8,128)(2,1)} %bitcast.135, bf16[768,2048]{1,0:T(8,128)(2,1)} %bitcast.125, bf16[256,2048]{1,0:T(8,128)(2,1)} %pad_maximum_fusion.2.refs_3_, ...), custom_call_target="tpu_custom_call" | custom-call | bytes 314572800 | tf_op jit(solution)/shard_map/last_scatter/pallas_call | solution.py:469
  940.1 5.3 add_add_fusion.2
  952.3 23.4 %sum_everywhere.1 = (f32[4,128]{1,0:T(4,128)}, bf16[1536,256]{1,0:T(8,128)(2,1)}) custom-call(f32[32,4,128]{2,1,0:T(4,128)} %reshape.206.refs_0_, bf16[192,2048]{1,0:T(8,128)(2,1)} %reduce-scatter.5.cloned.1.call-done.refs_1_), custom_call_target="tpu_custom_call" | custom-call | bytes 41943040 | tf_op jit(solution)/shard_map/sum_everywhere/pallas_call | solution.py:1601
  (209 shorter events, 134.1 us)
Async XLA Ops:
  7.2 33.7 %all-gather.4.cloned.1.call-start = ((), (), s32[]{:S(2)}) async-start(), calls=%async_computation.2 | async-start | bytes 1310720 | tf_op jit(solution)/shard_map/all_gather | solution.py:1184
  7.9 389.4 %all-gather.6.cloned.1.call-start = ((), (), s32[]{:S(2)}) async-start(), calls=%async_computation.3 | async-start | bytes 5242880 | tf_op jit(solution)/shard_map/all_gather | solution.py:1184
  32.3 257.8 %copy-start.19 = (f32[1,4,512]{2,0,1:T(1,128)}, f32[1,4,512]{2,0,1:T(1,128)S(1)}, u32[]{:S(2)}) copy-start(f32[1,4,512]{2,0,1:T(1,128)S(1)} %get-tuple-element.136) | copy-start | bytes 24580
  34.9 131.9 %copy-start.7 = (bf16[2,256,2048]{2,1,0:T(8,128)(2,1)S(1)}, bf16[2,256,2048]{2,1,0:T(8,128)(2,1)}, u32[]{:S(2)}) copy-start(bf16[2,256,2048]{2,1,0:T(8,128)(2,1)} %param.25) | copy-start | bytes 6291460
  164.8 258.8 %all-gather.8.cloned.1.call-start = ((), (), s32[]{:S(2)}) async-start(), calls=%async_computation.4 | async-start | bytes 5242880 | tf_op jit(solution)/shard_map/all_gather | solution.py:1184
  166.8 119.9 %collective-permute-start.1 = (bf16[512,2048]{1,0:T(8,128)(2,1)S(1)}, bf16[512,2048]{1,0:T(8,128)(2,1)}, u32[]{:S(2)}, u32[]{:S(2)}) collective-permute-start(bf16[512,2048]{1,0:T(8,128)(2,1)S(1)} %bitcast.118), channel_id=1, source_target_pairs={{0,16},{4,20},{8,24},{12,28},{16,0},{20,4},{24,8},{28,12},{1,17},{... | collective-permute-start | bytes 6291464 | tf_op jit(solution)/shard_map/ppermute | solution.py:308
  167.4 124.8 %collective-permute-start = (bf16[512,2048]{1,0:T(8,128)(2,1)S(1)}, bf16[512,2048]{1,0:T(8,128)(2,1)}, u32[]{:S(2)}, u32[]{:S(2)}) collective-permute-start(bf16[512,2048]{1,0:T(8,128)(2,1)S(1)} %bitcast.119), channel_id=1, source_target_pairs={{0,8},{4,12},{8,0},{12,4},{16,24},{20,28},{24,16},{28,20},{1,9},{5... | collective-permute-start | bytes 6291464 | tf_op jit(solution)/shard_map/ppermute | solution.py:308
  190.8 639.3 %reduce-scatter.3.cloned.1.call-start = ((), (), s32[]{:S(2)}) async-start(), calls=%async_computation.5 | async-start | bytes 5242880 | tf_op jit(solution)/shard_map/reduce_scatter | solution.py:1188
  288.8 18.5 %collective-permute-start.2 = (bf16[256,2048]{1,0:T(8,128)(2,1)S(1)}, bf16[256,2048]{1,0:T(8,128)(2,1)S(1)}, u32[]{:S(2)}, u32[]{:S(2)}) collective-permute-start(bf16[256,2048]{1,0:T(8,128)(2,1)S(1)} %slice.155), channel_id=1, source_target_pairs={{0,8},{4,12},{8,0},{12,4},{16,24},{20,28},{24,16},{28,20},{1,9},{5... | collective-permute-start | bytes 3145736 | tf_op jit(solution)/shard_map/ppermute | solution.py:308
  293.5 18.6 %collective-permute-start.3 = (bf16[256,2048]{1,0:T(8,128)(2,1)S(1)}, bf16[256,2048]{1,0:T(8,128)(2,1)S(1)}, u32[]{:S(2)}, u32[]{:S(2)}) collective-permute-start(bf16[256,2048]{1,0:T(8,128)(2,1)S(1)} %slice.156), channel_id=1, source_target_pairs={{0,16},{4,20},{8,24},{12,28},{16,0},{20,4},{24,8},{28,12},{1,17},{... | collective-permute-start | bytes 3145736 | tf_op jit(solution)/shard_map/ppermute | solution.py:308
  465.6 168.4 %copy-start.20 = (f32[1,4,512]{2,0,1:T(1,128)S(1)}, f32[1,4,512]{2,0,1:T(1,128)}, u32[]{:S(2)}) copy-start(f32[1,4,512]{2,0,1:T(1,128)} %copy-done.19) | copy-start | bytes 24580
  465.6 168.4 %copy-start.25 = (f32[512]{0:T(512)S(1)}, f32[512]{0:T(512)}, u32[]{:S(2)}) copy-start(f32[512]{0:T(512)} %copy-done.24) | copy-start | bytes 6148
  465.6 168.4 %copy-start.27 = (f32[512]{0:T(512)S(1)}, f32[512]{0:T(512)}, u32[]{:S(2)}) copy-start(f32[512]{0:T(512)} %copy-done.26) | copy-start | bytes 6148
  650.5 85.6 %collective-permute-start.4 = (bf16[1024,2048]{1,0:T(8,128)(2,1)}, bf16[1024,2048]{1,0:T(8,128)(2,1)}, u32[]{:S(2)}, u32[]{:S(2)}) collective-permute-start(bf16[1024,2048]{1,0:T(8,128)(2,1)} %convolution_convert_fusion), channel_id=1, source_target_pairs={{0,4},{4,0},{8,12},{12,8},{16,20},{20,16},{24,28},{28,24},{1,5},{5... | collective-permute-start | bytes 12582920 | tf_op jit(solution)/shard_map/ppermute | solution.py:308
  732.4 219.9 %reduce-scatter.5.cloned.1.call-start = ((), (), s32[]{:S(2)}) async-start(), calls=%async_computation.6 | async-start | bytes 3932160 | tf_op jit(solution)/shard_map/reduce_scatter | solution.py:1188
  739.9 27.6 %collective-permute-start.6 = (bf16[128,2048]{1,0:T(8,128)(2,1)S(1)}, bf16[128,2048]{1,0:T(8,128)(2,1)S(1)}, u32[]{:S(2)}, u32[]{:S(2)}) collective-permute-start(bf16[128,2048]{1,0:T(8,128)(2,1)S(1)} %get-tuple-element.127), channel_id=1, source_target_pairs={{0,16},{4,20},{8,24},{12,28},{16,0},{20,4},{24,8},{28,12},{1,17},{... | collective-permute-start | bytes 1572872 | tf_op jit(solution)/shard_map/ppermute | solution.py:308
  741.5 26.0 %collective-permute-start.5 = (bf16[128,2048]{1,0:T(8,128)(2,1)S(1)}, bf16[128,2048]{1,0:T(8,128)(2,1)S(1)}, u32[]{:S(2)}, u32[]{:S(2)}) collective-permute-start(bf16[128,2048]{1,0:T(8,128)(2,1)S(1)} %get-tuple-element.128), channel_id=1, source_target_pairs={{0,8},{4,12},{8,0},{12,4},{16,24},{20,28},{24,16},{28,20},{1,9},{5... | collective-permute-start | bytes 1572872 | tf_op jit(solution)/shard_map/ppermute | solution.py:308
  787.8 3.5 collective-permute-start.11
  795.4 14.0 %collective-permute-start.7 = (bf16[128,2048]{1,0:T(8,128)(2,1)S(1)}, bf16[128,2048]{1,0:T(8,128)(2,1)S(1)}, u32[]{:S(2)}, u32[]{:S(2)}) collective-permute-start(bf16[128,2048]{1,0:T(8,128)(2,1)S(1)} %get-tuple-element.125), channel_id=1, source_target_pairs={{0,8},{4,12},{8,0},{12,4},{16,24},{20,28},{24,16},{28,20},{1,9},{5... | collective-permute-start | bytes 1572872 | tf_op jit(solution)/shard_map/ppermute | solution.py:308
  796.8 13.7 %collective-permute-start.8 = (bf16[128,2048]{1,0:T(8,128)(2,1)S(1)}, bf16[128,2048]{1,0:T(8,128)(2,1)S(1)}, u32[]{:S(2)}, u32[]{:S(2)}) collective-permute-start(bf16[128,2048]{1,0:T(8,128)(2,1)S(1)} %get-tuple-element.126), channel_id=1, source_target_pairs={{0,16},{4,20},{8,24},{12,28},{16,0},{20,4},{24,8},{28,12},{1,17},{... | collective-permute-start | bytes 1572872 | tf_op jit(solution)/shard_map/ppermute | solution.py:308
  813.9 13.1 %collective-permute-start.10 = (bf16[128,2048]{1,0:T(8,128)(2,1)}, bf16[128,2048]{1,0:T(8,128)(2,1)}, u32[]{:S(2)}, u32[]{:S(2)}) collective-permute-start(bf16[128,2048]{1,0:T(8,128)(2,1)} %get-tuple-element.123), channel_id=1, source_target_pairs={{0,16},{4,20},{8,24},{12,28},{16,0},{20,4},{24,8},{28,12},{1,17},{... | collective-permute-start | bytes 1572872 | tf_op jit(solution)/shard_map/ppermute | solution.py:308
  814.5 12.7 %collective-permute-start.9 = (bf16[128,2048]{1,0:T(8,128)(2,1)S(1)}, bf16[128,2048]{1,0:T(8,128)(2,1)}, u32[]{:S(2)}, u32[]{:S(2)}) collective-permute-start(bf16[128,2048]{1,0:T(8,128)(2,1)S(1)} %get-tuple-element.124), channel_id=1, source_target_pairs={{0,8},{4,12},{8,0},{12,4},{16,24},{20,28},{24,16},{28,20},{1,9},{5... | collective-permute-start | bytes 1572872 | tf_op jit(solution)/shard_map/ppermute | solution.py:308
  830.1 103.9 %copy-start.18 = (f32[1,4,512]{2,0,1:T(1,128)S(1)}, f32[1,4,512]{2,0,1:T(1,128)}, u32[]{:S(2)}) copy-start(f32[1,4,512]{2,0,1:T(1,128)} %copy-done.17) | copy-start | bytes 24580
  830.1 103.9 %copy-start.22 = (f32[512]{0:T(512)S(1)}, f32[512]{0:T(512)}, u32[]{:S(2)}) copy-start(f32[512]{0:T(512)} %copy-done.21) | copy-start | bytes 6148
  (39 other events, 281.4 us)
Sparse Core Ops, SparseCore 0:
  9.6 31.2 all-gather.3
  164.9 113.2 all-gather.5
  279.8 79.4 all-gather.7
  732.5 75.5 reduce-scatter.2
  810.4 84.1 reduce-scatter.4

commit v3 on v2

--- a/solution.py
+++ b/solution.py
@@ -509,7 +509,7 @@
     )
 
 
-def gather_rows(moves, rows_ref, chips_ref, others_ref, ready=None, pieces=2):
+def gather_rows(moves, rows_ref, chips_ref, others_ref, ready=None, pieces=2, passed=None):
     d = lax.axis_index("dp")
     z = lax.axis_index("seq")
     size = chips_ref.shape[1] // pieces
@@ -518,6 +518,10 @@
 
     def far(source, target, mask):
         return moves.far(source, target, d ^ mask, z)
+
+    def keep(chip, move):
+        if passed is not None:
+            passed.setdefault(chip, []).append(move)
 
     if ready is None:
         moves.here(rows_ref, chips_ref.at[0])
@@ -532,11 +536,11 @@
             source = chips_ref.at[0, part]
         over_x[number] = far(source, chips_ref.at[1, part], X_WAY)
         over_y[number] = far(source, chips_ref.at[2, part], Y_WAY)
-        far(source, others_ref.at[0, part], CORE)
+        keep(0, far(source, others_ref.at[0, part], CORE))
 
     def pass_on(chip, number):
         part = parts[number]
-        far(chips_ref.at[chip, part], others_ref.at[chip, part], CORE)
+        keep(chip, far(chips_ref.at[chip, part], others_ref.at[chip, part], CORE))
 
     corner = {}
     for number in order:
@@ -659,34 +663,101 @@
     )[:5]
 
 
-def gather_kernel(rows_ref, held_ref, chips, others, held_others, *sems):
+def gather_kernel(
+    rows_ref,
+    held_ref,
+    weights_ref,
+    chips,
+    others,
+    held_others,
+    chips_out,
+    others_out,
+    weights,
+    blocks_held,
+    results_held,
+    weights_sem,
+    blocks_sem,
+    results_sem,
+    *sems,
+):
     moves = Moves(*sems)
     d = lax.axis_index("dp")
     z = lax.axis_index("seq")
+    count = rows_ref.shape[0]
+    blocks = Slots(blocks_held, blocks_sem)
+    results = Slots(results_held, results_sem)
+    weights_in = pltpu.make_async_copy(weights_ref, weights, weights_sem)
+    weights_in.start()
     meet_all((CORE, X_WAY, Y_WAY), lines=False)
-    steps = gather_rows(moves, rows_ref, chips, others)
+    passed = {}
+    done = []
+
+    def multiply(source, target, chip, block=None):
+        slot = len(done) % 2
+        done.append(chip)
+        if block is None:
+            blocks.load(slot, source.at[chip])
+            block = blocks.wait(slot)
+        result = results.wait(slot)
+
+        @pl.loop(0, count // 256)
+        def _(i):
+            at = pl.ds(pl.multiple_of(i * 256, 256), 256)
+            result[at, :] = lax.dot_general(
+                block[at, :], weights[...], (((1,), (1,)), ((), ())), preferred_element_type=F32
+            )
+
+        results.store(slot, target.at[pl.ds(chip * count, count)])
+
+    def multiply_others(chip):
+        all_landed(moves, passed[chip])
+        multiply(others, others_out, chip)
+
+    steps = gather_rows(moves, rows_ref, chips, others, passed=passed)
     next(steps)
     moves.far(held_ref, held_others, d ^ CORE, z)
-    for _ in steps:
-        pass
+    weights_in.wait()
+    multiply(None, chips_out, 0, rows_ref)
+    multiply_others(0)
+    next(steps)
+    next(steps)
+    for chip in (1, 2):
+        multiply(chips, chips_out, chip)
+    for chip in (1, 2):
+        multiply_others(chip)
+    next(steps, None)
+    multiply(chips, chips_out, 3)
+    multiply_others(3)
+    for slot in range(2):
+        results.wait(slot)
     moves.finish()
 
 
-def plane_gather_now(rows, held, number, late):
+def gather_multiply(rows, held, weights, number):
     count, width = rows.shape
-    chips, others, held_others = kernel_call(
+    units = weights.shape[0]
+    product = jax.ShapeDtypeStruct((4 * count, units), F32)
+    chips, others, held_others, chips_out, others_out = kernel_call(
         gather_kernel,
-        [rows, held],
-        [shaped(4, count, width), shaped(4, count, width), shaped(*held.shape)],
+        [rows, held, weights],
+        [shaped(4, count, width), shaped(4, count, width), shaped(*held.shape), product, product],
         GATHER_COPIES + 1,
         1,
         number,
-        "plane_gather",
-        76,
-        [pltpu.VMEM, pl.ANY],
-        late=late,
-    )
-    return [part.reshape(4 * count, width) for part in (chips, others)], held_others
+        "gather_multiply",
+        80,
+        [pltpu.VMEM, pl.ANY, pl.ANY],
+        [
+            pltpu.VMEM((units, width), BF16),
+            pltpu.VMEM((2, count, width), BF16),
+            pltpu.VMEM((2, count, units), F32),
+            pltpu.SemaphoreType.DMA(()),
+            pltpu.SemaphoreType.DMA((2,)),
+            pltpu.SemaphoreType.DMA((2,)),
+        ],
+    )
+    rows = [part.reshape(4 * count, width) for part in (chips, others)]
+    return rows, held_others, (chips_out, others_out)
 
 
 def add_rows(target, start, sources, count, step=64):
@@ -1232,10 +1303,14 @@
 
     def sides(self, tied):
         half = self.count // 2
-        self.far, tied = lax.optimization_barrier((self.far, tied))
+        self.far, self.near, tied = lax.optimization_barrier((self.far, self.near, tied))
         x_second = self.both(self.count + half, half) + self.far[1].astype(F32)
         y_first = self.both(2 * self.count, half) + self.far[0].astype(F32)
         self.last = swap(x_second.astype(BF16), X_WAY), swap(y_first.astype(BF16), Y_WAY)
+        return tied
+
+    def ends(self, tied):
+        self.last, tied = lax.optimization_barrier((self.last, tied))
         return tied
 
     def result(self):
@@ -1690,9 +1765,10 @@
         + jnp.dot(context_rows[:, width // 2 :], out_others, preferred_element_type=F32)
     )
     norm_two, pull_two = jax.vjp(layer_norm, mid_hidden, gain_two, bias_two)
-    ffn_input, cot_others = plane_gather_now(
-        norm_two.astype(BF16), cot_chips, 5, []
-    )
+    ffn_input, cot_others, ups = gather_multiply(
+        norm_two.astype(BF16), cot_chips, up_full, 5
+    )
+    cot_chips, ups = lax.optimization_barrier((cot_chips, ups))
     cots = (cot_chips, cot_others)
     def weight_grad(left, right):
         return sum(
@@ -1702,9 +1778,8 @@
 
     acts = []
     grad_ups = []
-    for cot_part, input_part in zip(cots, ffn_input):
+    for cot_part, up_value in zip(cots, ups):
         grad_act = jnp.einsum("td,id->ti", cot_part, down_full, preferred_element_type=F32)
-        up_value = jnp.einsum("td,id->ti", input_part, up_full, preferred_element_type=F32)
         activated, gelu_pull = jax.vjp(gelu_tanh, up_value)
         acts.append(activated.astype(BF16))
         grad_ups.append(gelu_pull(grad_act)[0].astype(BF16))
@@ -1736,7 +1811,8 @@
     grad_qkv = attend_back(qkv, grad_by_heads, lse, flags, heads)
     grad_qkv = [part.reshape(SEQS * rows, 3 * heads * HEAD_DIM) for part in grad_qkv]
     grad_qkv = out_scatter.sides(grad_qkv)
-    qkv_grad = shared_heads(weight_grad(grad_qkv, normed))
+    late_grad = out_scatter.ends(grad_qkv[1])
+    qkv_grad = shared_heads(weight_grad((grad_qkv[0], late_grad), normed))
     qkv_sum = sum_along_z(qkv_grad)
     grad_normed_one, out_sum, sum_down = last_scatter(
         grad_qkv, qkv_full, out_scatter.result().astype(BF16), down_sum, tokens.shape

time: 997 us -> 978 us (0.981)
  matrix products: 133 us -> 93.4 us
  other arithmetic: 51.5 us -> 70 us
    dot_general x2 -> x0, matrix products: 41.9 us -> none  [grouped_shards(): jnp.einsum('td,id->ti', input_part, up_full, preferred_element_type=F32)]
    convert_element_type x2 -> x3, other arithmetic: 3.55 us -> 26 us  [the longest x1 18.8 us: grouped_shards(): acts.append(activated.astype(BF16))]
    pallas_call x1, Pallas kernels: 23.4 us -> 35.5 us  [sum_everywhere(): pl.pallas_call(lambda *refs: sum_everywhere_kernel(number, *refs), out_sh...]
    unnamed x101 -> x85, local copies, waits for them, and re-layouts: 27.2 us -> 27 us
  transfers between devices with their start and end apart: 17 -> 17, of which waited for: 8 -> 6; matrix products, arithmetic and copies ran while one was open for 16% -> 14% of each run, Pallas kernels for 38% -> 39%
where the time goes in v3:
time: 978 us; the launch traced here: 972 us
  Pallas kernels  699 us (71%)
  matrix products  93.4 us (10%)
  other arithmetic  70 us (7%)
  local copies, waits for them, and re-layouts  49.6 us (5%)
  waiting for transfers between devices  33.5 us (3%)
  between operations  14.7 us (2%)
  starting transfers between devices  11.8 us (1%)
    pallas_call x6, Pallas kernels, kernel_call(): pl.pallas_call(body, out_shape=outputs, in_specs=[pl.BlockSpec(memory_spa...  459 us
    pallas_call x1, Pallas kernels, feed_back(): pl.pallas_call(feed_kernel, out_shape=[shaped(count, width)] * 2 + [shape...  159 us
    pallas_call x1, Pallas kernels, sum_everywhere(): pl.pallas_call(lambda *refs: sum_everywhere_kernel(number, *refs), out_sh...  35.5 us
    dot_general x2, matrix products, grouped_shards(): jnp.einsum('td,id->ti', cot_part, down_full, preferred_element_type=F32)  27.5 us
    unnamed x85, local copies, waits for them, and re-layouts  27 us
    ppermute x12, waiting for transfers between devices, swap(): return lax.ppermute(value, 'dp', [(i, i ^ mask) for i in range(dp)])  26.8 us
    pallas_call x1, Pallas kernels, attend_back(): pl.pallas_call(kernel, grid=(SEQS, heads), in_specs=[pl.BlockSpec(memory_...  25.3 us
    dot_general x2, matrix products, grouped_shards(): jnp.einsum('td,ed->te', part, qkv_full, preferred_element_type=F32)  21.7 us
  transfers between devices with their start and end apart: 17, of which 6 were waited for; matrix products, arithmetic and copies ran while one was open for 14% of the time, Pallas kernels for 39%

profile of v3, /device:TPU:0, one launch (start us, length us, event | category | flops | bytes accessed | tf_op | source)
XLA Modules:
  0.0 972.1 jit_solution(6500424106547413152)
XLA Ops:
  14.2 10.3 %intake.1 = (bf16[4,8,512]{2,1,0:T(8,128)(2,1)}, s32[8,8,128]{2,1,0:T(8,128)}) custom-call(bf16[8,512]{1,0:T(8,128)(2,1)} %concatenate.33.refs_0_, s32[8,128]{1,0:T(8,128)} %broadcast_in_dim.32.refs_1_), custom_call_target="tpu_custom_call" | custom-call | bytes 31457280 | tf_op jit(solution)/shard_map/intake/pallas_call | solution.py:469
  34.9 6.0 all-gather.4.cloned.1.call-done
  43.1 121.7 %first_gather.1 = (bf16[4,512,2048]{2,1,0:T(8,128)(2,1)}, bf16[4,512,2048]{2,1,0:T(8,128)(2,1)}, bf16[6,192,2048]{2,1,0:T(8,128)(2,1)}, bf16[256,2048]{1,0:T(8,1...) custom-call(bf16[2,256,2048]{2,1,0:T(8,128)(2,1)} %bitcast.124, bf16[1536,256]{1,0:T(8,128)(2,1)} %bitcast.136, ...), custom_call_target="tpu_custom_call" | custom-call | bytes 346030080 | tf_op jit(solution)/shard_map/first_gather/pallas_call | solution.py:469
  173.0 11.4 %convolution_convert_fusion.2 = bf16[2048,768]{1,0:T(8,128)(2,1)} fusion(bf16[2048,2048]{1,0:T(8,128)(2,1)} %bitcast.157, bf16[768,2048]{1,0:T(8,128)(2,1)} %bitcast.119), kind=kOutput, calls=%fused_computation.50 | convolution fusion | flops 6444023808 | bytes 14680064 | tf_op jit(solution)/shard_map/td,ed->te/dot_general | solution.py:1754
  184.3 10.3 %convolution_convert_fusion.3 = bf16[2048,768]{1,0:T(8,128)(2,1)} fusion(bf16[2048,2048]{1,0:T(8,128)(2,1)} %bitcast.155, bf16[768,2048]{1,0:T(8,128)(2,1)S(1)} %bitcast.121), kind=kOutput, calls=%fused_computation.51 | convolution fusion | flops 6444023808 | bytes 14680064 | tf_op jit(solution)/shard_map/td,ed->te/dot_general | solution.py:1754
  194.6 19.7 %attend.1 = (bf16[4,512,256]{2,1,0:T(8,128)(2,1)}, bf16[4,512,256]{2,1,0:T(8,128)(2,1)}, f32[4,2,8,512]{3,2,1,0:T(8,128)}, f32[4,2,8,512]{3,2,1,0:T(8,128)}) custom-call(s32[5]{0:T(128)} %pad_add_fusion.flags_ref, bf16[4,512,768]{2,1,0:T(8,128)(2,1)} %bitcast.171, bf16[4,512,768]{2,1,0:T(8,128)(2,1)} %bitcast.169), custom_call_target="tpu_custom_call" | custom-call | flops 3221225472 | bytes 8388608 | tf_op jit(solution)/shard_map/attend/pallas_call | solution.py:1538
  214.3 69.9 %contexts_home.1 = (bf16[2,256,2048]{2,1,0:T(8,128)(2,1)}, bf16[4,256,2048]{2,1,0:T(8,128)(2,1)}, bf16[4,256,2048]{2,1,0:T(8,128)(2,1)}) custom-call(bf16[4,512,256]{2,1,0:T(8,128)(2,1)} %get-tuple-element.67.refs_0_, bf16[4,512,256]{2,1,0:T(8,128)(2,1)} %get-tuple-element.68.refs_1_, bf16[256,2048]{1,0:T(8,128)(2,1)} %bitcast.130), custom_call_target="tpu_custom_call" | custom-call | bytes 188743680 | tf_op jit(solution)/shard_map/contexts_home/pallas_call | solution.py:469
  284.3 5.3 fusion.26
  309.5 12.1 %collective-permute-done.2 = bf16[256,2048]{1,0:T(8,128)(2,1)S(1)} collective-permute-done((bf16[256,2048]{1,0:T(8,128)(2,1)S(1)}, bf16[256,2048]{1,0:T(8,128)(2,1)S(1)}, u32[]{:S(2)}, u32[]{:S(2)}) %collective-permute-start.2) | collective-permute-done | bytes 1048608 | tf_op jit(solution)/shard_map/ppermute | solution.py:308
  327.1 85.2 %gather_multiply.1 = (bf16[4,512,2048]{2,1,0:T(8,128)(2,1)}, bf16[4,512,2048]{2,1,0:T(8,128)(2,1)}, bf16[2048,2048]{1,0:T(8,128)(2,1)}, f32[2048,1024]{1,0:T(8,128)}, f32[2048,1024]{1,0:T(8,128)}) custom-call(bf16[512,2048]{1,0:T(8,128)(2,1)} %add_convert_fusion.2.refs_0_, bf16[2048,2048]{1,0:T(8,128)(2,1)} %constant_dynamic-update-slice_fusion.refs_1_.cot_chips, ...), custom_call_target="tpu_custom_call" | custom-call | bytes 251658240 | tf_op jit(solution)/shard_map/gather_multiply/pallas_call | solution.py:469
  412.4 12.7 %fusion.38 = f32[2048,1024]{1,0:T(8,128)S(1)} fusion(bf16[2048,2048]{1,0:T(8,128)(2,1)} %constant_dynamic-update-slice_fusion.refs_1_.cot_chips, bf16[1024,2048]{1,0:T(8,128)(2,1)} %all-gather.8.cloned.1.call-done.down_ref), kind=kOutput, calls=%fused_computation.111 | convolution fusion | flops 8589934592 | bytes 20971520 | tf_op jit(solution)/shard_map/td,id->ti/dot_general | solution.py:1782
  425.1 14.9 %fusion.39 = f32[2048,1024]{1,0:T(8,128)} fusion(bf16[2048,2048]{1,0:T(8,128)(2,1)} %get-tuple-element.81.cot_others, bf16[1024,2048]{1,0:T(8,128)(2,1)} %all-gather.8.cloned.1.call-done.down_ref), kind=kOutput, calls=%fused_computation.112 | convolution fusion | flops 8589934592 | bytes 20971520 | tf_op jit(solution)/shard_map/td,id->ti/dot_general | solution.py:1782
  440.0 18.8 %multiply_convert_fusion = (bf16[2048,1024]{1,0:T(8,128)(2,1)}, bf16[2048,1024]{1,0:T(8,128)(2,1)}, bf16[2048,1024]{1,0:T(8,128)(2,1)}, bf16[2048,1024]{1,0:T(8,128)(2,1)}) fusion(f32[2048,1024]{1,0:T(8,128)S(1)} %bitcast.129, f32[2048,1024]{1,0:T(8,128)} %fusion.39, f32[2048,1024]{1,0:T(8,128)S(1)} %bitcast.127, f32[2048,1024]{1,0:T(8,128)S(1)} %fusion.38), kind=kLoop, calls=%fused_computation.20 | loop fusion | flops 109051904 | bytes 50331648 | tf_op jit(solution)/shard_map/convert_element_type | solution.py:1784
  458.8 159.3 %feed_back.1 = (bf16[512,2048]{1,0:T(8,128)(2,1)}, bf16[512,2048]{1,0:T(8,128)(2,1)}, bf16[4,256,2048]{2,1,0:T(8,128)(2,1)}, bf16[1024,2048]{1,0:T(8,128)(2,1)}) custom-call(bf16[2048,1024]{1,0:T(8,128)(2,1)} %get-tuple-element.169.grad_chips, bf16[2048,1024]{1,0:T(8,128)(2,1)} %get-tuple-element.151.grad_others, ...), custom_call_target="tpu_custom_call" | custom-call | flops 68719476736 | bytes 503316480 | tf_op jit(solution)/shard_map/feed_back/pallas_call | solution.py:1203
  618.1 4.4 fusion.17
  638.8 4.7 convolution_convert_fusion.4
  647.4 68.3 %gradients_out.1 = (bf16[2,4,512,256]{3,2,1,0:T(8,128)(2,1)}, bf16[2048,256]{1,0:T(8,128)(2,1)}) custom-call(bf16[2,256,2048]{2,1,0:T(8,128)(2,1)} %bitcast.125, bf16[256,2048]{1,0:T(8,128)(2,1)} %reduce_sum.128.refs_1_), custom_call_target="tpu_custom_call" | custom-call | bytes 157286400 | tf_op jit(solution)/shard_map/gradients_out/pallas_call | solution.py:469
  729.1 25.3 %attend_back.1 = (bf16[4,512,768]{2,1,0:T(8,128)(2,1)}, bf16[4,512,768]{2,1,0:T(8,128)(2,1)}) custom-call(s32[5]{0:T(128)} %pad_add_fusion.flags_ref, bf16[4,512,768]{2,1,0:T(8,128)(2,1)} %bitcast.172, bf16[4,512,768]{2,1,0:T(8,128)(2,1)} %bitcast.170, bf16[2,4,512,256]{3,2,1,0:T(8,128)(2,1)} %get-tuple-element.92.refs_2_, ...), custom_call_target="tpu_custom_call" | custom-call | flops 8589934592 | bytes 16777216 | tf_op jit(solution)/shard_map/attend_back/pallas_call | solution.py:1617
  761.0 6.8 collective-permute-done.10
  769.0 9.3 fusion.40
  778.3 9.6 add_convert_fusion
  799.8 104.0 %last_scatter.1 = (bf16[2,256,2048]{2,1,0:T(8,128)(2,1)}, bf16[256,512]{1,0:T(8,128)(2,1)}, bf16[2048,256]{1,0:T(8,128)(2,1)}) custom-call(bf16[2048,768]{1,0:T(8,128)(2,1)} %bitcast.132, bf16[2048,768]{1,0:T(8,128)(2,1)} %bitcast.134, bf16[768,2048]{1,0:T(8,128)(2,1)} %bitcast.120, bf16[256,2048]{1,0:T(8,128)(2,1)} %pad_maximum_fusion.2.refs_3_, ...), custom_call_target="tpu_custom_call" | custom-call | bytes 314572800 | tf_op jit(solution)/shard_map/last_scatter/pallas_call | solution.py:469
  912.2 5.3 add_add_fusion.2
  924.4 35.5 %sum_everywhere.1 = (f32[4,128]{1,0:T(4,128)}, bf16[1536,256]{1,0:T(8,128)(2,1)}) custom-call(f32[32,4,128]{2,1,0:T(4,128)} %reshape.206.refs_0_, bf16[192,2048]{1,0:T(8,128)(2,1)} %reduce-scatter.5.cloned.1.call-done.refs_1_), custom_call_target="tpu_custom_call" | custom-call | bytes 41943040 | tf_op jit(solution)/shard_map/sum_everywhere/pallas_call | solution.py:1676
  (192 shorter events, 126.7 us)
Async XLA Ops:
  7.2 22.6 %copy-start.15 = (bf16[2,256,2048]{2,1,0:T(8,128)(2,1)S(1)}, bf16[2,256,2048]{2,1,0:T(8,128)(2,1)}, u32[]{:S(2)}) copy-start(bf16[2,256,2048]{2,1,0:T(8,128)(2,1)} %param.13) | copy-start | bytes 6291460
  7.2 33.7 %all-gather.4.cloned.1.call-start = ((), (), s32[]{:S(2)}) async-start(), calls=%async_computation.2 | async-start | bytes 1310720 | tf_op jit(solution)/shard_map/all_gather | solution.py:1255
  7.9 319.2 %all-gather.6.cloned.1.call-start = ((), (), s32[]{:S(2)}) async-start(), calls=%async_computation.3 | async-start | bytes 5242880 | tf_op jit(solution)/shard_map/all_gather | solution.py:1255
  9.5 21.2 %copy-start.28 = (s32[1,2,2,128]{3,1,2,0:T(2,128)}, s32[1,2,2,128]{3,1,2,0:T(2,128)S(1)}, u32[]{:S(2)}) copy-start(s32[1,2,2,128]{3,1,2,0:T(2,128)S(1)} %copy.42) | copy-start | bytes 6148
  34.9 131.9 %copy-start.7 = (bf16[2,256,2048]{2,1,0:T(8,128)(2,1)S(1)}, bf16[2,256,2048]{2,1,0:T(8,128)(2,1)}, u32[]{:S(2)}) copy-start(bf16[2,256,2048]{2,1,0:T(8,128)(2,1)} %param.25) | copy-start | bytes 6291460
  164.8 247.5 %all-gather.8.cloned.1.call-start = ((), (), s32[]{:S(2)}) async-start(), calls=%async_computation.4 | async-start | bytes 5242880 | tf_op jit(solution)/shard_map/all_gather | solution.py:1255
  166.8 126.6 %collective-permute-start.1 = (bf16[512,2048]{1,0:T(8,128)(2,1)S(1)}, bf16[512,2048]{1,0:T(8,128)(2,1)}, u32[]{:S(2)}, u32[]{:S(2)}) collective-permute-start(bf16[512,2048]{1,0:T(8,128)(2,1)S(1)} %bitcast.114), channel_id=1, source_target_pairs={{0,16},{4,20},{8,24},{12,28},{16,0},{20,4},{24,8},{28,12},{1,17},{... | collective-permute-start | bytes 6291464 | tf_op jit(solution)/shard_map/ppermute | solution.py:308
  167.4 131.4 %collective-permute-start = (bf16[512,2048]{1,0:T(8,128)(2,1)S(1)}, bf16[512,2048]{1,0:T(8,128)(2,1)}, u32[]{:S(2)}, u32[]{:S(2)}) collective-permute-start(bf16[512,2048]{1,0:T(8,128)(2,1)S(1)} %bitcast.115), channel_id=1, source_target_pairs={{0,8},{4,12},{8,0},{12,4},{16,24},{20,28},{24,16},{28,20},{1,9},{5... | collective-permute-start | bytes 6291464 | tf_op jit(solution)/shard_map/ppermute | solution.py:308
  172.7 627.1 %reduce-scatter.3.cloned.1.call-start = ((), (), s32[]{:S(2)}) async-start(), calls=%async_computation.5 | async-start | bytes 5242880 | tf_op jit(solution)/shard_map/reduce_scatter | solution.py:1259
  295.5 26.1 %collective-permute-start.2 = (bf16[256,2048]{1,0:T(8,128)(2,1)S(1)}, bf16[256,2048]{1,0:T(8,128)(2,1)S(1)}, u32[]{:S(2)}, u32[]{:S(2)}) collective-permute-start(bf16[256,2048]{1,0:T(8,128)(2,1)S(1)} %slice.155), channel_id=1, source_target_pairs={{0,8},{4,12},{8,0},{12,4},{16,24},{20,28},{24,16},{28,20},{1,9},{5... | collective-permute-start | bytes 3145736 | tf_op jit(solution)/shard_map/ppermute | solution.py:308
  300.0 25.9 %collective-permute-start.3 = (bf16[256,2048]{1,0:T(8,128)(2,1)S(1)}, bf16[256,2048]{1,0:T(8,128)(2,1)S(1)}, u32[]{:S(2)}, u32[]{:S(2)}) collective-permute-start(bf16[256,2048]{1,0:T(8,128)(2,1)S(1)} %slice.156), channel_id=1, source_target_pairs={{0,16},{4,20},{8,24},{12,28},{16,0},{20,4},{24,8},{28,12},{1,17},{... | collective-permute-start | bytes 3145736 | tf_op jit(solution)/shard_map/ppermute | solution.py:308
  412.3 27.6 %slice-start = ((s8[8388608]{0:T(1024)(128)(4,1)}), s8[4194304]{0:T(1024)(128)(4,1)S(1)}, s32[]{:S(2)}) async-start(s8[8388608]{0:T(1024)(128)(4,1)} %bitcast.126), calls=%async_computation.7 | async-start | bytes 8388608
  412.3 27.6 %slice-start.2 = ((s8[8388608]{0:T(1024)(128)(4,1)}), s8[4194304]{0:T(1024)(128)(4,1)S(1)}, s32[]{:S(2)}) async-start(s8[8388608]{0:T(1024)(128)(4,1)} %bitcast.128), calls=%async_computation.9 | async-start | bytes 8388608
  634.6 84.9 %collective-permute-start.4 = (bf16[1024,2048]{1,0:T(8,128)(2,1)}, bf16[1024,2048]{1,0:T(8,128)(2,1)}, u32[]{:S(2)}, u32[]{:S(2)}) collective-permute-start(bf16[1024,2048]{1,0:T(8,128)(2,1)} %convolution_convert_fusion), channel_id=1, source_target_pairs={{0,4},{4,0},{8,12},{12,8},{16,20},{20,16},{24,28},{28,24},{1,5},{5... | collective-permute-start | bytes 12582920 | tf_op jit(solution)/shard_map/ppermute | solution.py:308
  715.8 208.6 %reduce-scatter.5.cloned.1.call-start = ((), (), s32[]{:S(2)}) async-start(), calls=%async_computation.6 | async-start | bytes 3932160 | tf_op jit(solution)/shard_map/reduce_scatter | solution.py:1259
  725.0 29.3 %collective-permute-start.8 = (bf16[128,2048]{1,0:T(8,128)(2,1)}, bf16[128,2048]{1,0:T(8,128)(2,1)}, u32[]{:S(2)}, u32[]{:S(2)}) collective-permute-start(bf16[128,2048]{1,0:T(8,128)(2,1)} %get-tuple-element.146), channel_id=1, source_target_pairs={{0,16},{4,20},{8,24},{12,28},{16,0},{20,4},{24,8},{28,12},{1,17},{... | collective-permute-start | bytes 1572872 | tf_op jit(solution)/shard_map/ppermute | solution.py:308
  726.5 27.8 %collective-permute-start.7 = (bf16[128,2048]{1,0:T(8,128)(2,1)}, bf16[128,2048]{1,0:T(8,128)(2,1)}, u32[]{:S(2)}, u32[]{:S(2)}) collective-permute-start(bf16[128,2048]{1,0:T(8,128)(2,1)} %get-tuple-element.147), channel_id=1, source_target_pairs={{0,8},{4,12},{8,0},{12,4},{16,24},{20,28},{24,16},{28,20},{1,9},{5... | collective-permute-start | bytes 1572872 | tf_op jit(solution)/shard_map/ppermute | solution.py:308
  728.1 26.3 %collective-permute-start.6 = (bf16[128,2048]{1,0:T(8,128)(2,1)}, bf16[128,2048]{1,0:T(8,128)(2,1)}, u32[]{:S(2)}, u32[]{:S(2)}) collective-permute-start(bf16[128,2048]{1,0:T(8,128)(2,1)} %get-tuple-element.148), channel_id=1, source_target_pairs={{0,16},{4,20},{8,24},{12,28},{16,0},{20,4},{24,8},{28,12},{1,17},{... | collective-permute-start | bytes 1572872 | tf_op jit(solution)/shard_map/ppermute | solution.py:308
  728.6 25.8 %collective-permute-start.5 = (bf16[128,2048]{1,0:T(8,128)(2,1)}, bf16[128,2048]{1,0:T(8,128)(2,1)}, u32[]{:S(2)}, u32[]{:S(2)}) collective-permute-start(bf16[128,2048]{1,0:T(8,128)(2,1)} %get-tuple-element.149), channel_id=1, source_target_pairs={{0,8},{4,12},{8,0},{12,4},{16,24},{20,28},{24,16},{28,20},{1,9},{5... | collective-permute-start | bytes 1572872 | tf_op jit(solution)/shard_map/ppermute | solution.py:308
  758.0 9.9 %collective-permute-start.10 = (bf16[128,2048]{1,0:T(8,128)(2,1)}, bf16[128,2048]{1,0:T(8,128)(2,1)}, u32[]{:S(2)}, u32[]{:S(2)}) collective-permute-start(bf16[128,2048]{1,0:T(8,128)(2,1)} %get-tuple-element.144), channel_id=1, source_target_pairs={{0,16},{4,20},{8,24},{12,28},{16,0},{20,4},{24,8},{28,12},{1,17},{... | collective-permute-start | bytes 1572872 | tf_op jit(solution)/shard_map/ppermute | solution.py:308
  759.5 9.5 collective-permute-start.9
  788.1 3.5 collective-permute-start.11
  799.8 106.2 %copy-start.20 = (f32[1,4,512]{2,0,1:T(1,128)S(1)}, f32[1,4,512]{2,0,1:T(1,128)}, u32[]{:S(2)}) copy-start(f32[1,4,512]{2,0,1:T(1,128)} %copy-done.19) | copy-start | bytes 24580
  799.8 106.2 %copy-start.22 = (f32[512]{0:T(512)S(1)}, f32[512]{0:T(512)}, u32[]{:S(2)}) copy-start(f32[512]{0:T(512)} %copy-done.21) | copy-start | bytes 6148
  (31 other events, 169.0 us)
Sparse Core Ops, SparseCore 0:
  9.6 31.2 all-gather.3
  164.9 110.7 all-gather.5
  277.3 79.3 all-gather.7
  715.9 76.1 reduce-scatter.2
  794.4 93.1 reduce-scatter.4

commit v4 on v3

--- a/solution.py
+++ b/solution.py
@@ -1094,9 +1094,8 @@
         for mask in (CORE, X_WAY, Y_WAY):
             pl.semaphore_signal(free_sem.at[side], inc=1, **at_plane(d ^ mask, z))
 
-    def weight_grad(rights, place):
+    def weight_grad(rights, place, base, slots):
         chunks = rights[0].shape[1] // columns
-        gone = {}
 
         def load(chunk):
             for side in range(2):
@@ -1109,9 +1108,8 @@
             if chunk + 1 < chunks:
                 load(chunk + 1)
             first, second = (stream.wait(2 * (chunk % 2) + side) for side in range(2))
-            result = results.wait(chunk % 2)
-            for move in gone.pop(chunk % 2, ()):
-                moves.sent(move)
+            slot = base + chunk % slots
+            result = results.wait(slot)
 
             @pl.loop(0, result.shape[0] // 256)
             def _(i):
@@ -1120,32 +1118,24 @@
                 total += jnp.dot(left[1, at, :], second[...], preferred_element_type=F32)
                 result[at, :] = total.astype(BF16)
 
-            gone[chunk % 2] = place(result, chunk)
+            place(slot, result, chunk)
             yield
-        for copies in gone.values():
-            for move in copies:
-                moves.sent(move)
 
     groups = lax.axis_size("seq")
     part = up_parts_ref.shape[1]
 
-    def to_line(result, chunk):
+    def to_line(slot, result, chunk):
         target = up_parts_ref.at[:, :, pl.ds(chunk * columns, columns)]
-        copies = []
         for step in range(1, groups):
             to = (z + step) % groups
             piece = result.at[pl.ds(pl.multiple_of(to * part, 256), part)]
-            copies.append(moves.far(piece, target.at[step], d, to))
+            moves.far(piece, target.at[step], d, to)
         piece = result.at[pl.ds(pl.multiple_of(z * part, 256), part)]
-        results.copies[chunk % 2] = pltpu.make_async_copy(
-            piece, target.at[0], results.sems.at[chunk % 2]
-        )
-        results.copies[chunk % 2].start()
-        return copies
-
-    def to_memory(result, chunk):
-        results.store(chunk % 2, down_grad_ref.at[:, pl.ds(chunk * columns, columns)])
-        return ()
+        results.copies[slot] = pltpu.make_async_copy(piece, target.at[0], results.sems.at[slot])
+        results.copies[slot].start()
+
+    def to_memory(slot, result, chunk):
+        results.store(slot, down_grad_ref.at[:, pl.ds(chunk * columns, columns)])
 
     def steps(work, number):
         for _ in range(number):
@@ -1161,8 +1151,9 @@
     norm_high = scatter(grads, 1, norm_ref, lambda: load_weights(down_ref, 1), False)
     out_low = scatter(acts, 0, out_ref, nothing, False)
     out_high = scatter(acts, 1, out_ref, nothing, True)
-    up_work = weight_grad((rows_chips, rows_others), to_line)
-    down_work = weight_grad((cot_chips, cot_others), to_memory)
+    line_slots = result_held.shape[0] - 2
+    up_work = weight_grad((rows_chips, rows_others), to_line, 0, line_slots)
+    down_work = weight_grad((cot_chips, cot_others), to_memory, line_slots, 2)
     next(norm_low)
     next(norm_low)
     steps(up_work, 3)
@@ -1186,7 +1177,7 @@
     next(out_high)
     steps(down_work, 5)
     next(out_high, None)
-    for slot in range(2):
+    for slot in range(line_slots + 2):
         results.wait(slot)
     moves.finish()
 
@@ -1217,11 +1208,11 @@
             pltpu.VMEM((2, count, half), BF16),
             pltpu.VMEM((2, count, half), BF16),
             pltpu.VMEM((4, total, columns), BF16),
-            pltpu.VMEM((2, units, columns), BF16),
+            pltpu.VMEM((width // columns + 2, units, columns), BF16),
             pltpu.SemaphoreType.DMA((2,)),
             pltpu.SemaphoreType.DMA((2,)),
             pltpu.SemaphoreType.DMA((4,)),
-            pltpu.SemaphoreType.DMA((2,)),
+            pltpu.SemaphoreType.DMA((width // columns + 2,)),
             pltpu.SemaphoreType.REGULAR((2,)),
             pltpu.SemaphoreType.DMA((copies,)),
             pltpu.SemaphoreType.DMA((copies,)),

time: 978 us -> 959 us (0.981)
  Pallas kernels: 699 us -> 680 us
    pallas_call x6, Pallas kernels: 459 us -> 448 us  [kernel_call(): pl.pallas_call(body, out_shape=outputs, in_specs=[pl.BlockSpec(memory_spa...]
where the time goes in v4:
time: 959 us; the launch traced here: 953 us
  Pallas kernels  680 us (71%)
  matrix products  93.4 us (10%)
  other arithmetic  69.8 us (7%)
  local copies, waits for them, and re-layouts  49.8 us (5%)
  waiting for transfers between devices  34.4 us (4%)
  between operations  14.7 us (2%)
  starting transfers between devices  10.9 us (1%)
    pallas_call x6, Pallas kernels, kernel_call(): pl.pallas_call(body, out_shape=outputs, in_specs=[pl.BlockSpec(memory_spa...  448 us
    pallas_call x1, Pallas kernels, feed_back(): pl.pallas_call(feed_kernel, out_shape=[shaped(count, width)] * 2 + [shape...  155 us
    pallas_call x1, Pallas kernels, sum_everywhere(): pl.pallas_call(lambda *refs: sum_everywhere_kernel(number, *refs), out_sh...  32.7 us
    ppermute x12, waiting for transfers between devices, swap(): return lax.ppermute(value, 'dp', [(i, i ^ mask) for i in range(dp)])  27.7 us
    dot_general x2, matrix products, grouped_shards(): jnp.einsum('td,id->ti', cot_part, down_full, preferred_element_type=F32)  27.5 us
    unnamed x85, local copies, waits for them, and re-layouts  27.1 us
    pallas_call x1, Pallas kernels, attend_back(): pl.pallas_call(kernel, grid=(SEQS, heads), in_specs=[pl.BlockSpec(memory_...  25.3 us
    dot_general x2, matrix products, grouped_shards(): jnp.einsum('td,ed->te', part, qkv_full, preferred_element_type=F32)  21.7 us
  transfers between devices with their start and end apart: 17, of which 6 were waited for; matrix products, arithmetic and copies ran while one was open for 14% of the time, Pallas kernels for 39%

profile of v4, /device:TPU:0, one launch (start us, length us, event | category | flops | bytes accessed | tf_op | source)
XLA Modules:
  0.0 953.1 jit_solution(843226897239283882)
XLA Ops:
  14.2 10.3 %intake.1 = (bf16[4,8,512]{2,1,0:T(8,128)(2,1)}, s32[8,8,128]{2,1,0:T(8,128)}) custom-call(bf16[8,512]{1,0:T(8,128)(2,1)} %concatenate.33.refs_0_, s32[8,128]{1,0:T(8,128)} %broadcast_in_dim.32.refs_1_), custom_call_target="tpu_custom_call" | custom-call | bytes 31457280 | tf_op jit(solution)/shard_map/intake/pallas_call | solution.py:469
  34.9 6.0 all-gather.4.cloned.1.call-done
  43.1 121.7 %first_gather.1 = (bf16[4,512,2048]{2,1,0:T(8,128)(2,1)}, bf16[4,512,2048]{2,1,0:T(8,128)(2,1)}, bf16[6,192,2048]{2,1,0:T(8,128)(2,1)}, bf16[256,2048]{1,0:T(8,1...) custom-call(bf16[2,256,2048]{2,1,0:T(8,128)(2,1)} %bitcast.124, bf16[1536,256]{1,0:T(8,128)(2,1)} %bitcast.136, ...), custom_call_target="tpu_custom_call" | custom-call | bytes 346030080 | tf_op jit(solution)/shard_map/first_gather/pallas_call | solution.py:469
  173.0 11.4 %convolution_convert_fusion.2 = bf16[2048,768]{1,0:T(8,128)(2,1)} fusion(bf16[2048,2048]{1,0:T(8,128)(2,1)} %bitcast.157, bf16[768,2048]{1,0:T(8,128)(2,1)} %bitcast.119), kind=kOutput, calls=%fused_computation.50 | convolution fusion | flops 6444023808 | bytes 14680064 | tf_op jit(solution)/shard_map/td,ed->te/dot_general | solution.py:1745
  184.3 10.3 %convolution_convert_fusion.3 = bf16[2048,768]{1,0:T(8,128)(2,1)} fusion(bf16[2048,2048]{1,0:T(8,128)(2,1)} %bitcast.155, bf16[768,2048]{1,0:T(8,128)(2,1)S(1)} %bitcast.121), kind=kOutput, calls=%fused_computation.51 | convolution fusion | flops 6444023808 | bytes 14680064 | tf_op jit(solution)/shard_map/td,ed->te/dot_general | solution.py:1745
  194.6 19.7 %attend.1 = (bf16[4,512,256]{2,1,0:T(8,128)(2,1)}, bf16[4,512,256]{2,1,0:T(8,128)(2,1)}, f32[4,2,8,512]{3,2,1,0:T(8,128)}, f32[4,2,8,512]{3,2,1,0:T(8,128)}) custom-call(s32[5]{0:T(128)} %pad_add_fusion.flags_ref, bf16[4,512,768]{2,1,0:T(8,128)(2,1)} %bitcast.171, bf16[4,512,768]{2,1,0:T(8,128)(2,1)} %bitcast.169), custom_call_target="tpu_custom_call" | custom-call | flops 3221225472 | bytes 8388608 | tf_op jit(solution)/shard_map/attend/pallas_call | solution.py:1529
  214.3 69.9 %contexts_home.1 = (bf16[2,256,2048]{2,1,0:T(8,128)(2,1)}, bf16[4,256,2048]{2,1,0:T(8,128)(2,1)}, bf16[4,256,2048]{2,1,0:T(8,128)(2,1)}) custom-call(bf16[4,512,256]{2,1,0:T(8,128)(2,1)} %get-tuple-element.67.refs_0_, bf16[4,512,256]{2,1,0:T(8,128)(2,1)} %get-tuple-element.68.refs_1_, bf16[256,2048]{1,0:T(8,128)(2,1)} %bitcast.130), custom_call_target="tpu_custom_call" | custom-call | bytes 188743680 | tf_op jit(solution)/shard_map/contexts_home/pallas_call | solution.py:469
  284.3 5.3 fusion.26
  309.5 12.1 %collective-permute-done.2 = bf16[256,2048]{1,0:T(8,128)(2,1)S(1)} collective-permute-done((bf16[256,2048]{1,0:T(8,128)(2,1)S(1)}, bf16[256,2048]{1,0:T(8,128)(2,1)S(1)}, u32[]{:S(2)}, u32[]{:S(2)}) %collective-permute-start.2) | collective-permute-done | bytes 1048608 | tf_op jit(solution)/shard_map/ppermute | solution.py:308
  327.1 85.2 %gather_multiply.1 = (bf16[4,512,2048]{2,1,0:T(8,128)(2,1)}, bf16[4,512,2048]{2,1,0:T(8,128)(2,1)}, bf16[2048,2048]{1,0:T(8,128)(2,1)}, f32[2048,1024]{1,0:T(8,128)}, f32[2048,1024]{1,0:T(8,128)}) custom-call(bf16[512,2048]{1,0:T(8,128)(2,1)} %add_convert_fusion.2.refs_0_, bf16[2048,2048]{1,0:T(8,128)(2,1)} %constant_dynamic-update-slice_fusion.refs_1_.cot_chips, ...), custom_call_target="tpu_custom_call" | custom-call | bytes 251658240 | tf_op jit(solution)/shard_map/gather_multiply/pallas_call | solution.py:469
  412.4 12.7 %fusion.38 = f32[2048,1024]{1,0:T(8,128)S(1)} fusion(bf16[2048,2048]{1,0:T(8,128)(2,1)} %constant_dynamic-update-slice_fusion.refs_1_.cot_chips, bf16[1024,2048]{1,0:T(8,128)(2,1)} %all-gather.8.cloned.1.call-done.down_ref), kind=kOutput, calls=%fused_computation.111 | convolution fusion | flops 8589934592 | bytes 20971520 | tf_op jit(solution)/shard_map/td,id->ti/dot_general | solution.py:1773
  425.1 14.9 %fusion.39 = f32[2048,1024]{1,0:T(8,128)} fusion(bf16[2048,2048]{1,0:T(8,128)(2,1)} %get-tuple-element.81.cot_others, bf16[1024,2048]{1,0:T(8,128)(2,1)} %all-gather.8.cloned.1.call-done.down_ref), kind=kOutput, calls=%fused_computation.112 | convolution fusion | flops 8589934592 | bytes 20971520 | tf_op jit(solution)/shard_map/td,id->ti/dot_general | solution.py:1773
  440.0 18.8 %multiply_convert_fusion = (bf16[2048,1024]{1,0:T(8,128)(2,1)}, bf16[2048,1024]{1,0:T(8,128)(2,1)}, bf16[2048,1024]{1,0:T(8,128)(2,1)}, bf16[2048,1024]{1,0:T(8,128)(2,1)}) fusion(f32[2048,1024]{1,0:T(8,128)S(1)} %bitcast.129, f32[2048,1024]{1,0:T(8,128)} %fusion.39, f32[2048,1024]{1,0:T(8,128)S(1)} %bitcast.127, f32[2048,1024]{1,0:T(8,128)S(1)} %fusion.38), kind=kLoop, calls=%fused_computation.20 | loop fusion | flops 109051904 | bytes 50331648 | tf_op jit(solution)/shard_map/convert_element_type | solution.py:1775
  458.8 154.9 %feed_back.1 = (bf16[512,2048]{1,0:T(8,128)(2,1)}, bf16[512,2048]{1,0:T(8,128)(2,1)}, bf16[4,256,2048]{2,1,0:T(8,128)(2,1)}, bf16[1024,2048]{1,0:T(8,128)(2,1)}) custom-call(bf16[2048,1024]{1,0:T(8,128)(2,1)} %get-tuple-element.169.grad_chips, bf16[2048,1024]{1,0:T(8,128)(2,1)} %get-tuple-element.151.grad_others, ...), custom_call_target="tpu_custom_call" | custom-call | flops 68719476736 | bytes 503316480 | tf_op jit(solution)/shard_map/feed_back/pallas_call | solution.py:1194
  613.7 4.4 fusion.17
  634.4 4.7 convolution_convert_fusion.4
  643.0 54.1 %gradients_out.1 = (bf16[2,4,512,256]{3,2,1,0:T(8,128)(2,1)}, bf16[2048,256]{1,0:T(8,128)(2,1)}) custom-call(bf16[2,256,2048]{2,1,0:T(8,128)(2,1)} %bitcast.125, bf16[256,2048]{1,0:T(8,128)(2,1)} %reduce_sum.128.refs_1_), custom_call_target="tpu_custom_call" | custom-call | bytes 157286400 | tf_op jit(solution)/shard_map/gradients_out/pallas_call | solution.py:469
  710.4 25.3 %attend_back.1 = (bf16[4,512,768]{2,1,0:T(8,128)(2,1)}, bf16[4,512,768]{2,1,0:T(8,128)(2,1)}) custom-call(s32[5]{0:T(128)} %pad_add_fusion.flags_ref, bf16[4,512,768]{2,1,0:T(8,128)(2,1)} %bitcast.172, bf16[4,512,768]{2,1,0:T(8,128)(2,1)} %bitcast.170, bf16[2,4,512,256]{3,2,1,0:T(8,128)(2,1)} %get-tuple-element.92.refs_2_, ...), custom_call_target="tpu_custom_call" | custom-call | flops 8589934592 | bytes 16777216 | tf_op jit(solution)/shard_map/attend_back/pallas_call | solution.py:1608
  741.5 7.6 collective-permute-done.10
  750.4 9.3 fusion.40
  759.8 9.6 %add_convert_fusion = bf16[768,2048]{1,0:T(8,128)(2,1)S(1)} fusion(f32[768,2048]{1,0:T(8,128)S(1)} %fusion.40, bf16[2048,768]{1,0:T(8,128)(2,1)S(1)} %bitcast.133, bf16[2048,2048]{1,0:T(8,128)(2,1)} %bitcast.156), kind=kOutput, calls=%fused_computation.22 | convolution fusion | flops 6445596672 | bytes 20971520 | tf_op jit(solution)/shard_map/ti,td->id/dot_general | solution.py:1766
  781.3 106.4 %last_scatter.1 = (bf16[2,256,2048]{2,1,0:T(8,128)(2,1)}, bf16[256,512]{1,0:T(8,128)(2,1)}, bf16[2048,256]{1,0:T(8,128)(2,1)}) custom-call(bf16[2048,768]{1,0:T(8,128)(2,1)} %bitcast.132, bf16[2048,768]{1,0:T(8,128)(2,1)} %bitcast.134, bf16[768,2048]{1,0:T(8,128)(2,1)} %bitcast.120, bf16[256,2048]{1,0:T(8,128)(2,1)} %pad_maximum_fusion.2.refs_3_, ...), custom_call_target="tpu_custom_call" | custom-call | bytes 314572800 | tf_op jit(solution)/shard_map/last_scatter/pallas_call | solution.py:469
  896.0 5.3 add_add_fusion.2
  908.2 32.7 %sum_everywhere.1 = (f32[4,128]{1,0:T(4,128)}, bf16[1536,256]{1,0:T(8,128)(2,1)}) custom-call(f32[32,4,128]{2,1,0:T(4,128)} %reshape.206.refs_0_, bf16[192,2048]{1,0:T(8,128)(2,1)} %reduce-scatter.5.cloned.1.call-done.refs_1_), custom_call_target="tpu_custom_call" | custom-call | bytes 41943040 | tf_op jit(solution)/shard_map/sum_everywhere/pallas_call | solution.py:1667
  (192 shorter events, 126.0 us)
Async XLA Ops:
  7.2 22.6 %copy-start.15 = (bf16[2,256,2048]{2,1,0:T(8,128)(2,1)S(1)}, bf16[2,256,2048]{2,1,0:T(8,128)(2,1)}, u32[]{:S(2)}) copy-start(bf16[2,256,2048]{2,1,0:T(8,128)(2,1)} %param.13) | copy-start | bytes 6291460
  7.2 33.7 %all-gather.4.cloned.1.call-start = ((), (), s32[]{:S(2)}) async-start(), calls=%async_computation.2 | async-start | bytes 1310720 | tf_op jit(solution)/shard_map/all_gather | solution.py:1246
  7.9 319.2 %all-gather.6.cloned.1.call-start = ((), (), s32[]{:S(2)}) async-start(), calls=%async_computation.3 | async-start | bytes 5242880 | tf_op jit(solution)/shard_map/all_gather | solution.py:1246
  9.5 21.2 %copy-start.28 = (s32[1,2,2,128]{3,1,2,0:T(2,128)}, s32[1,2,2,128]{3,1,2,0:T(2,128)S(1)}, u32[]{:S(2)}) copy-start(s32[1,2,2,128]{3,1,2,0:T(2,128)S(1)} %copy.42) | copy-start | bytes 6148
  34.9 131.9 %copy-start.7 = (bf16[2,256,2048]{2,1,0:T(8,128)(2,1)S(1)}, bf16[2,256,2048]{2,1,0:T(8,128)(2,1)}, u32[]{:S(2)}) copy-start(bf16[2,256,2048]{2,1,0:T(8,128)(2,1)} %param.25) | copy-start | bytes 6291460
  164.8 247.5 %all-gather.8.cloned.1.call-start = ((), (), s32[]{:S(2)}) async-start(), calls=%async_computation.4 | async-start | bytes 5242880 | tf_op jit(solution)/shard_map/all_gather | solution.py:1246
  166.8 126.6 %collective-permute-start.1 = (bf16[512,2048]{1,0:T(8,128)(2,1)S(1)}, bf16[512,2048]{1,0:T(8,128)(2,1)}, u32[]{:S(2)}, u32[]{:S(2)}) collective-permute-start(bf16[512,2048]{1,0:T(8,128)(2,1)S(1)} %bitcast.114), channel_id=1, source_target_pairs={{0,16},{4,20},{8,24},{12,28},{16,0},{20,4},{24,8},{28,12},{1,17},{... | collective-permute-start | bytes 6291464 | tf_op jit(solution)/shard_map/ppermute | solution.py:308
  167.4 131.4 %collective-permute-start = (bf16[512,2048]{1,0:T(8,128)(2,1)S(1)}, bf16[512,2048]{1,0:T(8,128)(2,1)}, u32[]{:S(2)}, u32[]{:S(2)}) collective-permute-start(bf16[512,2048]{1,0:T(8,128)(2,1)S(1)} %bitcast.115), channel_id=1, source_target_pairs={{0,8},{4,12},{8,0},{12,4},{16,24},{20,28},{24,16},{28,20},{1,9},{5... | collective-permute-start | bytes 6291464 | tf_op jit(solution)/shard_map/ppermute | solution.py:308
  172.7 608.6 %reduce-scatter.3.cloned.1.call-start = ((), (), s32[]{:S(2)}) async-start(), calls=%async_computation.5 | async-start | bytes 5242880 | tf_op jit(solution)/shard_map/reduce_scatter | solution.py:1250
  295.5 26.1 %collective-permute-start.2 = (bf16[256,2048]{1,0:T(8,128)(2,1)S(1)}, bf16[256,2048]{1,0:T(8,128)(2,1)S(1)}, u32[]{:S(2)}, u32[]{:S(2)}) collective-permute-start(bf16[256,2048]{1,0:T(8,128)(2,1)S(1)} %slice.155), channel_id=1, source_target_pairs={{0,8},{4,12},{8,0},{12,4},{16,24},{20,28},{24,16},{28,20},{1,9},{5... | collective-permute-start | bytes 3145736 | tf_op jit(solution)/shard_map/ppermute | solution.py:308
  300.0 25.9 %collective-permute-start.3 = (bf16[256,2048]{1,0:T(8,128)(2,1)S(1)}, bf16[256,2048]{1,0:T(8,128)(2,1)S(1)}, u32[]{:S(2)}, u32[]{:S(2)}) collective-permute-start(bf16[256,2048]{1,0:T(8,128)(2,1)S(1)} %slice.156), channel_id=1, source_target_pairs={{0,16},{4,20},{8,24},{12,28},{16,0},{20,4},{24,8},{28,12},{1,17},{... | collective-permute-start | bytes 3145736 | tf_op jit(solution)/shard_map/ppermute | solution.py:308
  412.3 27.6 %slice-start = ((s8[8388608]{0:T(1024)(128)(4,1)}), s8[4194304]{0:T(1024)(128)(4,1)S(1)}, s32[]{:S(2)}) async-start(s8[8388608]{0:T(1024)(128)(4,1)} %bitcast.126), calls=%async_computation.7 | async-start | bytes 8388608
  412.3 27.6 %slice-start.2 = ((s8[8388608]{0:T(1024)(128)(4,1)}), s8[4194304]{0:T(1024)(128)(4,1)S(1)}, s32[]{:S(2)}) async-start(s8[8388608]{0:T(1024)(128)(4,1)} %bitcast.128), calls=%async_computation.9 | async-start | bytes 8388608
  630.1 70.7 %collective-permute-start.4 = (bf16[1024,2048]{1,0:T(8,128)(2,1)}, bf16[1024,2048]{1,0:T(8,128)(2,1)}, u32[]{:S(2)}, u32[]{:S(2)}) collective-permute-start(bf16[1024,2048]{1,0:T(8,128)(2,1)} %convolution_convert_fusion), channel_id=1, source_target_pairs={{0,4},{4,0},{8,12},{12,8},{16,20},{20,16},{24,28},{28,24},{1,5},{5... | collective-permute-start | bytes 12582920 | tf_op jit(solution)/shard_map/ppermute | solution.py:308
  697.1 211.1 %reduce-scatter.5.cloned.1.call-start = ((), (), s32[]{:S(2)}) async-start(), calls=%async_computation.6 | async-start | bytes 3932160 | tf_op jit(solution)/shard_map/reduce_scatter | solution.py:1250
  706.4 29.4 %collective-permute-start.8 = (bf16[128,2048]{1,0:T(8,128)(2,1)}, bf16[128,2048]{1,0:T(8,128)(2,1)}, u32[]{:S(2)}, u32[]{:S(2)}) collective-permute-start(bf16[128,2048]{1,0:T(8,128)(2,1)} %get-tuple-element.146), channel_id=1, source_target_pairs={{0,16},{4,20},{8,24},{12,28},{16,0},{20,4},{24,8},{28,12},{1,17},{... | collective-permute-start | bytes 1572872 | tf_op jit(solution)/shard_map/ppermute | solution.py:308
  707.9 27.8 %collective-permute-start.7 = (bf16[128,2048]{1,0:T(8,128)(2,1)}, bf16[128,2048]{1,0:T(8,128)(2,1)}, u32[]{:S(2)}, u32[]{:S(2)}) collective-permute-start(bf16[128,2048]{1,0:T(8,128)(2,1)} %get-tuple-element.147), channel_id=1, source_target_pairs={{0,8},{4,12},{8,0},{12,4},{16,24},{20,28},{24,16},{28,20},{1,9},{5... | collective-permute-start | bytes 1572872 | tf_op jit(solution)/shard_map/ppermute | solution.py:308
  708.6 27.1 %collective-permute-start.6 = (bf16[128,2048]{1,0:T(8,128)(2,1)}, bf16[128,2048]{1,0:T(8,128)(2,1)}, u32[]{:S(2)}, u32[]{:S(2)}) collective-permute-start(bf16[128,2048]{1,0:T(8,128)(2,1)} %get-tuple-element.148), channel_id=1, source_target_pairs={{0,16},{4,20},{8,24},{12,28},{16,0},{20,4},{24,8},{28,12},{1,17},{... | collective-permute-start | bytes 1572872 | tf_op jit(solution)/shard_map/ppermute | solution.py:308
  709.2 26.5 %collective-permute-start.5 = (bf16[128,2048]{1,0:T(8,128)(2,1)}, bf16[128,2048]{1,0:T(8,128)(2,1)}, u32[]{:S(2)}, u32[]{:S(2)}) collective-permute-start(bf16[128,2048]{1,0:T(8,128)(2,1)} %get-tuple-element.149), channel_id=1, source_target_pairs={{0,8},{4,12},{8,0},{12,4},{16,24},{20,28},{24,16},{28,20},{1,9},{5... | collective-permute-start | bytes 1572872 | tf_op jit(solution)/shard_map/ppermute | solution.py:308
  739.4 9.8 %collective-permute-start.10 = (bf16[128,2048]{1,0:T(8,128)(2,1)}, bf16[128,2048]{1,0:T(8,128)(2,1)}, u32[]{:S(2)}, u32[]{:S(2)}) collective-permute-start(bf16[128,2048]{1,0:T(8,128)(2,1)} %get-tuple-element.144), channel_id=1, source_target_pairs={{0,16},{4,20},{8,24},{12,28},{16,0},{20,4},{24,8},{28,12},{1,17},{... | collective-permute-start | bytes 1572872 | tf_op jit(solution)/shard_map/ppermute | solution.py:308
  740.9 9.5 %collective-permute-start.9 = (bf16[128,2048]{1,0:T(8,128)(2,1)}, bf16[128,2048]{1,0:T(8,128)(2,1)}, u32[]{:S(2)}, u32[]{:S(2)}) collective-permute-start(bf16[128,2048]{1,0:T(8,128)(2,1)} %get-tuple-element.145), channel_id=1, source_target_pairs={{0,8},{4,12},{8,0},{12,4},{16,24},{20,28},{24,16},{28,20},{1,9},{5... | collective-permute-start | bytes 1572872 | tf_op jit(solution)/shard_map/ppermute | solution.py:308
  769.6 3.5 collective-permute-start.11
  781.3 108.6 %copy-start.20 = (f32[1,4,512]{2,0,1:T(1,128)S(1)}, f32[1,4,512]{2,0,1:T(1,128)}, u32[]{:S(2)}) copy-start(f32[1,4,512]{2,0,1:T(1,128)} %copy-done.19) | copy-start | bytes 24580
  781.3 108.6 %copy-start.22 = (f32[512]{0:T(512)S(1)}, f32[512]{0:T(512)}, u32[]{:S(2)}) copy-start(f32[512]{0:T(512)} %copy-done.21) | copy-start | bytes 6148
  (31 other events, 170.2 us)
Sparse Core Ops, SparseCore 0:
  9.6 31.2 all-gather.3
  164.9 110.7 all-gather.5
  277.3 79.3 all-gather.7
  697.3 75.5 reduce-scatter.2
  775.4 92.8 reduce-scatter.4
